TPU v7x, 512 devices: a whole 4x8x8 slice. The times are simulated.
512 devices in a mesh: rep: 8 (over z_hi, core), dp: 64 (over z_lo, x, y).
Axes of the slice: x: 4, y: 8, z: 8 (z_hi: 4, z_lo: 2; z = z_hi * 2 + z_lo), core: 2. Of those that a mesh axis runs over, the one named last changes fastest.
Arguments:
- frames: bfloat16 [98304, 1536], P(('rep', 'dp')), may hold values from -6 to 6
- lengths: int32 [512, 8], P(('rep', 'dp')), may hold values from 0 to 192, as said below
- destination: int32 [512, 48], P(('rep', 'dp')), may hold values from -1 to 63, as said below
- kernel: float32 [15, 1536], replicated, may hold values from -1.5 to 1.5
- norm_gain: float32 [1536], replicated, may hold values from 0.5 to 1.5
- master: float32 [1536, 1536], P('dp'), may hold values from -0.15625 to 0.15625
- moment: float32 [1536, 1536], P('dp'), may hold values from -0.18 to 0.18
- second: float32 [1536, 1536], P('dp'), may hold values from 0.0003 to 0.003
- gradient: float32 [1536, 1536], P('dp'), may hold values from -1.8 to 1.8
- bucket_order: int32 [64], replicated, may hold values from 0 to 63, each once
- cotangent: bfloat16 [65536, 1536], P(('rep', 'dp')), may hold values from -6 to 6
Outputs:
- projected: bfloat16 [65536, 1536], P(('rep', 'dp'))
- frame_grad: bfloat16 [98304, 1536], P(('rep', 'dp'))
- kernel_grad: float32 [15, 1536], replicated
- gain_grad: float32 [1536], replicated
- new_master: float32 [1536, 1536], P('dp')
Inputs may be any that keep to these rules, and one draw needn't show every extreme that they name: destination[i, b] is the device of i's replica group that takes block b of device i, or -1 for a block without frames; a device's blocks with frames come first and go to distinct devices; every device receives exactly 32 blocks. A device's lengths add up to 4 times the number of its blocks that destination sends.
All inputs are finite; a program needn't handle non-finite values.
Results may differ from a plain program's by a relative error of at most 0.012.
Values may be sent and summed in bfloat16 or wider, within the bound.
No kernel may reach another device: no remote copies, remote signals or barrier semaphores. Data moves between devices by JAX's collectives and lax.ppermute only.
A program may use at most 128 MiB of HBM per device.

v0:
```python
import math

import jax
import jax.numpy as jnp
from jax import lax
from jax.sharding import PartitionSpec as P

ROWS = 128


def adam_step(master, moment, second, gradient):
    moment_new = 0.9 * moment + 0.1 * gradient
    second_new = 0.999 * second + 0.001 * jnp.square(gradient)
    return master - 0.01 * (moment_new / (jnp.sqrt(second_new) + 1e-08) + 0.1 * master)


def layout(lengths_row, height):
    bounds = jnp.cumsum(lengths_row)
    position = jnp.arange(height, dtype=jnp.int32)
    segment = jnp.sum((position[:, None] >= bounds[None, :]).astype(jnp.int32), axis=1)
    living = (position < bounds[-1]).astype(jnp.float32)
    return (segment, living)


def activate(frames_f, kernel, norm_gain, segment, living):
    height = frames_f.shape[0]
    half_width = (kernel.shape[0] - 1) // 2
    padded = jnp.pad(frames_f, ((half_width, half_width), (0, 0)))
    padded_seg = jnp.pad(segment, (half_width, half_width), constant_values=-1)
    mixed_sum = jnp.zeros_like(frames_f)
    for tap_index in range(kernel.shape[0]):
        inside = (lax.slice_in_dim(padded_seg, tap_index, tap_index + height) == segment).astype(
            frames_f.dtype
        )
        mixed_sum = (
            mixed_sum
            + kernel[tap_index]
            * lax.slice_in_dim(padded, tap_index, tap_index + height)
            * inside[:, None]
        )
    mixed_sum = mixed_sum * living[:, None]
    center = jnp.mean(mixed_sum, axis=1, keepdims=True)
    spread = jnp.mean(jnp.square(mixed_sum - center), axis=1, keepdims=True)
    scaled = (mixed_sum - center) * lax.rsqrt(spread + 1e-05) * norm_gain
    return scaled * jax.nn.sigmoid(scaled)


def to_owners(payload, sending, has_block, blocks, block_rows, received_blocks):
    columns = payload.shape[1]
    outgoing = jnp.einsum(
        "pn,nf->pf",
        sending,
        payload.reshape(blocks, block_rows * columns),
        preferred_element_type=jnp.float32,
    ).astype(jnp.bfloat16)
    incoming, arrived = (
        lax.all_to_all(outgoing, "dp", split_axis=0, concat_axis=0, tiled=True),
        lax.all_to_all(has_block, "dp", split_axis=0, concat_axis=0, tiled=True),
    )
    arrived_flag = arrived[:, 0].astype(jnp.float32)
    ranking = jnp.cumsum(arrived_flag) - 1.0
    wanted = jnp.arange(received_blocks).astype(jnp.float32)
    picking = ((ranking[None, :] == wanted[:, None]) & (arrived_flag[None, :] > 0.5)).astype(
        jnp.bfloat16
    )
    compact = jnp.einsum("mp,pf->mf", picking, incoming, preferred_element_type=jnp.float32).astype(
        jnp.bfloat16
    )
    return (compact.reshape(received_blocks * block_rows, columns), picking)


def to_sources(payload, picking, sending, blocks, block_rows, received_blocks):
    columns = payload.shape[1]
    outgoing = jnp.einsum(
        "mp,mf->pf",
        picking,
        payload.reshape(received_blocks, block_rows * columns),
        preferred_element_type=jnp.float32,
    ).astype(jnp.bfloat16)
    incoming = lax.all_to_all(outgoing, "dp", split_axis=0, concat_axis=0, tiled=True)
    homed = jnp.einsum("pn,pf->nf", sending, incoming, preferred_element_type=jnp.float32).astype(
        jnp.bfloat16
    )
    return homed.reshape(blocks * block_rows, columns)


def body(
    frames,
    lengths,
    destination,
    kernel,
    norm_gain,
    master,
    moment,
    second,
    gradient,
    bucket_order,
    cotangent,
):
    owners = lax.axis_size("dp")
    columns = frames.shape[1]
    updated = adam_step(master, moment, second, gradient)
    bucket = updated.astype(jnp.bfloat16)
    bucket_rows = bucket.shape[0]
    gathered = lax.all_gather(bucket, "dp", axis=0, tiled=True)
    weight = jnp.take(gathered.reshape(owners, bucket_rows, columns), bucket_order, axis=0).reshape(
        owners * bucket_rows, columns
    )
    height = frames.shape[0]
    blocks = destination.shape[1]
    block_rows = height // blocks
    received_blocks = cotangent.shape[0] // block_rows
    segment, living = layout(lengths[0], height)
    activated, pullback = jax.vjp(
        lambda inputs, kernel_in, gain_in: activate(inputs, kernel_in, gain_in, segment, living),
        frames.astype(jnp.float32),
        kernel,
        norm_gain,
    )
    moved_rows = activated.astype(jnp.bfloat16)
    targets = jnp.arange(owners, dtype=jnp.int32)
    sending = (destination[0][None, :] == targets[:, None]).astype(jnp.bfloat16)
    has_block = jnp.sum(sending, axis=1, keepdims=True)
    dims_back = (((1,), (1,)), ((), ()))
    source_proj = jnp.dot(moved_rows, weight, preferred_element_type=jnp.float32).astype(
        jnp.bfloat16
    )
    projected, picking = to_owners(
        source_proj, sending, has_block, blocks, block_rows, received_blocks
    )
    cot_home = to_sources(cotangent, picking, sending, blocks, block_rows, received_blocks)
    returned = lax.dot_general(
        cot_home, weight, dims_back, preferred_element_type=jnp.float32
    ).astype(jnp.bfloat16)
    frame_term, kernel_term, gain_term = pullback(returned.astype(jnp.float32))
    kernel_total, gain_total = lax.psum((kernel_term, gain_term), ("rep", "dp"))
    divisor = math.sqrt(lax.axis_size("rep") * owners * ROWS)
    return (
        projected,
        frame_term.astype(jnp.bfloat16),
        kernel_total / divisor,
        gain_total / divisor,
        updated,
    )


def solution(mesh):
    return jax.shard_map(
        body,
        mesh=mesh,
        in_specs=(
            P(("rep", "dp"), None),
            P(("rep", "dp"), None),
            P(("rep", "dp"), None),
            P(),
            P(),
            P("dp", None),
            P("dp", None),
            P("dp", None),
            P("dp", None),
            P(),
            P(("rep", "dp"), None),
        ),
        out_specs=(P(("rep", "dp"), None), P(("rep", "dp"), None), P(), P(), P("dp", None)),
        check_vma=False,
    )
```

profile of v0, /device:TPU:1, one launch (start us, length us, event | category | flops | bytes accessed | tf_op | source)
XLA Modules:
  0.0 658.0 jit_solution(7766027091813819460)
XLA Ops:
  7.2 2.0 fusion.27
  9.3 0.7 fusion.15
  10.0 0.7 copy.26
  10.7 12.9 %all-to-all-start = ((bf16[64,1,1]{2,1,0:T(2,128)(2,1)}), bf16[64,1,1]{2,1,0:T(2,128)(2,1)S(1)}, u32[]{:S(2)}, u32[]{:S(2)}) async-start(bf16[64,1,1]{2,1,0:T(2,128)(2,1)} %copy.26), calls=%async_computation | async-start | bytes 65536 | tf_op jit(solution)/shard_map/all_to_all | solution.py:58
  23.7 0.8 reduce-window.14
  25.1 0.7 compare_select_fusion
  26.4 0.7 compare_and_fusion.3
  27.1 1.3 compare_convert_fusion.13
  28.5 0.7 broadcast_in_dim.23
  29.6 3.3 all-to-all-done
  33.2 1.2 compare_reduce_fusion
  36.0 1.1 reduce.36
  37.1 1.4 reshape.312
  38.6 7.8 %all-to-all-start.2 = ((bf16[64,2,3072]{2,1,0:T(2,128)(2,1)}), bf16[64,2,3072]{2,1,0:T(2,128)(2,1)S(1)}, u32[]{:S(2)}, u32[]{:S(2)}) async-start(bf16[64,2,3072]{2,1,0:T(2,128)(2,1)} %reshape.312), calls=%async_computation.2 | async-start | bytes 1572864 | tf_op jit(solution)/shard_map/all_to_all | solution.py:80
  47.0 3.9 fusion.26
  52.0 19.9 %all-to-all-done.2 = bf16[64,2,3072]{2,1,0:T(2,128)(2,1)S(1)} async-done(((bf16[64,2,3072]{2,1,0:T(2,128)(2,1)}), bf16[64,2,3072]{2,1,0:T(2,128)(2,1)S(1)}, u32[]{:S(2)}, u32[]{:S(2)}) %all-to-all-start.2) | async-done | bytes 786464 | tf_op jit(solution)/shard_map/all_to_all | solution.py:80
  71.9 2.0 reshape.313
  73.8 2.1 convolution_convert_fusion.2
  75.9 1.2 reshape.267
  77.1 206.7 %all-gather.2.cloned.1.call-done = bf16[1536,1536]{1,0:T(8,128)(2,1)} async-done(((bf16[24,1536]{1,0:T(8,128)(2,1)}), bf16[1536,1536]{1,0:T(8,128)(2,1)}) %all-gather.2.cloned.1.call-update) | async-done | bytes 4718608 | tf_op jit(solution)/shard_map/all_gather | solution.py:105
  283.8 5.4 gather_fusion
  289.3 2.9 broadcast_select_fusion
  292.2 2.6 multiply_reduce_fusion
  295.7 3.6 multiply_reduce_fusion.15
  299.4 4.3 multiply_reduce_fusion.5
  303.8 4.6 multiply_multiply_fusion.13
  308.4 0.9 bitcast_select_fusion
  309.3 2.0 convolution_convert_fusion.5
  311.4 2.3 reshape.264
  313.7 0.6 reshape.268
  319.1 1.5 fusion.1
  320.7 1.8 reduce.35
  322.5 3.2 reshape.310
  325.7 7.3 %all-to-all-start.1 = ((bf16[64,2,3072]{2,1,0:T(2,128)(2,1)}), bf16[64,2,3072]{2,1,0:T(2,128)(2,1)}, u32[]{:S(2)}, u32[]{:S(2)}) async-start(bf16[64,2,3072]{2,1,0:T(2,128)(2,1)} %reshape.310), calls=%async_computation.1 | async-start | bytes 1572864 | tf_op jit(solution)/shard_map/all_to_all | solution.py:57
  333.1 0.7 reshape.278
  333.8 0.7 reshape.279
  334.5 0.7 reshape.280
  335.2 0.7 reshape.281
  335.9 1.6 pad_add_fusion.6
  337.5 142.7 %psum.15 = f32[1536]{0:T(1024)S(1)} all-reduce(f32[1536]{0:T(1024)} %get-tuple-element.5), channel_id=1, replica_groups=mesh['rep'=8,'dp'=64] {'rep','dp'}, use_global_device_ids=true, to_apply=%region_26.27 | all-reduce | flops 1536 | bytes 12288 | tf_op jit(solution)/shard_map/psum | solution.py:136
  480.3 5.0 pad_add_fusion
  485.4 1.7 fusion.5
  487.0 0.6 broadcast_multiply_fusion.2
  487.6 155.4 %all-reduce.34.cloned.1.call-done = f32[15,1536]{1,0:T(8,128)} async-done(((f32[15,1536]{1,0:T(8,128)}), f32[15,1536]{1,0:T(8,128)}) %all-reduce.34.cloned.1.call-update) | async-done | bytes 92176 | tf_op jit(solution)/shard_map/psum | solution.py:136
  643.1 1.5 broadcast_multiply_fusion.1
  644.6 4.9 reshape.311
  649.6 0.6 convolution_convert_fusion.3
  650.2 1.0 reshape.265
  (230 shorter events, 10.6 us)
Async XLA Ops:
  7.2 22.0 %copy-start.9 = (bf16[128,1536]{1,0:T(8,128)(2,1)S(1)}, bf16[128,1536]{1,0:T(8,128)(2,1)}, u32[]{:S(2)}) copy-start(bf16[128,1536]{1,0:T(8,128)(2,1)} %param.21) | copy-start | bytes 1179652
  7.2 22.3 %copy-start.6 = (bf16[192,1536]{1,0:T(8,128)(2,1)S(1)}, bf16[192,1536]{1,0:T(8,128)(2,1)}, u32[]{:S(2)}) copy-start(bf16[192,1536]{1,0:T(8,128)(2,1)} %param.11) | copy-start | bytes 1769476
  7.2 276.6 %all-gather.2.cloned.1.call-start = ((), (), s32[]{:S(2)}) async-start(), calls=%async_computation.3 | async-start | bytes 4792320 | tf_op jit(solution)/shard_map/all_gather | solution.py:105
  10.7 22.2 %all-to-all-start = ((bf16[64,1,1]{2,1,0:T(2,128)(2,1)}), bf16[64,1,1]{2,1,0:T(2,128)(2,1)S(1)}, u32[]{:S(2)}, u32[]{:S(2)}) async-start(bf16[64,1,1]{2,1,0:T(2,128)(2,1)} %copy.26), calls=%async_computation | async-start | bytes 65536 | tf_op jit(solution)/shard_map/all_to_all | solution.py:58
  25.1 9.3 %copy-start.91 = (f32[32]{0:T(128)}, f32[32]{0:T(128)S(1)}, u32[]{:S(2)}) copy-start(f32[32]{0:T(128)S(1)} %iota_convert_fusion) | copy-start | bytes 388
  38.5 7.9 %copy-start.10 = (f32[15,1536]{1,0:T(8,128)S(1)}, f32[15,1536]{1,0:T(8,128)}, u32[]{:S(2)}) copy-start(f32[15,1536]{1,0:T(8,128)} %param.14) | copy-start | bytes 276484
  38.5 8.4 %copy-start.48 = (f32[192]{0:T(256)S(1)}, f32[192]{0:T(256)}, u32[]{:S(2)}) copy-start(f32[192]{0:T(256)} %get-tuple-element.71) | copy-start | bytes 2308
  38.5 8.4 %copy-start.68 = (f32[192]{0:T(256)S(1)}, f32[192]{0:T(256)}, u32[]{:S(2)}) copy-start(f32[192]{0:T(256)} %get-tuple-element.67) | copy-start | bytes 2308
  38.5 8.4 %copy-start.70 = (f32[192]{0:T(256)S(1)}, f32[192]{0:T(256)}, u32[]{:S(2)}) copy-start(f32[192]{0:T(256)} %get-tuple-element.68) | copy-start | bytes 2308
  38.5 8.5 %copy-start.72 = (f32[192]{0:T(256)S(1)}, f32[192]{0:T(256)}, u32[]{:S(2)}) copy-start(f32[192]{0:T(256)} %get-tuple-element.69) | copy-start | bytes 2308
  38.6 8.5 %copy-start.74 = (f32[192]{0:T(256)S(1)}, f32[192]{0:T(256)}, u32[]{:S(2)}) copy-start(f32[192]{0:T(256)} %get-tuple-element.70) | copy-start | bytes 2308
  38.6 8.5 %copy-start.76 = (f32[192]{0:T(256)S(1)}, f32[192]{0:T(256)}, u32[]{:S(2)}) copy-start(f32[192]{0:T(256)} %get-tuple-element.73) | copy-start | bytes 2308
  38.6 33.3 %all-to-all-start.2 = ((bf16[64,2,3072]{2,1,0:T(2,128)(2,1)}), bf16[64,2,3072]{2,1,0:T(2,128)(2,1)S(1)}, u32[]{:S(2)}, u32[]{:S(2)}) async-start(bf16[64,2,3072]{2,1,0:T(2,128)(2,1)} %reshape.312), calls=%async_computation.2 | async-start | bytes 1572864 | tf_op jit(solution)/shard_map/all_to_all | solution.py:80
  51.1 22.7 %copy-start.66 = (f32[192]{0:T(256)}, f32[192]{0:T(256)S(1)}, u32[]{:S(2)}) copy-start(f32[192]{0:T(256)S(1)} %broadcast_multiply_fusion.3) | copy-start | bytes 2308
  51.4 22.4 %copy-start.80 = (f32[192]{0:T(256)}, f32[192]{0:T(256)S(1)}, u32[]{:S(2)}) copy-start(f32[192]{0:T(256)S(1)} %multiply_reduce_fusion.17) | copy-start | bytes 2308
  52.0 21.9 %copy-start.89 = (s32[1,48]{1,0:T(1,128)S(1)}, s32[1,48]{1,0:T(1,128)}, u32[]{:S(2)}) copy-start(s32[1,48]{1,0:T(1,128)} %param.13) | copy-start | bytes 580
  283.8 5.4 copy-start.94
  299.3 4.4 copy-start.20
  299.3 4.4 copy-start.22
  299.3 4.3 copy-start.24
  299.4 4.3 copy-start.26
  299.4 4.3 copy-start.28
  299.4 4.3 copy-start.30
  299.4 4.3 copy-start.32
  299.4 4.3 copy-start.34
  299.4 4.3 copy-start.36
  299.4 9.0 %slice-start = ((s8[4718592]{0:T(1024)(128)(4,1)}), s8[4194304]{0:T(1024)(128)(4,1)S(1)}, s32[]{:S(2)}) async-start(s8[4718592]{0:T(1024)(128)(4,1)} %bitcast.25), calls=%async_computation.5 | async-start | bytes 8388608
  303.7 4.6 slice-start.1
  303.8 4.6 copy-start.83
  311.3 4.8 copy-start.43
  311.3 5.4 copy-start.42
  311.3 6.0 copy-start.41
  311.3 6.6 copy-start.40
  311.4 7.2 %copy-start.39 = (f32[1536]{0:T(1024)S(1)}, f32[1536]{0:T(1024)}, u32[]{:S(2)}) copy-start(f32[1536]{0:T(1024)} %get-tuple-element.15) | copy-start | bytes 18436
  311.4 7.8 %copy-start.90 = (s32[1,48]{1,0:T(1,128)S(1)}, s32[1,48]{1,0:T(1,128)}, u32[]{:S(2)}) copy-start(s32[1,48]{1,0:T(1,128)} %param.13) | copy-start | bytes 580
  325.7 10.2 %copy-start.38 = (f32[1536]{0:T(1024)S(1)}, f32[1536]{0:T(1024)}, u32[]{:S(2)}) copy-start(f32[1536]{0:T(1024)} %get-tuple-element.20) | copy-start | bytes 18436
  325.7 10.2 %copy-start.37 = (f32[1536]{0:T(1024)S(1)}, f32[1536]{0:T(1024)}, u32[]{:S(2)}) copy-start(f32[1536]{0:T(1024)} %get-tuple-element.22) | copy-start | bytes 18436
  325.7 154.5 %copy-start = (f32[192,1536]{1,0:T(8,128)S(1)}, f32[192,1536]{1,0:T(8,128)}, u32[]{:S(2)}) copy-start(f32[192,1536]{1,0:T(8,128)} %get-tuple-element.50) | copy-start | bytes 3538948
  325.7 318.9 %all-to-all-start.1 = ((bf16[64,2,3072]{2,1,0:T(2,128)(2,1)}), bf16[64,2,3072]{2,1,0:T(2,128)(2,1)}, u32[]{:S(2)}, u32[]{:S(2)}) async-start(bf16[64,2,3072]{2,1,0:T(2,128)(2,1)} %reshape.310), calls=%async_computation.1 | async-start | bytes 1572864 | tf_op jit(solution)/shard_map/all_to_all | solution.py:57
  333.0 310.1 %all-reduce.34.cloned.1.call-start = ((), (), s32[]{:S(2)}) async-start(), calls=%async_computation.4 | async-start | bytes 196608 | tf_op jit(solution)/shard_map/psum | solution.py:136
  480.2 5.1 copy-start.1
  480.2 5.1 copy-start.2
  480.2 5.1 copy-start.3
  480.2 5.1 copy-start.4
  480.2 5.1 copy-start.5
  644.6 4.9 copy-start.85
  644.6 4.9 copy-start.87
  644.6 4.9 copy-start.92
  (54 other events, 168.3 us)
Sparse Core Ops, SparseCore 0:
  10.7 273.0 all-gather.1
  339.4 303.6 all-reduce.33
where the time goes:
time: 659 us; the launch traced here: 658 us
  waiting for transfers between devices  385 us (58%)
  blocking collectives  143 us (22%)
  other arithmetic  43.2 us (7%)
  local copies, waits for them, and re-layouts  34.2 us (5%)
  starting transfers between devices  28.1 us (4%)
  between operations  15.3 us (2%)
  matrix products  9.28 us (1%)
    all_gather x1, waiting for transfers between devices, body(): gathered = lax.all_gather(bucket, 'dp', axis=0, tiled=True)  207 us
    psum x1, waiting for transfers between devices, body(): kernel_total, gain_total = lax.psum((kernel_term, gain_term), ('rep', 'dp'))  155 us
    psum x1, blocking collectives, body(): kernel_total, gain_total = lax.psum((kernel_term, gain_term), ('rep', 'dp'))  143 us
    all_to_all x1, waiting for transfers between devices, to_sources(): lax.all_to_all(outgoing, 'dp', split_axis=0, concat_axis=0, tiled=True)  19.9 us
  transfers between devices with their start and end apart: 5, of which 4 were waited for; matrix products, arithmetic and copies ran while one was open for 5% of the time, Pallas kernels for 0%

commit v1 on v0

v1 whole, which is shorter than its diff:
```python
import functools
import math

import jax
import jax.numpy as jnp
import numpy as np
from jax import lax
from jax.experimental import pallas as pl
from jax.experimental.pallas import tpu as pltpu
from jax.sharding import Mesh, PartitionSpec as P

ROWS = 128
BLK = 4
CHUNK = 256
DP = ("zl", "x", "y")
NEAR = ("c", "zl", "x")
FAR = ("zh", "y")
F32 = jnp.float32
BF16 = jnp.bfloat16


def params(mib):
    return pltpu.CompilerParams(vmem_limit_bytes=mib * 1024 * 1024)


def adam_step(master, moment, second, gradient):
    moment_new = 0.9 * moment + 0.1 * gradient
    second_new = 0.999 * second + 0.001 * jnp.square(gradient)
    return master - 0.01 * (moment_new / (jnp.sqrt(second_new) + 1e-08) + 0.1 * master)


def write_shifts(lengths_ref, shift_ref):
    taps, height, _ = shift_ref.shape
    half = (taps - 1) // 2
    row = lax.broadcasted_iota(jnp.int32, (height, height), 0)
    col = lax.broadcasted_iota(jnp.int32, (height, height), 1)
    bound = jnp.int32(0)
    row_seg = jnp.zeros((height, height), jnp.int32)
    col_seg = jnp.zeros((height, height), jnp.int32)
    for u in range(lengths_ref.shape[0]):
        bound = bound + lengths_ref[u]
        row_seg = row_seg + jnp.where(row >= bound, 1, 0)
        col_seg = col_seg + jnp.where(col >= bound, 1, 0)
    same = (row_seg == col_seg) & (row < bound)
    offset = jnp.where(same, col - row + half, -1)
    for j in range(taps):
        shift_ref[j] = jnp.where(offset == j, 1.0, 0.0).astype(F32).astype(BF16)


def forward_kernel(lengths_ref, dest_ref, frames_ref, kernel_ref, gain_ref, slots_ref, mixed_ref, shift_ref, act_ref):
    taps, height, _ = shift_ref.shape
    columns = frames_ref.shape[1]
    write_shifts(lengths_ref, shift_ref)

    def conv(i, carry):
        at = pl.ds(pl.multiple_of(i * CHUNK, CHUNK), CHUNK)
        piece = frames_ref[:, at]
        total = jnp.zeros((height, CHUNK), F32)
        for j in range(taps):
            total = total + kernel_ref[pl.ds(j, 1), at] * jnp.dot(shift_ref[j], piece, preferred_element_type=F32)
        mixed_ref[:, at] = total
        return carry

    lax.fori_loop(0, columns // CHUNK, conv, 0)
    step = 16

    def norm(i, carry):
        at = pl.ds(pl.multiple_of(i * step, step), step)
        mixed = mixed_ref[at, :]
        center = jnp.mean(mixed, axis=1, keepdims=True)
        off = mixed - center
        spread = jnp.mean(off * off, axis=1, keepdims=True)
        scaled = off * lax.rsqrt(spread + 1e-05) * gain_ref[...]
        act_ref[at, :] = scaled * jax.nn.sigmoid(scaled)
        return carry

    lax.fori_loop(0, height // step, norm, 0)
    for b in range(height // BLK):
        where = dest_ref[b]

        @pl.when(where >= 0)
        def _():
            slots_ref[where] = act_ref[b * BLK : (b + 1) * BLK, :].astype(BF16)


def find_senders(flags_ref, table_ref):
    for k in range(table_ref.shape[0]):
        table_ref[k] = 0

    def look(s, count):
        sends = flags_ref[s] > 0

        @pl.when(sends)
        def _():
            table_ref[count] = s

        return count + jnp.where(sends, 1, 0)

    lax.fori_loop(0, flags_ref.shape[0], look, jnp.int32(0))


def scatter_kernel(flags_ref, cot_ref, slots_ref, table_ref):
    find_senders(flags_ref, table_ref)
    for k in range(cot_ref.shape[0] // BLK):
        base = k // 4 * 16
        rows = cot_ref[base : base + 16, :].astype(F32)
        low = k % 4 * BLK
        slots_ref[table_ref[k]] = rows[low : low + BLK, :].astype(BF16)


def load_weight(place_ref, own, cross, weight_ref, sems):
    size, width = own[0].shape
    part = size // 2
    core = place_ref[1]
    copies = []
    for h in range(2):
        start = core * width if h == 0 else (1 - core) * width
        at = pl.ds(pl.multiple_of(start, 128), width)
        pairs = [(own[h], 0, size), (cross[h][0], size, part), (cross[h][1], size + part, part)]
        for source, row, count in pairs:
            copies.append(
                pltpu.make_async_copy(source, weight_ref.at[pl.ds(row, count), at], sems.at[len(copies)])
            )
    for copy in copies:
        copy.start()
    return copies


def block_place(place_ref, owner, blocks):
    nx, ny = 4, blocks // 8
    other = jnp.where(owner // (ny * nx) != place_ref[0], blocks // 2, 0)
    return other + owner % ny * nx + owner // ny % nx


def backward_kernel(
    lengths_ref, dest_ref, place_ref, order_ref,
    frames_ref, kernel_ref, gain_ref, mixed_ref, slots_ref, o0, o1, c00, c01, c10, c11,
    frame_ref, term_ref,
    shift_ref, home_ref, homeb_ref, weight_ref, raw_ref, sorted_ref, grad_ref, gradb_ref, sems,
):
    taps, height, _ = shift_ref.shape
    columns = frames_ref.shape[1]
    blocks = order_ref.shape[0]
    size = columns // blocks
    copies = load_weight(place_ref, (o0, o1), ((c00, c01), (c10, c11)), weight_ref, sems)
    write_shifts(lengths_ref, shift_ref)
    for b in range(height // BLK):
        where = dest_ref[b]
        rows = slots_ref[jnp.maximum(where, 0)].astype(F32)
        home_ref[b * BLK : (b + 1) * BLK, :] = jnp.where(where >= 0, rows, 0.0)
    homeb_ref[...] = home_ref[...].astype(BF16)
    for copy in copies:
        copy.wait()

    def back(i, carry):
        at = pl.ds(pl.multiple_of(i * CHUNK, CHUNK), CHUNK)
        raw_ref[at, :] = lax.dot_general(
            weight_ref[at, :], homeb_ref[...], (((1,), (1,)), ((), ())), preferred_element_type=F32
        )
        return carry

    lax.fori_loop(0, columns // CHUNK, back, 0)

    def order(b, carry):
        at = pl.multiple_of(block_place(place_ref, order_ref[b], blocks) * size, 8)
        sorted_ref[pl.ds(pl.multiple_of(b * size, 8), size), :] = raw_ref[pl.ds(at, size), :]
        return carry

    lax.fori_loop(0, blocks, order, 0)

    def turn(i, carry):
        at = pl.ds(pl.multiple_of(i * CHUNK, CHUNK), CHUNK)
        home_ref[:, at] = sorted_ref[at, :].T.astype(BF16).astype(F32)
        return carry

    lax.fori_loop(0, columns // CHUNK, turn, 0)
    step = 8
    gain = gain_ref[...]

    def norm(i, total):
        at = pl.ds(pl.multiple_of(i * step, step), step)
        mixed = mixed_ref[at, :]
        center = jnp.mean(mixed, axis=1, keepdims=True)
        off = mixed - center
        inv = lax.rsqrt(jnp.mean(off * off, axis=1, keepdims=True) + 1e-05)
        unit = off * inv
        scaled = unit * gain
        sig = jax.nn.sigmoid(scaled)
        slope = home_ref[at, :] * (sig * (1.0 + scaled * (1.0 - sig)))
        total = total + slope * unit
        slope = slope * gain
        mean_slope = jnp.mean(slope, axis=1, keepdims=True)
        mean_unit = jnp.mean(slope * unit, axis=1, keepdims=True)
        grad_ref[at, :] = inv * (slope - mean_slope - unit * mean_unit)
        return total

    total = lax.fori_loop(0, height // step, norm, jnp.zeros((step, columns), F32))
    term_ref[taps] = jnp.sum(total, axis=0, keepdims=True)
    gradb_ref[...] = grad_ref[...].astype(BF16)

    def conv(i, carry):
        at = pl.ds(pl.multiple_of(i * CHUNK, CHUNK), CHUNK)
        piece = frames_ref[:, at]
        grad = grad_ref[:, at]
        gradb = gradb_ref[:, at]
        out = jnp.zeros((height, CHUNK), F32)
        for j in range(taps):
            moved = jnp.dot(shift_ref[j], piece, preferred_element_type=F32)
            term_ref[j, :, at] = jnp.sum(grad * moved, axis=0, keepdims=True)
            out = out + kernel_ref[pl.ds(taps - 1 - j, 1), at] * jnp.dot(shift_ref[j], gradb, preferred_element_type=F32)
        frame_ref[:, at] = out.astype(BF16)
        return carry

    lax.fori_loop(0, columns // CHUNK, conv, 0)


def project_kernel(
    flags_ref, place_ref, order_ref,
    slots_ref, o0, o1, c00, c01, c10, c11,
    out_ref,
    table_ref, rows_ref, turned_ref, weight_ref, sems,
):
    blocks = order_ref.shape[0]
    size = weight_ref.shape[0] // blocks
    copies = load_weight(place_ref, (o0, o1), ((c00, c01), (c10, c11)), weight_ref, sems)
    find_senders(flags_ref, table_ref)
    for k in range(rows_ref.shape[0] // BLK):
        rows_ref[k * BLK : (k + 1) * BLK, :] = slots_ref[table_ref[k]].astype(F32)
    turned = rows_ref[...].T
    for b in range(blocks):
        at = pl.multiple_of(block_place(place_ref, order_ref[b], blocks) * size, 8)
        turned_ref[pl.ds(at, size), :] = turned[b * size : (b + 1) * size, :]
    rows = turned_ref[...].T.astype(BF16)
    for copy in copies:
        copy.wait()
    out_ref[...] = jnp.dot(rows, weight_ref[...], preferred_element_type=F32).astype(BF16)


VM = pl.BlockSpec(memory_space=pltpu.VMEM)
SM = pl.BlockSpec(memory_space=pltpu.SMEM)
HB = pl.BlockSpec(memory_space=pl.ANY)


def call(fn, ins, outs, scratch, mib, name, flops, nbytes):
    return pl.pallas_call(
        fn,
        in_specs=ins,
        out_specs=[VM] * len(outs),
        out_shape=outs,
        scratch_shapes=scratch,
        compiler_params=params(mib),
        cost_estimate=pl.CostEstimate(flops=flops, transcendentals=0, bytes_accessed=nbytes),
        name=name,
    )


def exchange(x, axes):
    return lax.all_to_all(x, axes, split_axis=0, concat_axis=0, tiled=True)


def body(frames, lengths, destination, kernel, norm_gain, master, moment, second, gradient, bucket_order, cotangent):
    height, columns = frames.shape
    taps = kernel.shape[0]
    owners = bucket_order.shape[0]
    half = columns // 2
    core, zl = lax.axis_index("c"), lax.axis_index("zl")
    dest = destination[0]
    lens = lengths[0]
    place = jnp.stack([zl, core]).astype(jnp.int32)
    gain = norm_gain[None, :]

    sends = jnp.any(dest[None, :] == jnp.arange(owners, dtype=jnp.int32)[:, None], axis=1).astype(jnp.int32)
    flags = exchange(jnp.broadcast_to(sends[:, None, None], (owners, 1, 128)), DP)[:, 0, 0]

    updated = adam_step(master, moment, second, gradient)
    bucket = lax.dynamic_slice_in_dim(updated, core * half, half, axis=1).astype(BF16)
    near = lax.all_gather(bucket, "x", axis=0, tiled=True)
    own = lax.all_gather(near, "y", axis=0, tiled=True)
    slots = jax.ShapeDtypeStruct((owners, BLK, columns), BF16)
    sent, mixed = call(
        forward_kernel,
        [SM, SM, VM, VM, VM],
        [slots, jax.ShapeDtypeStruct((height, columns), F32)],
        [pltpu.VMEM((taps, height, height), BF16), pltpu.VMEM((height, columns), F32)],
        40,
        "forward",
        8 * taps * height * height * columns,
        16 * height * columns,
    )(lens, dest, frames, kernel, gain)

    own, sent = lax.optimization_barrier((own, sent))
    part = own.shape[0] // 2
    nz = lax.axis_size("zh") * lax.axis_size("zl")
    up = [(i, (i + 1) % nz) for i in range(nz)]
    down = [((i + 1) % nz, i) for i in range(nz)]
    swap = [(0, 1), (1, 0)]
    c00 = lax.ppermute(own[:part], ("zh", "zl"), up)
    c01 = lax.ppermute(own[part:], ("zh", "zl"), down)
    own1 = lax.ppermute(own, "c", swap)
    c10 = lax.ppermute(c00, "c", swap)
    c11 = lax.ppermute(c01, "c", swap)
    pieces = (own, own1, c00, c01, c10, c11)

    (cot_sent,) = call(
        scatter_kernel, [SM, VM], [slots], [pltpu.SMEM((owners,), jnp.int32)], 40, "scatter", 0, 6 * cotangent.size
    )(flags, cotangent)
    cot_slots = exchange(cot_sent, DP)
    sent, cot_slots = lax.optimization_barrier((sent, cot_slots))
    act_slots = exchange(sent, DP)

    frame_grad, term = call(
        backward_kernel,
        [SM] * 4 + [VM] * 5 + [HB] * 6,
        [
            jax.ShapeDtypeStruct((height, columns), BF16),
            jax.ShapeDtypeStruct((taps + 1, 1, columns), F32),
        ],
        [
            pltpu.VMEM((taps, height, height), BF16),
            pltpu.VMEM((height, columns), F32),
            pltpu.VMEM((height, columns), BF16),
            pltpu.VMEM((columns, columns), BF16),
            pltpu.VMEM((columns, height), F32),
            pltpu.VMEM((columns, height), F32),
            pltpu.VMEM((height, columns), F32),
            pltpu.VMEM((height, columns), BF16),
            pltpu.SemaphoreType.DMA((6,)),
        ],
        48,
        "backward",
        8 * taps * height * height * columns + 2 * height * columns * columns,
        16 * height * columns + 2 * columns * columns,
    )(lens, dest, place, bucket_order, frames, kernel, gain, mixed, cot_slots, *pieces)

    mine = jnp.sum(exchange(term, NEAR), axis=0, keepdims=True)
    far = lax.axis_size(FAR)
    mine = jnp.sum(exchange(jnp.broadcast_to(mine, (far, 1, columns)), FAR), axis=0, keepdims=True)
    divisor = math.sqrt(lax.axis_size(("zh", "c")) * owners * ROWS)
    sums = exchange(jnp.broadcast_to(mine / divisor, (taps + 1, 1, columns)), NEAR)[:, 0, :]

    (projected,) = call(
        project_kernel,
        [SM] * 3 + [VM] + [HB] * 6,
        [jax.ShapeDtypeStruct(cotangent.shape, BF16)],
        [
            pltpu.SMEM((owners,), jnp.int32),
            pltpu.VMEM(cotangent.shape, F32),
            pltpu.VMEM(cotangent.shape[::-1], F32),
            pltpu.VMEM((columns, columns), BF16),
            pltpu.SemaphoreType.DMA((6,)),
        ],
        40,
        "project",
        2 * cotangent.size * columns,
        4 * cotangent.size + 2 * columns * columns,
    )(flags, place, bucket_order, act_slots, *pieces)
    return projected, frame_grad, sums[:taps], sums[taps], updated


def solution(mesh):
    fine = Mesh(mesh.devices.reshape(4, 2, 2, 4, 8), ("zh", "c", "zl", "x", "y"))
    rep, dp = ("zh", "c"), ("zl", "x", "y")
    every, rows = P(rep + dp, None), P(dp, None)
    return jax.shard_map(
        body,
        mesh=fine,
        in_specs=(every, every, every, P(), P(), rows, rows, rows, rows, P(), every),
        out_specs=(every, every, P(), P(), rows),
        check_vma=False,
    )
```

time: 659 us -> 211 us (0.32)
  waiting for transfers between devices: 385 us -> 55.9 us
  blocking collectives: 143 us -> 43 us
  other arithmetic: 43.2 us -> 2.31 us
  Pallas kernels: 0 us -> 34.4 us
  local copies, waits for them, and re-layouts: 34.2 us -> 13.5 us
  starting transfers between devices: 28.1 us -> 46.9 us
  matrix products: 9.28 us -> 0 us
    all_gather x1, waiting for transfers between devices: 207 us -> 12.3 us  [body(): own = lax.all_gather(near, 'y', axis=0, tiled=True)]
    psum x1 -> x0, waiting for transfers between devices: 155 us -> none  [body(): kernel_total, gain_total = lax.psum((kernel_term, gain_term), ('rep', 'dp'))]
    psum x1 -> x0, blocking collectives: 143 us -> none  [body(): kernel_total, gain_total = lax.psum((kernel_term, gain_term), ('rep', 'dp'))]
    pallas_call x0 -> x4, Pallas kernels: none -> 34.4 us  [the longest x1 20.9 us: body(): call(backward_kernel, [SM] * 4 + [VM] * 5 + [HB] * 6, [jax.ShapeDtypeStru...]
    all_to_all x0 -> x2, blocking collectives: none -> 32 us  [exchange(): return lax.all_to_all(x, axes, split_axis=0, concat_axis=0, tiled=True)]
    ppermute x0 -> x5, starting transfers between devices: none -> 17.2 us  [the longest x1 6.06 us: body(): own1 = lax.ppermute(own, 'c', swap)]
    ppermute x0 -> x5, waiting for transfers between devices: none -> 13.5 us  [the longest x1 11.5 us: body(): c00 = lax.ppermute(own[:part], ('zh', 'zl'), up)]
    reshape x19 -> x0, local copies, waits for them, and re-layouts: 13 us -> none  [the longest x15 8.18 us: activate(): kernel[tap_index] * lax.slice_in_dim(padded, tap_index, tap_index + height)]
  transfers between devices with their start and end apart: 5 -> 10, of which waited for: 4 -> 5; matrix products, arithmetic and copies ran while one was open for 5% -> 2% of each run, Pallas kernels for 0% -> 6%
where the time goes in v1:
time: 211 us
  waiting for transfers between devices  55.9 us (26%)
  starting transfers between devices  46.9 us (22%)
  blocking collectives  43 us (20%)
  Pallas kernels  34.4 us (16%)
  between operations  14.4 us (7%)
  local copies, waits for them, and re-layouts  13.5 us (6%)
  other arithmetic  2.31 us (1%)
    all_to_all x2, blocking collectives, exchange(): return lax.all_to_all(x, axes, split_axis=0, concat_axis=0, tiled=True)  32 us
    all_to_all x4, waiting for transfers between devices, exchange(): return lax.all_to_all(x, axes, split_axis=0, concat_axis=0, tiled=True)  30.2 us
    all_to_all x4, starting transfers between devices, exchange(): return lax.all_to_all(x, axes, split_axis=0, concat_axis=0, tiled=True)  29.6 us
    pallas_call x1, Pallas kernels, body(): call(backward_kernel, [SM] * 4 + [VM] * 5 + [HB] * 6, [jax.ShapeDtypeStru...  20.9 us
    all_gather x1, waiting for transfers between devices, body(): own = lax.all_gather(near, 'y', axis=0, tiled=True)  12.3 us
    ppermute x1, waiting for transfers between devices, body(): c00 = lax.ppermute(own[:part], ('zh', 'zl'), up)  11.5 us
    all_gather x1, blocking collectives, body(): near = lax.all_gather(bucket, 'x', axis=0, tiled=True)  11.1 us
    unnamed x39, local copies, waits for them, and re-layouts  8.71 us
  transfers between devices with their start and end apart: 10, of which 5 were waited for; matrix products, arithmetic and copies ran while one was open for 2% of the time, Pallas kernels for 6%

profile of v1, /device:TPU:1, one launch (start us, length us, event | category | flops | bytes accessed | tf_op | source)
XLA Modules:
  0.0 210.5 jit_solution(2149681556449834140)
XLA Ops:
  7.2 0.0 all-gather.2.cloned.1.call-start
  7.2 1.3 multiply_subtract_fusion
  8.5 0.0 copy-start.17
  8.6 11.1 %all_gather.6 = bf16[96,768]{1,0:T(8,128)(2,1)} all-gather(bf16[24,768]{1,0:T(8,128)(2,1)S(1)} %dynamic-slice_convert_fusion), channel_id=1, replica_groups=mesh['zh'=4,'c'=2,'zl'=2,'x'=4,'y'=8] {'x'}, dimensions={0}, use_global_device_ids=true | all-gather | bytes 184320 | tf_op jit(solution)/shard_map/all_gather | solution.py:277
  19.6 0.0 all-gather.2.cloned.1.call-update
  19.6 0.7 fusion
  20.4 0.8 broadcast_in_dim.8
  21.1 11.5 %all-to-all-start = ((s32[64,1,128]{2,1,0:T(1,128)}), s32[64,1,128]{2,1,0:T(1,128)S(1)}, u32[]{:S(2)}, u32[]{:S(2)}) async-start(s32[64,1,128]{2,1,0:T(1,128)} %broadcast_in_dim.8), calls=%async_computation | async-start | bytes 65536 | tf_op jit(solution)/shard_map/all_to_all | solution.py:258
  32.7 9.2 %all-to-all-done = s32[64,1,128]{2,1,0:T(1,128)S(1)} async-done(((s32[64,1,128]{2,1,0:T(1,128)}), s32[64,1,128]{2,1,0:T(1,128)S(1)}, u32[]{:S(2)}, u32[]{:S(2)}) %all-to-all-start) | async-done | bytes 32800 | tf_op jit(solution)/shard_map/all_to_all | solution.py:258
  41.9 1.3 slice_reduce_fusion.flags_ref
  43.1 0.0 copy-start.10
  43.2 0.0 copy-start.12
  43.2 0.0 copy-start.13
  43.2 0.0 copy-start.14
  43.2 2.1 %scatter.1 = bf16[64,4,1536]{2,1,0:T(4,128)(2,1)} custom-call(s32[64]{0:T(128)S(1)} %slice_reduce_fusion.flags_ref, bf16[128,1536]{1,0:T(8,128)(2,1)S(1)} %copy-done.8), custom_call_target="tpu_custom_call" | custom-call | bytes 1179648 | tf_op jit(solution)/shard_map/scatter/pallas_call | solution.py:304
  45.3 4.6 %all-to-all-start.1 = ((bf16[64,4,1536]{2,1,0:T(4,128)(2,1)}), bf16[64,4,1536]{2,1,0:T(4,128)(2,1)S(1)}, u32[]{:S(2)}, u32[]{:S(2)}) async-start(bf16[64,4,1536]{2,1,0:T(4,128)(2,1)} %scatter.1), calls=%async_computation.1 | async-start | bytes 1572864 | tf_op jit(solution)/shard_map/all_to_all | solution.py:258
  50.0 7.2 %forward.1 = (bf16[64,4,1536]{2,1,0:T(4,128)(2,1)S(1)}, f32[192,1536]{1,0:T(8,128)S(1)}) custom-call(s32[8]{0:T(128)S(1)} %bitcast.10, s32[48]{0:T(128)S(1)} %bitcast.8, bf16[192,1536]{1,0:T(8,128)(2,1)S(1)} %copy-done.10, f32[15,1536]{1,0:T(8,128)S(1)} %copy-done.12, f32[1,1536]{1,0:T(1,128)S(1)} %broadcast_in_dim.9.gain_ref), custom_call_target="tpu_custom_call" | custom-call | flops 6794772480 | bytes 4718592 | tf_op jit(solution)/shard_map/forward/pallas_call | solution.py:280
  57.2 0.9 copy-done.3
  58.1 1.0 copy-done.15
  59.1 12.3 %all-gather.2.cloned.1.call-done.o0 = bf16[768,768]{1,0:T(8,128)(2,1)} async-done(((bf16[96,768]{1,0:T(8,128)(2,1)}), bf16[768,768]{1,0:T(8,128)(2,1)}) %all-gather.2.cloned.1.call-update) | async-done | bytes 1179664 | tf_op jit(solution)/shard_map/all_gather | solution.py:278
  71.4 6.1 %collective-permute-start = (bf16[768,768]{1,0:T(8,128)(2,1)}, bf16[768,768]{1,0:T(8,128)(2,1)S(1)}, u32[]{:S(2)}, u32[]{:S(2)}) collective-permute-start(bf16[768,768]{1,0:T(8,128)(2,1)} %all-gather.2.cloned.1.call-done.o0), channel_id=1, source_target_pairs={{0,64},{64,0},{1,65},{65,1},{2,66},{66,2},{3,67},{67,3},{4,68},{68... | collective-permute-start | bytes 3538952 | tf_op jit(solution)/shard_map/ppermute | solution.py:299
  77.5 1.3 fusion.1
  78.8 3.2 %collective-permute-start.1 = (bf16[384,768]{1,0:T(8,128)(2,1)S(1)}, bf16[384,768]{1,0:T(8,128)(2,1)S(1)}, u32[]{:S(2)}, u32[]{:S(2)}) collective-permute-start(bf16[384,768]{1,0:T(8,128)(2,1)S(1)} %get-tuple-element.22), channel_id=1, source_target_pairs={{0,32},{32,128},{128,160},{160,256},{256,288},{288,384},{384,416},... | collective-permute-start | bytes 1769480 | tf_op jit(solution)/shard_map/ppermute | solution.py:297
  82.0 3.3 %collective-permute-start.2 = (bf16[384,768]{1,0:T(8,128)(2,1)S(1)}, bf16[384,768]{1,0:T(8,128)(2,1)S(1)}, u32[]{:S(2)}, u32[]{:S(2)}) collective-permute-start(bf16[384,768]{1,0:T(8,128)(2,1)S(1)} %get-tuple-element.21), channel_id=1, source_target_pairs={{32,0},{128,32},{160,128},{256,160},{288,256},{384,288},{416,384},... | collective-permute-start | bytes 1769480 | tf_op jit(solution)/shard_map/ppermute | solution.py:298
  85.3 11.5 %collective-permute-done.1.c00 = bf16[384,768]{1,0:T(8,128)(2,1)S(1)} collective-permute-done((bf16[384,768]{1,0:T(8,128)(2,1)S(1)}, bf16[384,768]{1,0:T(8,128)(2,1)S(1)}, u32[]{:S(2)}, u32[]{:S(2)}) %collective-permute-start.1) | collective-permute-done | bytes 589856 | tf_op jit(solution)/shard_map/ppermute | solution.py:297
  96.9 2.7 %collective-permute-start.3 = (bf16[384,768]{1,0:T(8,128)(2,1)S(1)}, bf16[384,768]{1,0:T(8,128)(2,1)}, u32[]{:S(2)}, u32[]{:S(2)}) collective-permute-start(bf16[384,768]{1,0:T(8,128)(2,1)S(1)} %collective-permute-done.1.c00), channel_id=1, source_target_pairs={{0,64},{64,0},{1,65},{65,1},{2,66},{66,2},{3,67},{67,3},{4,68},{68... | collective-permute-start | bytes 1769480 | tf_op jit(solution)/shard_map/ppermute | solution.py:300
  99.6 2.0 collective-permute-start.4
  101.6 0.1 pad_add_fusion.place_ref
  101.7 1.9 collective-permute-done.4.c11
  103.6 1.1 copy-done.11
  104.7 1.3 copy-done.16
  106.0 20.9 %backward.1 = (bf16[192,1536]{1,0:T(8,128)(2,1)}, f32[16,1,1536]{2,1,0:T(1,128)S(1)}) custom-call(s32[8]{0:T(128)S(1)} %bitcast.11, s32[48]{0:T(128)S(1)} %bitcast.9, s32[2]{0:T(128)S(1)} %pad_add_fusion.place_ref, s32[64]{0:T(128)S(1)} %copy-done.9, bf16[192,1536]{1,0:T(8,128)(2,1)S(1)} %copy-done.11, f32[15,1536]{1,0:T(8,128)S(1)} %copy-done.12, ...), custom_call_target="tpu_custom_call" | custom-call | flops 7700742144 | bytes 9437184 | tf_op jit(solution)/shard_map/backward/pallas_call | solution.py:311
  126.9 0.8 copy-done.4
  127.7 0.8 copy-done.6
  128.5 11.3 %all_to_all.30 = f32[16,1,1536]{2,1,0:T(1,128)S(1)} all-to-all(f32[16,1,1536]{2,1,0:T(1,128)S(1)} %get-tuple-element.20), channel_id=1, replica_groups=mesh['zh'=4,'c'=2,'zl'=2,'x'=4,'y'=8] {'c','zl','x'}, dimensions={0} | all-to-all | bytes 196608 | tf_op jit(solution)/shard_map/all_to_all | solution.py:258
  139.8 0.1 reduce_sum.18
  139.9 0.1 broadcast_in_dim.10
  140.0 20.7 %all_to_all.31 = f32[32,1,1536]{2,1,0:T(1,128)S(1)} all-to-all(f32[32,1,1536]{2,1,0:T(1,128)S(1)} %broadcast_in_dim.10), channel_id=1, replica_groups=mesh['zh'=4,'c'=2,'zl'=2,'x'=4,'y'=8] {'zh','y'}, dimensions={0} | all-to-all | bytes 393216 | tf_op jit(solution)/shard_map/all_to_all | solution.py:258
  160.7 6.0 %all-to-all-start.2 = ((bf16[64,4,1536]{2,1,0:T(4,128)(2,1)}), bf16[64,4,1536]{2,1,0:T(4,128)(2,1)S(1)}, u32[]{:S(2)}, u32[]{:S(2)}) async-start(bf16[64,4,1536]{2,1,0:T(4,128)(2,1)} %copy-done.3), calls=%async_computation.2 | async-start | bytes 1572864 | tf_op jit(solution)/shard_map/all_to_all | solution.py:258
  166.7 0.1 reduce_sum.19
  166.8 21.0 %all-to-all-done.2.slots_ref = bf16[64,4,1536]{2,1,0:T(4,128)(2,1)S(1)} async-done(((bf16[64,4,1536]{2,1,0:T(4,128)(2,1)}), bf16[64,4,1536]{2,1,0:T(4,128)(2,1)S(1)}, u32[]{:S(2)}, u32[]{:S(2)}) %all-to-all-start.2) | async-done | bytes 786464 | tf_op jit(solution)/shard_map/all_to_all | solution.py:258
  187.8 0.7 broadcast_in_dim.11
  188.5 7.6 %all-to-all-start.5 = ((f32[16,1,1536]{2,1,0:T(1,128)}), f32[16,1,1536]{2,1,0:T(1,128)S(1)}, u32[]{:S(2)}, u32[]{:S(2)}) async-start(f32[16,1,1536]{2,1,0:T(1,128)} %broadcast_in_dim.11), calls=%async_computation.5 | async-start | bytes 196608 | tf_op jit(solution)/shard_map/all_to_all | solution.py:258
  196.1 1.1 copy-done.5
  197.1 1.1 copy-done.7
  198.2 4.2 %project.1 = bf16[128,1536]{1,0:T(8,128)(2,1)} custom-call(s32[64]{0:T(128)S(1)} %slice_reduce_fusion.flags_ref, s32[2]{0:T(128)S(1)} %pad_add_fusion.place_ref, s32[64]{0:T(128)S(1)} %copy-done.9, bf16[64,4,1536]{2,1,0:T(4,128)(2,1)S(1)} %all-to-all-done.2.slots_ref, bf16[768,768]{1,0:T(8,128)(2,1)S(1)} %copy-done, bf16[768,768]{1,0:T(8,128)(2,1)S(1)} %copy-done.2, ...), custom_call_target="tpu_custom_call" | custom-call | flops 603979776 | bytes 5505024 | tf_op jit(solution)/shard_map/project/pallas_call | solution.py:341
  202.4 0.7 copy.20
  203.0 0.6 slice_reduce_fusion.1
  (35 shorter events, 0.1 us)
Async XLA Ops:
  7.2 25.5 %copy-start.18 = (f32[1536]{0:T(1024)S(1)}, f32[1536]{0:T(1024)}, u32[]{:S(2)}) copy-start(f32[1536]{0:T(1024)} %param.15) | copy-start | bytes 18436
  7.2 36.0 %copy-start.8 = (bf16[128,1536]{1,0:T(8,128)(2,1)S(1)}, bf16[128,1536]{1,0:T(8,128)(2,1)}, u32[]{:S(2)}) copy-start(bf16[128,1536]{1,0:T(8,128)(2,1)} %cot_ref.1) | copy-start | bytes 1179652
  7.2 64.2 %all-gather.2.cloned.1.call-start = ((), (), s32[]{:S(2)}) async-start(), calls=%async_computation.6 | async-start | bytes 1327104 | tf_op jit(solution)/shard_map/all_gather | solution.py:278
  8.5 36.8 %copy-start.17 = (f32[24,1536]{1,0:T(8,128)}, f32[24,1536]{1,0:T(8,128)S(1)}, u32[]{:S(2)}) copy-start(f32[24,1536]{1,0:T(8,128)S(1)} %multiply_subtract_fusion) | copy-start | bytes 442372
  21.1 20.7 %all-to-all-start = ((s32[64,1,128]{2,1,0:T(1,128)}), s32[64,1,128]{2,1,0:T(1,128)S(1)}, u32[]{:S(2)}, u32[]{:S(2)}) async-start(s32[64,1,128]{2,1,0:T(1,128)} %broadcast_in_dim.8), calls=%async_computation | async-start | bytes 65536 | tf_op jit(solution)/shard_map/all_to_all | solution.py:258
  43.1 6.8 %copy-start.10 = (bf16[192,1536]{1,0:T(8,128)(2,1)S(1)}, bf16[192,1536]{1,0:T(8,128)(2,1)}, u32[]{:S(2)}) copy-start(bf16[192,1536]{1,0:T(8,128)(2,1)} %frames_ref.3) | copy-start | bytes 1769476
  43.2 6.8 %copy-start.12 = (f32[15,1536]{1,0:T(8,128)S(1)}, f32[15,1536]{1,0:T(8,128)}, u32[]{:S(2)}) copy-start(f32[15,1536]{1,0:T(8,128)} %kernel_ref.3) | copy-start | bytes 276484
  43.2 6.8 %copy-start.13 = (s32[1,48]{1,0:T(1,128)S(1)}, s32[1,48]{1,0:T(1,128)}, u32[]{:S(2)}) copy-start(s32[1,48]{1,0:T(1,128)} %param.13) | copy-start | bytes 580
  43.2 6.8 %copy-start.14 = (s32[1,8]{1,0:T(1,128)S(1)}, s32[1,8]{1,0:T(1,128)}, u32[]{:S(2)}) copy-start(s32[1,8]{1,0:T(1,128)} %param.12) | copy-start | bytes 100
  45.3 56.3 %all-to-all-start.1 = ((bf16[64,4,1536]{2,1,0:T(4,128)(2,1)}), bf16[64,4,1536]{2,1,0:T(4,128)(2,1)S(1)}, u32[]{:S(2)}, u32[]{:S(2)}) async-start(bf16[64,4,1536]{2,1,0:T(4,128)(2,1)} %scatter.1), calls=%async_computation.1 | async-start | bytes 1572864 | tf_op jit(solution)/shard_map/all_to_all | solution.py:258
  57.2 0.9 copy-start.3
  58.1 1.0 copy-start.15
  71.4 32.2 %copy-start.9 = (s32[64]{0:T(128)S(1)}, s32[64]{0:T(128)}, u32[]{:S(2)}) copy-start(s32[64]{0:T(128)} %order_ref.3) | copy-start | bytes 772
  71.4 30.3 %collective-permute-start = (bf16[768,768]{1,0:T(8,128)(2,1)}, bf16[768,768]{1,0:T(8,128)(2,1)S(1)}, u32[]{:S(2)}, u32[]{:S(2)}) collective-permute-start(bf16[768,768]{1,0:T(8,128)(2,1)} %all-gather.2.cloned.1.call-done.o0), channel_id=1, source_target_pairs={{0,64},{64,0},{1,65},{65,1},{2,66},{66,2},{3,67},{67,3},{4,68},{68... | collective-permute-start | bytes 3538952 | tf_op jit(solution)/shard_map/ppermute | solution.py:299
  78.8 18.1 %collective-permute-start.1 = (bf16[384,768]{1,0:T(8,128)(2,1)S(1)}, bf16[384,768]{1,0:T(8,128)(2,1)S(1)}, u32[]{:S(2)}, u32[]{:S(2)}) collective-permute-start(bf16[384,768]{1,0:T(8,128)(2,1)S(1)} %get-tuple-element.22), channel_id=1, source_target_pairs={{0,32},{32,128},{128,160},{160,256},{256,288},{288,384},{384,416},... | collective-permute-start | bytes 1769480 | tf_op jit(solution)/shard_map/ppermute | solution.py:297
  82.0 17.5 %collective-permute-start.2 = (bf16[384,768]{1,0:T(8,128)(2,1)S(1)}, bf16[384,768]{1,0:T(8,128)(2,1)S(1)}, u32[]{:S(2)}, u32[]{:S(2)}) collective-permute-start(bf16[384,768]{1,0:T(8,128)(2,1)S(1)} %get-tuple-element.21), channel_id=1, source_target_pairs={{32,0},{128,32},{160,128},{256,160},{288,256},{384,288},{416,384},... | collective-permute-start | bytes 1769480 | tf_op jit(solution)/shard_map/ppermute | solution.py:298
  96.9 4.8 %collective-permute-start.3 = (bf16[384,768]{1,0:T(8,128)(2,1)S(1)}, bf16[384,768]{1,0:T(8,128)(2,1)}, u32[]{:S(2)}, u32[]{:S(2)}) collective-permute-start(bf16[384,768]{1,0:T(8,128)(2,1)S(1)} %collective-permute-done.1.c00), channel_id=1, source_target_pairs={{0,64},{64,0},{1,65},{65,1},{2,66},{66,2},{3,67},{67,3},{4,68},{68... | collective-permute-start | bytes 1769480 | tf_op jit(solution)/shard_map/ppermute | solution.py:300
  99.6 4.0 %collective-permute-start.4 = (bf16[384,768]{1,0:T(8,128)(2,1)S(1)}, bf16[384,768]{1,0:T(8,128)(2,1)}, u32[]{:S(2)}, u32[]{:S(2)}) collective-permute-start(bf16[384,768]{1,0:T(8,128)(2,1)S(1)} %collective-permute-done.2.c01), channel_id=1, source_target_pairs={{0,64},{64,0},{1,65},{65,1},{2,66},{66,2},{3,67},{67,3},{4,68},{68... | collective-permute-start | bytes 1769480 | tf_op jit(solution)/shard_map/ppermute | solution.py:301
  101.7 1.9 copy-start.1
  103.6 1.1 copy-start.11
  104.7 1.3 copy-start.16
  126.9 0.8 copy-start.4
  127.7 0.8 copy-start.6
  140.0 56.0 %copy-start = (bf16[768,768]{1,0:T(8,128)(2,1)S(1)}, bf16[768,768]{1,0:T(8,128)(2,1)}, u32[]{:S(2)}) copy-start(bf16[768,768]{1,0:T(8,128)(2,1)} %all-gather.2.cloned.1.call-done.o0) | copy-start | bytes 3538948
  140.0 56.0 %copy-start.2 = (bf16[768,768]{1,0:T(8,128)(2,1)S(1)}, bf16[768,768]{1,0:T(8,128)(2,1)}, u32[]{:S(2)}) copy-start(bf16[768,768]{1,0:T(8,128)(2,1)} %copy-done.1) | copy-start | bytes 3538948
  160.7 27.1 %all-to-all-start.2 = ((bf16[64,4,1536]{2,1,0:T(4,128)(2,1)}), bf16[64,4,1536]{2,1,0:T(4,128)(2,1)S(1)}, u32[]{:S(2)}, u32[]{:S(2)}) async-start(bf16[64,4,1536]{2,1,0:T(4,128)(2,1)} %copy-done.3), calls=%async_computation.2 | async-start | bytes 1572864 | tf_op jit(solution)/shard_map/all_to_all | solution.py:258
  188.5 13.9 %all-to-all-start.5 = ((f32[16,1,1536]{2,1,0:T(1,128)}), f32[16,1,1536]{2,1,0:T(1,128)S(1)}, u32[]{:S(2)}, u32[]{:S(2)}) async-start(f32[16,1,1536]{2,1,0:T(1,128)} %broadcast_in_dim.11), calls=%async_computation.5 | async-start | bytes 196608 | tf_op jit(solution)/shard_map/all_to_all | solution.py:258
  196.1 1.1 copy-start.5
  197.1 1.1 copy-start.7
Sparse Core Ops, SparseCore 0:
  19.8 51.6 all-gather.1

commit v2 on v1

--- a/solution.py
+++ b/solution.py
@@ -1,9 +1,7 @@
-import functools
 import math
 
 import jax
 import jax.numpy as jnp
-import numpy as np
 from jax import lax
 from jax.experimental import pallas as pl
 from jax.experimental.pallas import tpu as pltpu
@@ -12,9 +10,11 @@
 ROWS = 128
 BLK = 4
 CHUNK = 256
+EMPTY = -2.0
 DP = ("zl", "x", "y")
 NEAR = ("c", "zl", "x")
 FAR = ("zh", "y")
+NX = 4
 F32 = jnp.float32
 BF16 = jnp.bfloat16
 
@@ -29,8 +29,8 @@
     return master - 0.01 * (moment_new / (jnp.sqrt(second_new) + 1e-08) + 0.1 * master)
 
 
-def write_shifts(lengths_ref, shift_ref):
-    taps, height, _ = shift_ref.shape
+def write_shifts(lengths_ref, shift_ref, taps):
+    height = shift_ref.shape[1]
     half = (taps - 1) // 2
     row = lax.broadcasted_iota(jnp.int32, (height, height), 0)
     col = lax.broadcasted_iota(jnp.int32, (height, height), 1)
@@ -44,37 +44,50 @@
     same = (row_seg == col_seg) & (row < bound)
     offset = jnp.where(same, col - row + half, -1)
     for j in range(taps):
-        shift_ref[j] = jnp.where(offset == j, 1.0, 0.0).astype(F32).astype(BF16)
-
-
-def forward_kernel(lengths_ref, dest_ref, frames_ref, kernel_ref, gain_ref, slots_ref, mixed_ref, shift_ref, act_ref):
-    taps, height, _ = shift_ref.shape
-    columns = frames_ref.shape[1]
-    write_shifts(lengths_ref, shift_ref)
+        shift_ref[j * height : (j + 1) * height, :] = jnp.where(offset == j, 1.0, 0.0).astype(F32).astype(BF16)
+
+
+def forward_kernel(
+    lengths_ref, dest_ref, frames_ref, kernel_ref, gain_ref,
+    slots_ref, unit_ref, factor_ref, inv_ref, shift_ref,
+    act_ref,
+):
+    taps = kernel_ref.shape[0]
+    height, columns = frames_ref.shape
+    write_shifts(lengths_ref, shift_ref, taps)
 
     def conv(i, carry):
         at = pl.ds(pl.multiple_of(i * CHUNK, CHUNK), CHUNK)
         piece = frames_ref[:, at]
         total = jnp.zeros((height, CHUNK), F32)
         for j in range(taps):
-            total = total + kernel_ref[pl.ds(j, 1), at] * jnp.dot(shift_ref[j], piece, preferred_element_type=F32)
-        mixed_ref[:, at] = total
+            moved = jnp.dot(shift_ref[j * height : (j + 1) * height, :], piece, preferred_element_type=F32)
+            total = total + kernel_ref[pl.ds(j, 1), at] * moved
+        act_ref[:, at] = total
         return carry
 
     lax.fori_loop(0, columns // CHUNK, conv, 0)
     step = 16
+    gain = gain_ref[...]
 
     def norm(i, carry):
         at = pl.ds(pl.multiple_of(i * step, step), step)
-        mixed = mixed_ref[at, :]
+        mixed = act_ref[at, :]
         center = jnp.mean(mixed, axis=1, keepdims=True)
         off = mixed - center
-        spread = jnp.mean(off * off, axis=1, keepdims=True)
-        scaled = off * lax.rsqrt(spread + 1e-05) * gain_ref[...]
-        act_ref[at, :] = scaled * jax.nn.sigmoid(scaled)
+        inv = lax.rsqrt(jnp.mean(off * off, axis=1, keepdims=True) + 1e-05)
+        unit = off * inv
+        scaled = unit * gain
+        sig = jax.nn.sigmoid(scaled)
+        act = scaled * sig
+        act_ref[at, :] = act
+        unit_ref[at, :] = unit
+        factor_ref[at, :] = sig + act * (1.0 - sig)
+        inv_ref[at, :] = jnp.broadcast_to(inv, (step, inv_ref.shape[1]))
         return carry
 
     lax.fori_loop(0, height // step, norm, 0)
+    slots_ref[:, :, 0:128] = jnp.full((slots_ref.shape[0], BLK, 128), EMPTY, BF16)
     for b in range(height // BLK):
         where = dest_ref[b]
 
@@ -127,23 +140,23 @@
 
 
 def block_place(place_ref, owner, blocks):
-    nx, ny = 4, blocks // 8
+    nx, ny = NX, blocks // (2 * NX)
     other = jnp.where(owner // (ny * nx) != place_ref[0], blocks // 2, 0)
-    return other + owner % ny * nx + owner // ny % nx
+    return other + (owner // ny % nx - place_ref[2] + nx) % nx * ny + owner % ny
 
 
 def backward_kernel(
-    lengths_ref, dest_ref, place_ref, order_ref,
-    frames_ref, kernel_ref, gain_ref, mixed_ref, slots_ref, o0, o1, c00, c01, c10, c11,
+    dest_ref, place_ref, order_ref,
+    frames_ref, kernel_ref, gain_ref, unit_ref, factor_ref, inv_ref, shift_ref, slots_ref,
+    o0, o1, c00, c01, c10, c11,
     frame_ref, term_ref,
-    shift_ref, home_ref, homeb_ref, weight_ref, raw_ref, sorted_ref, grad_ref, gradb_ref, sems,
+    home_ref, homeb_ref, weight_ref, raw_ref, sorted_ref, grad_ref, moved_ref, sum_ref, sems,
 ):
-    taps, height, _ = shift_ref.shape
-    columns = frames_ref.shape[1]
+    taps = kernel_ref.shape[0]
+    height, columns = frames_ref.shape
     blocks = order_ref.shape[0]
     size = columns // blocks
     copies = load_weight(place_ref, (o0, o1), ((c00, c01), (c10, c11)), weight_ref, sems)
-    write_shifts(lengths_ref, shift_ref)
     for b in range(height // BLK):
         where = dest_ref[b]
         rows = slots_ref[jnp.maximum(where, 0)].astype(F32)
@@ -153,20 +166,16 @@
         copy.wait()
 
     def back(i, carry):
-        at = pl.ds(pl.multiple_of(i * CHUNK, CHUNK), CHUNK)
+        at = pl.ds(pl.multiple_of(i * 2 * CHUNK, CHUNK), 2 * CHUNK)
         raw_ref[at, :] = lax.dot_general(
             weight_ref[at, :], homeb_ref[...], (((1,), (1,)), ((), ())), preferred_element_type=F32
         )
         return carry
 
-    lax.fori_loop(0, columns // CHUNK, back, 0)
-
-    def order(b, carry):
+    lax.fori_loop(0, columns // (2 * CHUNK), back, 0)
+    for b in range(blocks):
         at = pl.multiple_of(block_place(place_ref, order_ref[b], blocks) * size, 8)
-        sorted_ref[pl.ds(pl.multiple_of(b * size, 8), size), :] = raw_ref[pl.ds(at, size), :]
-        return carry
-
-    lax.fori_loop(0, blocks, order, 0)
+        sorted_ref[b * size : (b + 1) * size, :] = raw_ref[pl.ds(at, size), :]
 
     def turn(i, carry):
         at = pl.ds(pl.multiple_of(i * CHUNK, CHUNK), CHUNK)
@@ -174,41 +183,44 @@
         return carry
 
     lax.fori_loop(0, columns // CHUNK, turn, 0)
-    step = 8
+    step = 16
     gain = gain_ref[...]
 
     def norm(i, total):
         at = pl.ds(pl.multiple_of(i * step, step), step)
-        mixed = mixed_ref[at, :]
-        center = jnp.mean(mixed, axis=1, keepdims=True)
-        off = mixed - center
-        inv = lax.rsqrt(jnp.mean(off * off, axis=1, keepdims=True) + 1e-05)
-        unit = off * inv
-        scaled = unit * gain
-        sig = jax.nn.sigmoid(scaled)
-        slope = home_ref[at, :] * (sig * (1.0 + scaled * (1.0 - sig)))
-        total = total + slope * unit
+        unit = unit_ref[at, :]
+        slope = home_ref[at, :] * factor_ref[at, :]
+        along = slope * unit
+        total = total + along[0:8] + along[8:16]
         slope = slope * gain
         mean_slope = jnp.mean(slope, axis=1, keepdims=True)
-        mean_unit = jnp.mean(slope * unit, axis=1, keepdims=True)
-        grad_ref[at, :] = inv * (slope - mean_slope - unit * mean_unit)
+        mean_unit = jnp.mean(along * gain, axis=1, keepdims=True)
+        grad_ref[at, :] = (inv_ref[at, 0:1] * (slope - mean_slope - unit * mean_unit)).astype(BF16)
         return total
 
-    total = lax.fori_loop(0, height // step, norm, jnp.zeros((step, columns), F32))
+    total = lax.fori_loop(0, height // step, norm, jnp.zeros((8, columns), F32))
     term_ref[taps] = jnp.sum(total, axis=0, keepdims=True)
-    gradb_ref[...] = grad_ref[...].astype(BF16)
+    part = 64
 
     def conv(i, carry):
         at = pl.ds(pl.multiple_of(i * CHUNK, CHUNK), CHUNK)
-        piece = frames_ref[:, at]
-        grad = grad_ref[:, at]
-        gradb = gradb_ref[:, at]
-        out = jnp.zeros((height, CHUNK), F32)
-        for j in range(taps):
-            moved = jnp.dot(shift_ref[j], piece, preferred_element_type=F32)
-            term_ref[j, :, at] = jnp.sum(grad * moved, axis=0, keepdims=True)
-            out = out + kernel_ref[pl.ds(taps - 1 - j, 1), at] * jnp.dot(shift_ref[j], gradb, preferred_element_type=F32)
-        frame_ref[:, at] = out.astype(BF16)
+        moved_ref[...] = jnp.dot(shift_ref[...], grad_ref[:, at], preferred_element_type=F32)
+        for p in range(height // part):
+            rows = slice(p * part, (p + 1) * part)
+            frames = frames_ref[rows, at].astype(F32)
+            out = jnp.zeros((part, CHUNK), F32)
+            for j in range(taps):
+                tap = taps - 1 - j
+                moved = moved_ref[j * height + p * part : j * height + (p + 1) * part, :]
+                out = out + kernel_ref[pl.ds(tap, 1), at] * moved
+                add = jnp.sum((frames * moved).reshape(part // 8, 8, CHUNK), axis=0)
+                if p == 0:
+                    sum_ref[tap] = add
+                elif p < height // part - 1:
+                    sum_ref[tap] = sum_ref[tap] + add
+                else:
+                    term_ref[tap, :, at] = jnp.sum(sum_ref[tap] + add, axis=0, keepdims=True)
+            frame_ref[rows, at] = out.astype(BF16)
         return carry
 
     lax.fori_loop(0, columns // CHUNK, conv, 0)
@@ -263,74 +275,82 @@
     taps = kernel.shape[0]
     owners = bucket_order.shape[0]
     half = columns // 2
-    core, zl = lax.axis_index("c"), lax.axis_index("zl")
+    core, zl, x = lax.axis_index("c"), lax.axis_index("zl"), lax.axis_index("x")
     dest = destination[0]
     lens = lengths[0]
-    place = jnp.stack([zl, core]).astype(jnp.int32)
+    place = jnp.stack([zl, core, x]).astype(jnp.int32)
     gain = norm_gain[None, :]
-
-    sends = jnp.any(dest[None, :] == jnp.arange(owners, dtype=jnp.int32)[:, None], axis=1).astype(jnp.int32)
-    flags = exchange(jnp.broadcast_to(sends[:, None, None], (owners, 1, 128)), DP)[:, 0, 0]
 
     updated = adam_step(master, moment, second, gradient)
     bucket = lax.dynamic_slice_in_dim(updated, core * half, half, axis=1).astype(BF16)
-    near = lax.all_gather(bucket, "x", axis=0, tiled=True)
-    own = lax.all_gather(near, "y", axis=0, tiled=True)
+    ny = lax.axis_size("y")
+    line = exchange(jnp.broadcast_to(bucket[None], (ny, *bucket.shape)), "y").reshape(-1, half)
+
     slots = jax.ShapeDtypeStruct((owners, BLK, columns), BF16)
-    sent, mixed = call(
+    whole = jax.ShapeDtypeStruct((height, columns), F32)
+    sent, unit, factor, inv, shifts = call(
         forward_kernel,
         [SM, SM, VM, VM, VM],
-        [slots, jax.ShapeDtypeStruct((height, columns), F32)],
-        [pltpu.VMEM((taps, height, height), BF16), pltpu.VMEM((height, columns), F32)],
+        [
+            slots,
+            whole,
+            whole,
+            jax.ShapeDtypeStruct((height, 128), F32),
+            jax.ShapeDtypeStruct((taps * height, height), BF16),
+        ],
+        [pltpu.VMEM((height, columns), F32)],
         40,
         "forward",
         8 * taps * height * height * columns,
         16 * height * columns,
     )(lens, dest, frames, kernel, gain)
-
-    own, sent = lax.optimization_barrier((own, sent))
-    part = own.shape[0] // 2
+    line, sent = lax.optimization_barrier((line, sent))
+    act_slots = exchange(sent, DP)
+
+    nx = lax.axis_size("x")
+    by_x = [line] + [lax.ppermute(line, "x", [((i + k) % nx, i) for i in range(nx)]) for k in range(1, nx)]
     nz = lax.axis_size("zh") * lax.axis_size("zl")
     up = [(i, (i + 1) % nz) for i in range(nz)]
     down = [((i + 1) % nz, i) for i in range(nz)]
     swap = [(0, 1), (1, 0)]
-    c00 = lax.ppermute(own[:part], ("zh", "zl"), up)
-    c01 = lax.ppermute(own[part:], ("zh", "zl"), down)
+    low, high = jnp.concatenate(by_x[: nx // 2]), jnp.concatenate(by_x[nx // 2 :])
+    c00 = lax.ppermute(low, ("zh", "zl"), up)
+    c01 = lax.ppermute(high, ("zh", "zl"), down)
+    own = jnp.concatenate(by_x)
     own1 = lax.ppermute(own, "c", swap)
     c10 = lax.ppermute(c00, "c", swap)
     c11 = lax.ppermute(c01, "c", swap)
     pieces = (own, own1, c00, c01, c10, c11)
 
+    flags = (act_slots[:, 0, 0] > EMPTY / 2).astype(jnp.int32)
     (cot_sent,) = call(
         scatter_kernel, [SM, VM], [slots], [pltpu.SMEM((owners,), jnp.int32)], 40, "scatter", 0, 6 * cotangent.size
     )(flags, cotangent)
     cot_slots = exchange(cot_sent, DP)
-    sent, cot_slots = lax.optimization_barrier((sent, cot_slots))
-    act_slots = exchange(sent, DP)
 
     frame_grad, term = call(
         backward_kernel,
-        [SM] * 4 + [VM] * 5 + [HB] * 6,
+        [SM] * 3 + [VM] * 8 + [HB] * 6,
         [
             jax.ShapeDtypeStruct((height, columns), BF16),
             jax.ShapeDtypeStruct((taps + 1, 1, columns), F32),
         ],
         [
-            pltpu.VMEM((taps, height, height), BF16),
             pltpu.VMEM((height, columns), F32),
             pltpu.VMEM((height, columns), BF16),
             pltpu.VMEM((columns, columns), BF16),
             pltpu.VMEM((columns, height), F32),
             pltpu.VMEM((columns, height), F32),
-            pltpu.VMEM((height, columns), F32),
             pltpu.VMEM((height, columns), BF16),
+            pltpu.VMEM((taps * height, CHUNK), F32),
+            pltpu.VMEM((taps, 8, CHUNK), F32),
             pltpu.SemaphoreType.DMA((6,)),
         ],
         48,
         "backward",
         8 * taps * height * height * columns + 2 * height * columns * columns,
         16 * height * columns + 2 * columns * columns,
-    )(lens, dest, place, bucket_order, frames, kernel, gain, mixed, cot_slots, *pieces)
+    )(dest, place, bucket_order, frames, kernel, gain, unit, factor, inv, shifts, cot_slots, *pieces)
 
     mine = jnp.sum(exchange(term, NEAR), axis=0, keepdims=True)
     far = lax.axis_size(FAR)
@@ -358,7 +378,7 @@
 
 
 def solution(mesh):
-    fine = Mesh(mesh.devices.reshape(4, 2, 2, 4, 8), ("zh", "c", "zl", "x", "y"))
+    fine = Mesh(mesh.devices.reshape(4, 2, 2, NX, 8), ("zh", "c", "zl", "x", "y"))
     rep, dp = ("zh", "c"), ("zl", "x", "y")
     every, rows = P(rep + dp, None), P(dp, None)
     return jax.shard_map(

time: 211 us -> 174 us (0.82)
  waiting for transfers between devices: 55.9 us -> 25.4 us
  starting transfers between devices: 46.9 us -> 68.8 us
  between operations: 14.4 us -> 1.04 us
  blocking collectives: 43 us -> 34.2 us
  Pallas kernels: 34.4 us -> 28.5 us
  local copies, waits for them, and re-layouts: 13.5 us -> 11.2 us
    all_to_all x4, waiting for transfers between devices: 30.2 us -> 2.36 us  [exchange(): return lax.all_to_all(x, axes, split_axis=0, concat_axis=0, tiled=True)]
    ppermute x2 -> x5, starting transfers between devices: 6.49 us -> 20.9 us  [the longest x3 9.24 us: body(): lax.ppermute(line, 'x', [((i + k) % nx, i) for i in range(nx)])]
    all_gather x1 -> x0, waiting for transfers between devices: 12.3 us -> none  [body(): own = lax.all_gather(near, 'y', axis=0, tiled=True)]
    all_gather x1 -> x0, blocking collectives: 11.1 us -> none  [body(): near = lax.all_gather(bucket, 'x', axis=0, tiled=True)]
    ppermute x2 -> x5, waiting for transfers between devices: 11.5 us -> 20.8 us  [the longest x1 11.8 us: body(): c00 = lax.ppermute(low, ('zh', 'zl'), up)]
    all_to_all x4, starting transfers between devices: 29.6 us -> 38.5 us  [exchange(): return lax.all_to_all(x, axes, split_axis=0, concat_axis=0, tiled=True)]
    pallas_call x2, Pallas kernels: 28.1 us -> 22.1 us  [the longest x1 13.9 us: body(): call(backward_kernel, [SM] * 3 + [VM] * 8 + [HB] * 6, [jax.ShapeDtypeStru...]
    slice x2 -> x0, local copies, waits for them, and re-layouts: 2.59 us -> none  [the longest x1 1.32 us: body(): c01 = lax.ppermute(own[part:], ('zh', 'zl'), down)]
  transfers between devices with their start and end apart: 10 -> 12, of which waited for: 5 -> 6; matrix products, arithmetic and copies ran while one was open for 2% -> 1% of each run, Pallas kernels for 6% -> 8%
where the time goes in v2:
time: 174 us; the launch traced here: 173 us
  starting transfers between devices  68.8 us (40%)
  blocking collectives  34.2 us (20%)
  Pallas kernels  28.5 us (16%)
  waiting for transfers between devices  25.4 us (15%)
  local copies, waits for them, and re-layouts  11.2 us (6%)
  other arithmetic  3.94 us (2%)
    all_to_all x4, starting transfers between devices, exchange(): return lax.all_to_all(x, axes, split_axis=0, concat_axis=0, tiled=True)  38.5 us
    all_to_all x2, blocking collectives, exchange(): return lax.all_to_all(x, axes, split_axis=0, concat_axis=0, tiled=True)  34.2 us
    pallas_call x1, Pallas kernels, body(): call(backward_kernel, [SM] * 3 + [VM] * 8 + [HB] * 6, [jax.ShapeDtypeStru...  13.9 us
    ppermute x1, waiting for transfers between devices, body(): c00 = lax.ppermute(low, ('zh', 'zl'), up)  11.8 us
    ppermute x3, starting transfers between devices, body(): lax.ppermute(line, 'x', [((i + k) % nx, i) for i in range(nx)])  9.24 us
    ppermute x3, waiting for transfers between devices, body(): lax.ppermute(line, 'x', [((i + k) % nx, i) for i in range(nx)])  9.04 us
    unnamed x50, local copies, waits for them, and re-layouts  9 us
    ppermute x1, starting transfers between devices, body(): c01 = lax.ppermute(high, ('zh', 'zl'), down)  8.41 us
  transfers between devices with their start and end apart: 12, of which 6 were waited for; matrix products, arithmetic and copies ran while one was open for 1% of the time, Pallas kernels for 8%

profile of v2, /device:TPU:1, one launch (start us, length us, event | category | flops | bytes accessed | tf_op | source)
XLA Modules:
  0.0 173.0 jit_solution(13904097688020106885)
XLA Ops:
  0.7 0.0 copy-start.6
  0.7 1.3 multiply_subtract_fusion
  2.0 0.0 copy-start.21
  2.0 0.7 broadcast_in_dim.8
  2.8 7.7 %all-to-all-start = ((bf16[8,24,768]{2,1,0:T(8,128)(2,1)}), bf16[8,24,768]{2,1,0:T(8,128)(2,1)S(1)}, u32[]{:S(2)}, u32[]{:S(2)}) async-start(bf16[8,24,768]{2,1,0:T(8,128)(2,1)} %broadcast_in_dim.8), calls=%async_computation | async-start | bytes 589824 | tf_op jit(solution)/shard_map/all_to_all | solution.py:270
  10.5 8.1 %forward.1 = (bf16[64,4,1536]{2,1,0:T(4,128)(2,1)}, f32[192,1536]{1,0:T(8,128)S(1)}, f32[192,1536]{1,0:T(8,128)S(1)}, f32[192,128]{1,0:T(8,128)S(1)}, bf16[2880,192]{1,0:T(8,128)(2,1)S(1)}) custom-call(s32[8]{0:T(128)S(1)} %bitcast.9, s32[48]{0:T(128)S(1)} %bitcast.10, bf16[192,1536]{1,0:T(8,128)(2,1)S(1)} %copy-done.6, f32[15,1536]{1,0:T(8,128)S(1)} %copy-done.8, ...), custom_call_target="tpu_custom_call" | custom-call | flops 6794772480 | bytes 4718592 | tf_op jit(solution)/shard_map/forward/pallas_call | solution.py:291
  18.6 1.1 copy-done.11
  19.8 1.0 copy-done.12
  20.8 1.0 copy-done.14
  21.8 12.0 %all-to-all-start.1 = ((bf16[64,4,1536]{2,1,0:T(4,128)(2,1)}), bf16[64,4,1536]{2,1,0:T(4,128)(2,1)S(1)}, u32[]{:S(2)}, u32[]{:S(2)}) async-start(bf16[64,4,1536]{2,1,0:T(4,128)(2,1)} %get-tuple-element.15), calls=%async_computation.1 | async-start | bytes 1572864 | tf_op jit(solution)/shard_map/all_to_all | solution.py:270
  33.8 0.0 copy-start.4
  33.8 4.3 %collective-permute-start = (bf16[192,768]{1,0:T(8,128)(2,1)S(1)}, bf16[192,768]{1,0:T(8,128)(2,1)S(1)}, u32[]{:S(2)}, u32[]{:S(2)}) collective-permute-start(bf16[192,768]{1,0:T(8,128)(2,1)S(1)} %bitcast.12), channel_id=1, source_target_pairs={{8,0},{16,8},{24,16},{0,24},{9,1},{17,9},{25,17},{1,25},{10,2},{18... | collective-permute-start | bytes 884744 | tf_op jit(solution)/shard_map/ppermute | solution.py:311
  38.1 2.4 %collective-permute-start.1 = (bf16[192,768]{1,0:T(8,128)(2,1)S(1)}, bf16[192,768]{1,0:T(8,128)(2,1)S(1)}, u32[]{:S(2)}, u32[]{:S(2)}) collective-permute-start(bf16[192,768]{1,0:T(8,128)(2,1)S(1)} %bitcast.13), channel_id=1, source_target_pairs={{16,0},{24,8},{0,16},{8,24},{17,1},{25,9},{1,17},{9,25},{18,2},{26... | collective-permute-start | bytes 884744 | tf_op jit(solution)/shard_map/ppermute | solution.py:311
  40.6 2.5 %collective-permute-start.2 = (bf16[192,768]{1,0:T(8,128)(2,1)S(1)}, bf16[192,768]{1,0:T(8,128)(2,1)S(1)}, u32[]{:S(2)}, u32[]{:S(2)}) collective-permute-start(bf16[192,768]{1,0:T(8,128)(2,1)S(1)} %bitcast.14), channel_id=1, source_target_pairs={{24,0},{0,8},{8,16},{16,24},{25,1},{1,9},{9,17},{17,25},{26,2},{2,... | collective-permute-start | bytes 884744 | tf_op jit(solution)/shard_map/ppermute | solution.py:311
  43.1 5.9 %collective-permute-done = bf16[192,768]{1,0:T(8,128)(2,1)S(1)} collective-permute-done((bf16[192,768]{1,0:T(8,128)(2,1)S(1)}, bf16[192,768]{1,0:T(8,128)(2,1)S(1)}, u32[]{:S(2)}, u32[]{:S(2)}) %collective-permute-start) | collective-permute-done | bytes 294944 | tf_op jit(solution)/shard_map/ppermute | solution.py:311
  49.1 3.1 %collective-permute-done.1 = bf16[192,768]{1,0:T(8,128)(2,1)S(1)} collective-permute-done((bf16[192,768]{1,0:T(8,128)(2,1)S(1)}, bf16[192,768]{1,0:T(8,128)(2,1)S(1)}, u32[]{:S(2)}, u32[]{:S(2)}) %collective-permute-start.1) | collective-permute-done | bytes 294944 | tf_op jit(solution)/shard_map/ppermute | solution.py:311
  52.2 0.7 copy-done.16
  52.9 1.9 %all-to-all-done.1.slots_ref = bf16[64,4,1536]{2,1,0:T(4,128)(2,1)S(1)} async-done(((bf16[64,4,1536]{2,1,0:T(4,128)(2,1)}), bf16[64,4,1536]{2,1,0:T(4,128)(2,1)S(1)}, u32[]{:S(2)}, u32[]{:S(2)}) %all-to-all-start.1) | async-done | bytes 786464 | tf_op jit(solution)/shard_map/all_to_all | solution.py:270
  54.9 1.2 fusion.flags_ref
  56.1 2.1 %scatter.1 = bf16[64,4,1536]{2,1,0:T(4,128)(2,1)} custom-call(s32[64]{0:T(128)S(1)} %fusion.flags_ref, bf16[128,1536]{1,0:T(8,128)(2,1)S(1)} %copy-done.4), custom_call_target="tpu_custom_call" | custom-call | bytes 1179648 | tf_op jit(solution)/shard_map/scatter/pallas_call | solution.py:326
  58.2 12.6 %all-to-all-start.2 = ((bf16[64,4,1536]{2,1,0:T(4,128)(2,1)}), bf16[64,4,1536]{2,1,0:T(4,128)(2,1)}, u32[]{:S(2)}, u32[]{:S(2)}) async-start(bf16[64,4,1536]{2,1,0:T(4,128)(2,1)} %scatter.1), calls=%async_computation.2 | async-start | bytes 1572864 | tf_op jit(solution)/shard_map/all_to_all | solution.py:270
  70.9 0.7 copy-done.19
  71.6 0.0 copy-start.5
  71.7 5.0 %collective-permute-start.3 = (bf16[768,768]{1,0:T(8,128)(2,1)S(1)}, bf16[768,768]{1,0:T(8,128)(2,1)S(1)}, u32[]{:S(2)}, u32[]{:S(2)}) collective-permute-start(bf16[768,768]{1,0:T(8,128)(2,1)S(1)} %constant_dynamic-update-slice_fusion.o0), channel_id=1, source_target_pairs={{0,64},{64,0},{1,65},{65,1},{2,66},{66,2},{3,67},{67,3},{4,68},{68... | collective-permute-start | bytes 3538952 | tf_op jit(solution)/shard_map/ppermute | solution.py:320
  76.6 1.1 pad_maximum_fusion
  77.7 3.2 %collective-permute-start.4 = (bf16[384,768]{1,0:T(8,128)(2,1)S(1)}, bf16[384,768]{1,0:T(8,128)(2,1)}, u32[]{:S(2)}, u32[]{:S(2)}) collective-permute-start(bf16[384,768]{1,0:T(8,128)(2,1)S(1)} %pad_maximum_fusion), channel_id=1, source_target_pairs={{0,32},{32,128},{128,160},{160,256},{256,288},{288,384},{384,416},... | collective-permute-start | bytes 1769480 | tf_op jit(solution)/shard_map/ppermute | solution.py:317
  81.1 8.4 %collective-permute-start.5 = (bf16[384,768]{1,0:T(8,128)(2,1)S(1)}, bf16[384,768]{1,0:T(8,128)(2,1)}, u32[]{:S(2)}, u32[]{:S(2)}) collective-permute-start(bf16[384,768]{1,0:T(8,128)(2,1)S(1)} %pad_maximum_fusion.1), channel_id=1, source_target_pairs={{32,0},{128,32},{160,128},{256,160},{288,256},{384,288},{416,384},... | collective-permute-start | bytes 1769480 | tf_op jit(solution)/shard_map/ppermute | solution.py:318
  89.5 11.8 %collective-permute-done.4.c00 = bf16[384,768]{1,0:T(8,128)(2,1)} collective-permute-done((bf16[384,768]{1,0:T(8,128)(2,1)S(1)}, bf16[384,768]{1,0:T(8,128)(2,1)}, u32[]{:S(2)}, u32[]{:S(2)}) %collective-permute-start.4) | collective-permute-done | bytes 589856 | tf_op jit(solution)/shard_map/ppermute | solution.py:317
  101.3 2.5 %collective-permute-start.6 = (bf16[384,768]{1,0:T(8,128)(2,1)}, bf16[384,768]{1,0:T(8,128)(2,1)}, u32[]{:S(2)}, u32[]{:S(2)}) collective-permute-start(bf16[384,768]{1,0:T(8,128)(2,1)} %collective-permute-done.4.c00), channel_id=1, source_target_pairs={{0,64},{64,0},{1,65},{65,1},{2,66},{66,2},{3,67},{67,3},{4,68},{68... | collective-permute-start | bytes 1769480 | tf_op jit(solution)/shard_map/ppermute | solution.py:321
  103.8 1.9 %collective-permute-start.7 = (bf16[384,768]{1,0:T(8,128)(2,1)}, bf16[384,768]{1,0:T(8,128)(2,1)}, u32[]{:S(2)}, u32[]{:S(2)}) collective-permute-start(bf16[384,768]{1,0:T(8,128)(2,1)} %collective-permute-done.5.c01), channel_id=1, source_target_pairs={{0,64},{64,0},{1,65},{65,1},{2,66},{66,2},{3,67},{67,3},{4,68},{68... | collective-permute-start | bytes 1769480 | tf_op jit(solution)/shard_map/ppermute | solution.py:322
  105.7 0.1 pad_add_fusion.place_ref
  105.8 2.2 %collective-permute-done.7.c11 = bf16[384,768]{1,0:T(8,128)(2,1)} collective-permute-done((bf16[384,768]{1,0:T(8,128)(2,1)}, bf16[384,768]{1,0:T(8,128)(2,1)}, u32[]{:S(2)}, u32[]{:S(2)}) %collective-permute-start.7) | collective-permute-done | bytes 589856 | tf_op jit(solution)/shard_map/ppermute | solution.py:322
  108.0 0.0 copy-start.7
  108.0 1.1 copy-done.7
  109.1 1.3 copy-done.13
  110.4 13.9 %backward.1 = (bf16[192,1536]{1,0:T(8,128)(2,1)}, f32[16,1,1536]{2,1,0:T(1,128)S(1)}) custom-call(s32[48]{0:T(128)S(1)} %bitcast.11, s32[3]{0:T(128)S(1)} %pad_add_fusion.place_ref, s32[64]{0:T(128)S(1)} %copy-done.5, bf16[192,1536]{1,0:T(8,128)(2,1)S(1)} %copy-done.7, f32[15,1536]{1,0:T(8,128)S(1)} %copy-done.8, f32[1,1536]{1,0:T(1,128)S(1)} %broadcast_in_dim.9.gain_ref, ...), custom_call_target="tpu_custom_call" | custom-call | flops 7700742144 | bytes 9437184 | tf_op jit(solution)/shard_map/backward/pallas_call | solution.py:331
  124.3 10.4 %all_to_all.30 = f32[16,1,1536]{2,1,0:T(1,128)S(1)} all-to-all(f32[16,1,1536]{2,1,0:T(1,128)S(1)} %get-tuple-element.22), channel_id=1, replica_groups=mesh['zh'=4,'c'=2,'zl'=2,'x'=4,'y'=8] {'c','zl','x'}, dimensions={0} | all-to-all | bytes 196608 | tf_op jit(solution)/shard_map/all_to_all | solution.py:270
  134.7 0.1 reduce_sum.18
  134.8 0.1 broadcast_in_dim.10
  134.9 23.7 %all_to_all.31 = f32[32,1,1536]{2,1,0:T(1,128)S(1)} all-to-all(f32[32,1,1536]{2,1,0:T(1,128)S(1)} %broadcast_in_dim.10), channel_id=1, replica_groups=mesh['zh'=4,'c'=2,'zl'=2,'x'=4,'y'=8] {'zh','y'}, dimensions={0} | all-to-all | bytes 393216 | tf_op jit(solution)/shard_map/all_to_all | solution.py:270
  158.6 0.1 reduce_sum.19
  158.8 0.7 broadcast_in_dim.11
  159.5 6.3 %all-to-all-start.5 = ((f32[16,1,1536]{2,1,0:T(1,128)}), f32[16,1,1536]{2,1,0:T(1,128)S(1)}, u32[]{:S(2)}, u32[]{:S(2)}) async-start(f32[16,1,1536]{2,1,0:T(1,128)} %broadcast_in_dim.11), calls=%async_computation.5 | async-start | bytes 196608 | tf_op jit(solution)/shard_map/all_to_all | solution.py:270
  165.8 1.3 copy-done.3
  167.0 4.3 %project.1 = bf16[128,1536]{1,0:T(8,128)(2,1)} custom-call(s32[64]{0:T(128)S(1)} %fusion.flags_ref, s32[3]{0:T(128)S(1)} %pad_add_fusion.place_ref, s32[64]{0:T(128)S(1)} %copy-done.5, bf16[64,4,1536]{2,1,0:T(4,128)(2,1)S(1)} %all-to-all-done.1.slots_ref, bf16[768,768]{1,0:T(8,128)(2,1)S(1)} %copy-done.1, bf16[768,768]{1,0:T(8,128)(2,1)S(1)} %copy-done.3, ...), custom_call_target="tpu_custom_call" | custom-call | flops 603979776 | bytes 5505024 | tf_op jit(solution)/shard_map/project/pallas_call | solution.py:361
  171.3 0.5 all-to-all-done.5
  171.8 0.7 copy.20
  172.4 0.6 slice_reduce_fusion
  (48 shorter events, 0.2 us)
Async XLA Ops:
  0.6 9.8 %copy-start.22 = (f32[1536]{0:T(1024)S(1)}, f32[1536]{0:T(1024)}, u32[]{:S(2)}) copy-start(f32[1536]{0:T(1024)} %param.15) | copy-start | bytes 18436
  0.6 9.8 %copy-start.9 = (s32[1,8]{1,0:T(1,128)S(1)}, s32[1,8]{1,0:T(1,128)}, u32[]{:S(2)}) copy-start(s32[1,8]{1,0:T(1,128)} %param.12) | copy-start | bytes 100
  0.7 9.8 %copy-start.10 = (s32[1,48]{1,0:T(1,128)S(1)}, s32[1,48]{1,0:T(1,128)}, u32[]{:S(2)}) copy-start(s32[1,48]{1,0:T(1,128)} %param.13) | copy-start | bytes 580
  0.7 9.8 %copy-start.6 = (bf16[192,1536]{1,0:T(8,128)(2,1)S(1)}, bf16[192,1536]{1,0:T(8,128)(2,1)}, u32[]{:S(2)}) copy-start(bf16[192,1536]{1,0:T(8,128)(2,1)} %frames_ref.3) | copy-start | bytes 1769476
  0.7 9.8 %copy-start.8 = (f32[15,1536]{1,0:T(8,128)S(1)}, f32[15,1536]{1,0:T(8,128)}, u32[]{:S(2)}) copy-start(f32[15,1536]{1,0:T(8,128)} %kernel_ref.3) | copy-start | bytes 276484
  2.0 16.6 %copy-start.21 = (f32[24,1536]{1,0:T(8,128)}, f32[24,1536]{1,0:T(8,128)S(1)}, u32[]{:S(2)}) copy-start(f32[24,1536]{1,0:T(8,128)S(1)} %multiply_subtract_fusion) | copy-start | bytes 442372
  2.8 19.0 %all-to-all-start = ((bf16[8,24,768]{2,1,0:T(8,128)(2,1)}), bf16[8,24,768]{2,1,0:T(8,128)(2,1)S(1)}, u32[]{:S(2)}, u32[]{:S(2)}) async-start(bf16[8,24,768]{2,1,0:T(8,128)(2,1)} %broadcast_in_dim.8), calls=%async_computation | async-start | bytes 589824 | tf_op jit(solution)/shard_map/all_to_all | solution.py:270
  18.6 1.1 copy-start.11
  19.8 1.0 copy-start.12
  20.8 1.0 copy-start.14
  21.8 27.3 %copy-start.15 = (bf16[8,24,768]{2,1,0:T(8,128)(2,1)}, bf16[8,24,768]{2,1,0:T(8,128)(2,1)S(1)}, u32[]{:S(2)}) copy-start(bf16[8,24,768]{2,1,0:T(8,128)(2,1)S(1)} %all-to-all-done) | copy-start | bytes 884740
  21.8 33.0 %all-to-all-start.1 = ((bf16[64,4,1536]{2,1,0:T(4,128)(2,1)}), bf16[64,4,1536]{2,1,0:T(4,128)(2,1)S(1)}, u32[]{:S(2)}, u32[]{:S(2)}) async-start(bf16[64,4,1536]{2,1,0:T(4,128)(2,1)} %get-tuple-element.15), calls=%async_computation.1 | async-start | bytes 1572864 | tf_op jit(solution)/shard_map/all_to_all | solution.py:270
  33.8 22.3 %copy-start.4 = (bf16[128,1536]{1,0:T(8,128)(2,1)S(1)}, bf16[128,1536]{1,0:T(8,128)(2,1)}, u32[]{:S(2)}) copy-start(bf16[128,1536]{1,0:T(8,128)(2,1)} %cot_ref.1) | copy-start | bytes 1179652
  33.8 15.2 %collective-permute-start = (bf16[192,768]{1,0:T(8,128)(2,1)S(1)}, bf16[192,768]{1,0:T(8,128)(2,1)S(1)}, u32[]{:S(2)}, u32[]{:S(2)}) collective-permute-start(bf16[192,768]{1,0:T(8,128)(2,1)S(1)} %bitcast.12), channel_id=1, source_target_pairs={{8,0},{16,8},{24,16},{0,24},{9,1},{17,9},{25,17},{1,25},{10,2},{18... | collective-permute-start | bytes 884744 | tf_op jit(solution)/shard_map/ppermute | solution.py:311
  38.1 14.0 %collective-permute-start.1 = (bf16[192,768]{1,0:T(8,128)(2,1)S(1)}, bf16[192,768]{1,0:T(8,128)(2,1)S(1)}, u32[]{:S(2)}, u32[]{:S(2)}) collective-permute-start(bf16[192,768]{1,0:T(8,128)(2,1)S(1)} %bitcast.13), channel_id=1, source_target_pairs={{16,0},{24,8},{0,16},{8,24},{17,1},{25,9},{1,17},{9,25},{18,2},{26... | collective-permute-start | bytes 884744 | tf_op jit(solution)/shard_map/ppermute | solution.py:311
  40.6 30.3 %collective-permute-start.2 = (bf16[192,768]{1,0:T(8,128)(2,1)S(1)}, bf16[192,768]{1,0:T(8,128)(2,1)S(1)}, u32[]{:S(2)}, u32[]{:S(2)}) collective-permute-start(bf16[192,768]{1,0:T(8,128)(2,1)S(1)} %bitcast.14), channel_id=1, source_target_pairs={{24,0},{0,8},{8,16},{16,24},{25,1},{1,9},{9,17},{17,25},{26,2},{2,... | collective-permute-start | bytes 884744 | tf_op jit(solution)/shard_map/ppermute | solution.py:311
  49.0 3.1 %copy-start.18 = (bf16[192,768]{1,0:T(8,128)(2,1)}, bf16[192,768]{1,0:T(8,128)(2,1)S(1)}, u32[]{:S(2)}) copy-start(bf16[192,768]{1,0:T(8,128)(2,1)S(1)} %collective-permute-done) | copy-start | bytes 884740
  52.2 0.7 copy-start.16
  58.2 49.8 %all-to-all-start.2 = ((bf16[64,4,1536]{2,1,0:T(4,128)(2,1)}), bf16[64,4,1536]{2,1,0:T(4,128)(2,1)}, u32[]{:S(2)}, u32[]{:S(2)}) async-start(bf16[64,4,1536]{2,1,0:T(4,128)(2,1)} %scatter.1), calls=%async_computation.2 | async-start | bytes 1572864 | tf_op jit(solution)/shard_map/all_to_all | solution.py:270
  70.9 10.1 %copy-start.17 = (bf16[192,768]{1,0:T(8,128)(2,1)S(1)}, bf16[192,768]{1,0:T(8,128)(2,1)}, u32[]{:S(2)}) copy-start(bf16[192,768]{1,0:T(8,128)(2,1)} %copy-done.16) | copy-start | bytes 884740
  70.9 0.7 copy-start.19
  71.6 9.4 %copy-start = (bf16[768,768]{1,0:T(8,128)(2,1)}, bf16[768,768]{1,0:T(8,128)(2,1)S(1)}, u32[]{:S(2)}) copy-start(bf16[768,768]{1,0:T(8,128)(2,1)S(1)} %constant_dynamic-update-slice_fusion.o0) | copy-start | bytes 3538948
  71.6 9.4 %copy-start.20 = (bf16[192,768]{1,0:T(8,128)(2,1)S(1)}, bf16[192,768]{1,0:T(8,128)(2,1)}, u32[]{:S(2)}) copy-start(bf16[192,768]{1,0:T(8,128)(2,1)} %copy-done.19) | copy-start | bytes 884740
  71.6 36.4 %copy-start.5 = (s32[64]{0:T(128)S(1)}, s32[64]{0:T(128)}, u32[]{:S(2)}) copy-start(s32[64]{0:T(128)} %order_ref.3) | copy-start | bytes 772
  71.7 34.1 %collective-permute-start.3 = (bf16[768,768]{1,0:T(8,128)(2,1)S(1)}, bf16[768,768]{1,0:T(8,128)(2,1)S(1)}, u32[]{:S(2)}, u32[]{:S(2)}) collective-permute-start(bf16[768,768]{1,0:T(8,128)(2,1)S(1)} %constant_dynamic-update-slice_fusion.o0), channel_id=1, source_target_pairs={{0,64},{64,0},{1,65},{65,1},{2,66},{66,2},{3,67},{67,3},{4,68},{68... | collective-permute-start | bytes 3538952 | tf_op jit(solution)/shard_map/ppermute | solution.py:320
  77.7 23.5 %collective-permute-start.4 = (bf16[384,768]{1,0:T(8,128)(2,1)S(1)}, bf16[384,768]{1,0:T(8,128)(2,1)}, u32[]{:S(2)}, u32[]{:S(2)}) collective-permute-start(bf16[384,768]{1,0:T(8,128)(2,1)S(1)} %pad_maximum_fusion), channel_id=1, source_target_pairs={{0,32},{32,128},{128,160},{160,256},{256,288},{288,384},{384,416},... | collective-permute-start | bytes 1769480 | tf_op jit(solution)/shard_map/ppermute | solution.py:317
  81.1 22.7 %collective-permute-start.5 = (bf16[384,768]{1,0:T(8,128)(2,1)S(1)}, bf16[384,768]{1,0:T(8,128)(2,1)}, u32[]{:S(2)}, u32[]{:S(2)}) collective-permute-start(bf16[384,768]{1,0:T(8,128)(2,1)S(1)} %pad_maximum_fusion.1), channel_id=1, source_target_pairs={{32,0},{128,32},{160,128},{256,160},{288,256},{384,288},{416,384},... | collective-permute-start | bytes 1769480 | tf_op jit(solution)/shard_map/ppermute | solution.py:318
  101.3 4.5 %collective-permute-start.6 = (bf16[384,768]{1,0:T(8,128)(2,1)}, bf16[384,768]{1,0:T(8,128)(2,1)}, u32[]{:S(2)}, u32[]{:S(2)}) collective-permute-start(bf16[384,768]{1,0:T(8,128)(2,1)} %collective-permute-done.4.c00), channel_id=1, source_target_pairs={{0,64},{64,0},{1,65},{65,1},{2,66},{66,2},{3,67},{67,3},{4,68},{68... | collective-permute-start | bytes 1769480 | tf_op jit(solution)/shard_map/ppermute | solution.py:321
  103.8 4.2 %collective-permute-start.7 = (bf16[384,768]{1,0:T(8,128)(2,1)}, bf16[384,768]{1,0:T(8,128)(2,1)}, u32[]{:S(2)}, u32[]{:S(2)}) collective-permute-start(bf16[384,768]{1,0:T(8,128)(2,1)} %collective-permute-done.5.c01), channel_id=1, source_target_pairs={{0,64},{64,0},{1,65},{65,1},{2,66},{66,2},{3,67},{67,3},{4,68},{68... | collective-permute-start | bytes 1769480 | tf_op jit(solution)/shard_map/ppermute | solution.py:322
  105.8 2.2 %copy-start.2 = (bf16[768,768]{1,0:T(8,128)(2,1)}, bf16[768,768]{1,0:T(8,128)(2,1)S(1)}, u32[]{:S(2)}) copy-start(bf16[768,768]{1,0:T(8,128)(2,1)S(1)} %collective-permute-done.3.o1) | copy-start | bytes 3538948
  108.0 1.1 copy-start.7
  109.1 1.3 copy-start.13
  124.3 41.5 %copy-start.1 = (bf16[768,768]{1,0:T(8,128)(2,1)S(1)}, bf16[768,768]{1,0:T(8,128)(2,1)}, u32[]{:S(2)}) copy-start(bf16[768,768]{1,0:T(8,128)(2,1)} %copy-done) | copy-start | bytes 3538948
  159.5 12.3 %all-to-all-start.5 = ((f32[16,1,1536]{2,1,0:T(1,128)}), f32[16,1,1536]{2,1,0:T(1,128)S(1)}, u32[]{:S(2)}, u32[]{:S(2)}) async-start(f32[16,1,1536]{2,1,0:T(1,128)} %broadcast_in_dim.11), calls=%async_computation.5 | async-start | bytes 196608 | tf_op jit(solution)/shard_map/all_to_all | solution.py:270
  165.8 1.3 copy-start.3

commit v3 on v2

--- a/solution.py
+++ b/solution.py
@@ -10,7 +10,6 @@
 ROWS = 128
 BLK = 4
 CHUNK = 256
-EMPTY = -2.0
 DP = ("zl", "x", "y")
 NEAR = ("c", "zl", "x")
 FAR = ("zh", "y")
@@ -49,12 +48,15 @@
 
 def forward_kernel(
     lengths_ref, dest_ref, frames_ref, kernel_ref, gain_ref,
-    slots_ref, unit_ref, factor_ref, inv_ref, shift_ref,
-    act_ref,
+    slots_ref, inv_ref, unit_hbm, factor_hbm, shift_hbm,
+    unit_ref, factor_ref, shift_ref, act_ref, sems,
 ):
     taps = kernel_ref.shape[0]
     height, columns = frames_ref.shape
     write_shifts(lengths_ref, shift_ref, taps)
+    saved = [(shift_ref, shift_hbm), (unit_ref, unit_hbm), (factor_ref, factor_hbm)]
+    copies = [pltpu.make_async_copy(a, b, sems.at[i]) for i, (a, b) in enumerate(saved)]
+    copies[0].start()
 
     def conv(i, carry):
         at = pl.ds(pl.multiple_of(i * CHUNK, CHUNK), CHUNK)
@@ -87,13 +89,17 @@
         return carry
 
     lax.fori_loop(0, height // step, norm, 0)
-    slots_ref[:, :, 0:128] = jnp.full((slots_ref.shape[0], BLK, 128), EMPTY, BF16)
+    copies[1].start()
+    copies[2].start()
     for b in range(height // BLK):
         where = dest_ref[b]
 
         @pl.when(where >= 0)
         def _():
-            slots_ref[where] = act_ref[b * BLK : (b + 1) * BLK, :].astype(BF16)
+            slots_ref[where, 0:BLK, :] = act_ref[b * BLK : (b + 1) * BLK, :].astype(BF16)
+
+    for copy in copies:
+        copy.wait()
 
 
 def find_senders(flags_ref, table_ref):
@@ -112,13 +118,14 @@
     lax.fori_loop(0, flags_ref.shape[0], look, jnp.int32(0))
 
 
-def scatter_kernel(flags_ref, cot_ref, slots_ref, table_ref):
+def pack_kernel(flags_ref, cot_ref, act_ref, slots_ref, table_ref):
     find_senders(flags_ref, table_ref)
+    slots_ref[...] = act_ref[...]
     for k in range(cot_ref.shape[0] // BLK):
         base = k // 4 * 16
         rows = cot_ref[base : base + 16, :].astype(F32)
         low = k % 4 * BLK
-        slots_ref[table_ref[k]] = rows[low : low + BLK, :].astype(BF16)
+        slots_ref[table_ref[k], BLK : 2 * BLK, :] = rows[low : low + BLK, :].astype(BF16)
 
 
 def load_weight(place_ref, own, cross, weight_ref, sems):
@@ -147,9 +154,10 @@
 
 def backward_kernel(
     dest_ref, place_ref, order_ref,
-    frames_ref, kernel_ref, gain_ref, unit_ref, factor_ref, inv_ref, shift_ref, slots_ref,
-    o0, o1, c00, c01, c10, c11,
+    kernel_ref, gain_ref, inv_ref, slots_ref,
+    frames_hbm, unit_hbm, factor_hbm, shift_hbm, o0, o1, c00, c01, c10, c11,
     frame_ref, term_ref,
+    frames_ref, unit_ref, factor_ref, shift_ref,
     home_ref, homeb_ref, weight_ref, raw_ref, sorted_ref, grad_ref, moved_ref, sum_ref, sems,
 ):
     taps = kernel_ref.shape[0]
@@ -157,9 +165,13 @@
     blocks = order_ref.shape[0]
     size = columns // blocks
     copies = load_weight(place_ref, (o0, o1), ((c00, c01), (c10, c11)), weight_ref, sems)
+    saved = [(unit_hbm, unit_ref), (factor_hbm, factor_ref), (shift_hbm, shift_ref), (frames_hbm, frames_ref)]
+    late = [pltpu.make_async_copy(a, b, sems.at[len(copies) + i]) for i, (a, b) in enumerate(saved)]
+    for copy in late:
+        copy.start()
     for b in range(height // BLK):
         where = dest_ref[b]
-        rows = slots_ref[jnp.maximum(where, 0)].astype(F32)
+        rows = slots_ref[jnp.maximum(where, 0), BLK : 2 * BLK, :].astype(F32)
         home_ref[b * BLK : (b + 1) * BLK, :] = jnp.where(where >= 0, rows, 0.0)
     homeb_ref[...] = home_ref[...].astype(BF16)
     for copy in copies:
@@ -183,6 +195,8 @@
         return carry
 
     lax.fori_loop(0, columns // CHUNK, turn, 0)
+    for copy in late:
+        copy.wait()
     step = 16
     gain = gain_ref[...]
 
@@ -237,7 +251,7 @@
     copies = load_weight(place_ref, (o0, o1), ((c00, c01), (c10, c11)), weight_ref, sems)
     find_senders(flags_ref, table_ref)
     for k in range(rows_ref.shape[0] // BLK):
-        rows_ref[k * BLK : (k + 1) * BLK, :] = slots_ref[table_ref[k]].astype(F32)
+        rows_ref[k * BLK : (k + 1) * BLK, :] = slots_ref[table_ref[k], 0:BLK, :].astype(F32)
     turned = rows_ref[...].T
     for b in range(blocks):
         at = pl.multiple_of(block_place(place_ref, order_ref[b], blocks) * size, 8)
@@ -250,14 +264,15 @@
 
 VM = pl.BlockSpec(memory_space=pltpu.VMEM)
 SM = pl.BlockSpec(memory_space=pltpu.SMEM)
-HB = pl.BlockSpec(memory_space=pl.ANY)
-
-
-def call(fn, ins, outs, scratch, mib, name, flops, nbytes):
+AN = pl.BlockSpec(memory_space=pl.ANY)
+HB = pl.BlockSpec(memory_space=pltpu.HBM)
+
+
+def call(fn, ins, outs, scratch, mib, name, flops, nbytes, out_specs=None):
     return pl.pallas_call(
         fn,
         in_specs=ins,
-        out_specs=[VM] * len(outs),
+        out_specs=out_specs or [VM] * len(outs),
         out_shape=outs,
         scratch_shapes=scratch,
         compiler_params=params(mib),
@@ -286,56 +301,64 @@
     ny = lax.axis_size("y")
     line = exchange(jnp.broadcast_to(bucket[None], (ny, *bucket.shape)), "y").reshape(-1, half)
 
-    slots = jax.ShapeDtypeStruct((owners, BLK, columns), BF16)
+    slots = jax.ShapeDtypeStruct((owners, 2 * BLK, columns), BF16)
     whole = jax.ShapeDtypeStruct((height, columns), F32)
-    sent, unit, factor, inv, shifts = call(
+    shifts = jax.ShapeDtypeStruct((taps * height, height), BF16)
+    sent, inv, unit, factor, shifts = call(
         forward_kernel,
         [SM, SM, VM, VM, VM],
+        [slots, jax.ShapeDtypeStruct((height, 128), F32), whole, whole, shifts],
         [
-            slots,
-            whole,
-            whole,
-            jax.ShapeDtypeStruct((height, 128), F32),
-            jax.ShapeDtypeStruct((taps * height, height), BF16),
+            pltpu.VMEM(whole.shape, F32),
+            pltpu.VMEM(whole.shape, F32),
+            pltpu.VMEM(shifts.shape, BF16),
+            pltpu.VMEM(whole.shape, F32),
+            pltpu.SemaphoreType.DMA((3,)),
         ],
-        [pltpu.VMEM((height, columns), F32)],
-        40,
+        60,
         "forward",
         8 * taps * height * height * columns,
         16 * height * columns,
+        [VM] * 2 + [HB] * 3,
     )(lens, dest, frames, kernel, gain)
-    line, sent = lax.optimization_barrier((line, sent))
-    act_slots = exchange(sent, DP)
+    sends = jnp.any(dest[None, :] == jnp.arange(owners, dtype=jnp.int32)[:, None], axis=1).astype(jnp.int32)
+    sends = jnp.broadcast_to(sends[:, None, None], (owners, 1, 128))
+    line, sent, sends = lax.optimization_barrier((line, sent, sends))
 
     nx = lax.axis_size("x")
     by_x = [line] + [lax.ppermute(line, "x", [((i + k) % nx, i) for i in range(nx)]) for k in range(1, nx)]
+    flags = exchange(sends, DP)[:, 0, 0]
     nz = lax.axis_size("zh") * lax.axis_size("zl")
     up = [(i, (i + 1) % nz) for i in range(nz)]
     down = [((i + 1) % nz, i) for i in range(nz)]
     swap = [(0, 1), (1, 0)]
     low, high = jnp.concatenate(by_x[: nx // 2]), jnp.concatenate(by_x[nx // 2 :])
+    own = jnp.concatenate(by_x)
+    low, high, own, flags = lax.optimization_barrier((low, high, own, flags))
     c00 = lax.ppermute(low, ("zh", "zl"), up)
     c01 = lax.ppermute(high, ("zh", "zl"), down)
-    own = jnp.concatenate(by_x)
     own1 = lax.ppermute(own, "c", swap)
     c10 = lax.ppermute(c00, "c", swap)
     c11 = lax.ppermute(c01, "c", swap)
+
+    (packed,) = call(
+        pack_kernel, [SM, VM, VM], [slots], [pltpu.SMEM((owners,), jnp.int32)], 60, "pack", 0, 10 * cotangent.size
+    )(flags, cotangent, sent)
+    both_slots = exchange(packed, DP)
+
     pieces = (own, own1, c00, c01, c10, c11)
-
-    flags = (act_slots[:, 0, 0] > EMPTY / 2).astype(jnp.int32)
-    (cot_sent,) = call(
-        scatter_kernel, [SM, VM], [slots], [pltpu.SMEM((owners,), jnp.int32)], 40, "scatter", 0, 6 * cotangent.size
-    )(flags, cotangent)
-    cot_slots = exchange(cot_sent, DP)
-
     frame_grad, term = call(
         backward_kernel,
-        [SM] * 3 + [VM] * 8 + [HB] * 6,
+        [SM] * 3 + [VM] * 4 + [HB] * 4 + [AN] * 6,
         [
             jax.ShapeDtypeStruct((height, columns), BF16),
             jax.ShapeDtypeStruct((taps + 1, 1, columns), F32),
         ],
         [
+            pltpu.VMEM((height, columns), BF16),
+            pltpu.VMEM((height, columns), F32),
+            pltpu.VMEM((height, columns), F32),
+            pltpu.VMEM(shifts.shape, BF16),
             pltpu.VMEM((height, columns), F32),
             pltpu.VMEM((height, columns), BF16),
             pltpu.VMEM((columns, columns), BF16),
@@ -344,13 +367,13 @@
             pltpu.VMEM((height, columns), BF16),
             pltpu.VMEM((taps * height, CHUNK), F32),
             pltpu.VMEM((taps, 8, CHUNK), F32),
-            pltpu.SemaphoreType.DMA((6,)),
+            pltpu.SemaphoreType.DMA((10,)),
         ],
-        48,
+        60,
         "backward",
         8 * taps * height * height * columns + 2 * height * columns * columns,
         16 * height * columns + 2 * columns * columns,
-    )(dest, place, bucket_order, frames, kernel, gain, unit, factor, inv, shifts, cot_slots, *pieces)
+    )(dest, place, bucket_order, kernel, gain, inv, both_slots, frames, unit, factor, shifts, *pieces)
 
     mine = jnp.sum(exchange(term, NEAR), axis=0, keepdims=True)
     far = lax.axis_size(FAR)
@@ -360,7 +383,7 @@
 
     (projected,) = call(
         project_kernel,
-        [SM] * 3 + [VM] + [HB] * 6,
+        [SM] * 3 + [VM] + [AN] * 6,
         [jax.ShapeDtypeStruct(cotangent.shape, BF16)],
         [
             pltpu.SMEM((owners,), jnp.int32),
@@ -369,11 +392,11 @@
             pltpu.VMEM((columns, columns), BF16),
             pltpu.SemaphoreType.DMA((6,)),
         ],
-        40,
+        60,
         "project",
         2 * cotangent.size * columns,
         4 * cotangent.size + 2 * columns * columns,
-    )(flags, place, bucket_order, act_slots, *pieces)
+    )(flags, place, bucket_order, both_slots, *pieces)
     return projected, frame_grad, sums[:taps], sums[taps], updated
 
 

time: 174 us -> 171 us (0.983)
  waiting for transfers between devices: 25.4 us -> 15.7 us
  starting transfers between devices: 68.8 us -> 72.9 us
  local copies, waits for them, and re-layouts: 11.2 us -> 7.21 us
  Pallas kernels: 28.5 us -> 32.4 us
  blocking collectives: 34.2 us -> 36.8 us
    unnamed x50 -> x13, local copies, waits for them, and re-layouts: 9 us -> 1.87 us
    all_to_all x4, starting transfers between devices: 38.5 us -> 32.2 us  [exchange(): return lax.all_to_all(x, axes, split_axis=0, concat_axis=0, tiled=True)]
    ppermute x1, waiting for transfers between devices: 11.8 us -> 6.55 us  [body(): c00 = lax.ppermute(low, ('zh', 'zl'), up)]
    pallas_call x4, Pallas kernels: 28.5 us -> 32.4 us  [the longest x1 13.6 us: body(): call(backward_kernel, [SM] * 3 + [VM] * 4 + [HB] * 4 + [AN] * 6, [jax.Sha...]
    ppermute x3, waiting for transfers between devices: 9.04 us -> 5.16 us  [body(): lax.ppermute(line, 'x', [((i + k) % nx, i) for i in range(nx)])]
    ppermute x1, starting transfers between devices: 1.92 us -> 5.69 us  [body(): c11 = lax.ppermute(c01, 'c', swap)]
    ppermute x1, starting transfers between devices: 2.49 us -> 6.25 us  [body(): c10 = lax.ppermute(c00, 'c', swap)]
    ppermute x3, starting transfers between devices: 9.24 us -> 12.1 us  [body(): lax.ppermute(line, 'x', [((i + k) % nx, i) for i in range(nx)])]
  transfers between devices with their start and end apart: 12 -> 12, of which waited for: 6 -> 5; matrix products, arithmetic and copies ran while one was open for 1% -> 2% of each run, Pallas kernels for 8% -> 9%
where the time goes in v3:
time: 171 us; the launch traced here: 170 us
  starting transfers between devices  72.9 us (43%)
  blocking collectives  36.8 us (22%)
  Pallas kernels  32.4 us (19%)
  waiting for transfers between devices  15.7 us (9%)
  local copies, waits for them, and re-layouts  7.21 us (4%)
  other arithmetic  4.09 us (2%)
    all_to_all x2, blocking collectives, exchange(): return lax.all_to_all(x, axes, split_axis=0, concat_axis=0, tiled=True)  36.8 us
    all_to_all x4, starting transfers between devices, exchange(): return lax.all_to_all(x, axes, split_axis=0, concat_axis=0, tiled=True)  32.2 us
    pallas_call x1, Pallas kernels, body(): call(backward_kernel, [SM] * 3 + [VM] * 4 + [HB] * 4 + [AN] * 6, [jax.Sha...  13.6 us
    ppermute x3, starting transfers between devices, body(): lax.ppermute(line, 'x', [((i + k) % nx, i) for i in range(nx)])  12.1 us
    pallas_call x1, Pallas kernels, body(): call(forward_kernel, [SM, SM, VM, VM, VM], [slots, jax.ShapeDtypeStruct((...  9.96 us
    ppermute x1, starting transfers between devices, body(): c01 = lax.ppermute(high, ('zh', 'zl'), down)  8.59 us
    ppermute x1, waiting for transfers between devices, body(): c00 = lax.ppermute(low, ('zh', 'zl'), up)  6.55 us
    ppermute x1, starting transfers between devices, body(): c10 = lax.ppermute(c00, 'c', swap)  6.25 us
  transfers between devices with their start and end apart: 12, of which 5 were waited for; matrix products, arithmetic and copies ran while one was open for 2% of the time, Pallas kernels for 9%

profile of v3, /device:TPU:1, one launch (start us, length us, event | category | flops | bytes accessed | tf_op | source)
XLA Modules:
  0.0 170.0 jit_solution(6960639915798804367)
XLA Ops:
  0.6 0.0 copy-start.5
  0.7 1.2 multiply_subtract_fusion
  1.9 0.0 copy-start.3
  1.9 0.7 broadcast_in_dim.10
  2.7 7.7 %all-to-all-start = ((bf16[8,24,768]{2,1,0:T(8,128)(2,1)}), bf16[8,24,768]{2,1,0:T(8,128)(2,1)S(1)}, u32[]{:S(2)}, u32[]{:S(2)}) async-start(bf16[8,24,768]{2,1,0:T(8,128)(2,1)} %broadcast_in_dim.10), calls=%async_computation | async-start | bytes 589824 | tf_op jit(solution)/shard_map/all_to_all | solution.py:285
  10.3 0.1 fusion
  10.4 0.6 broadcast_in_dim.11.gain_ref
  11.0 10.0 %forward.1 = (bf16[64,8,1536]{2,1,0:T(8,128)(2,1)}, f32[192,128]{1,0:T(8,128)}, f32[192,1536]{1,0:T(8,128)}, f32[192,1536]{1,0:T(8,128)}, bf16[2880,192]{1,0:T(8,128)(2,1)}) custom-call(s32[8]{0:T(128)} %bitcast.15, s32[48]{0:T(128)} %bitcast.16, bf16[192,1536]{1,0:T(8,128)(2,1)} %frames_hbm.1, f32[15,1536]{1,0:T(8,128)} %kernel_ref.3, ...), custom_call_target="tpu_custom_call" | custom-call | flops 6794772480 | bytes 4718592 | tf_op jit(solution)/shard_map/forward/pallas_call | solution.py:307
  21.0 0.0 all-to-all-done
  21.0 0.7 broadcast_in_dim.12
  21.8 4.8 %collective-permute-start = (bf16[192,768]{1,0:T(8,128)(2,1)S(1)}, bf16[192,768]{1,0:T(8,128)(2,1)S(1)}, u32[]{:S(2)}, u32[]{:S(2)}) collective-permute-start(bf16[192,768]{1,0:T(8,128)(2,1)S(1)} %bitcast.9), channel_id=1, source_target_pairs={{8,0},{16,8},{24,16},{0,24},{9,1},{17,9},{25,17},{1,25},{10,2},{18... | collective-permute-start | bytes 884744 | tf_op jit(solution)/shard_map/ppermute | solution.py:329
  26.6 9.3 %all-to-all-start.1 = ((s32[64,1,128]{2,1,0:T(1,128)}), s32[64,1,128]{2,1,0:T(1,128)S(1)}, u32[]{:S(2)}, u32[]{:S(2)}) async-start(s32[64,1,128]{2,1,0:T(1,128)} %broadcast_in_dim.12), calls=%async_computation.1 | async-start | bytes 65536 | tf_op jit(solution)/shard_map/all_to_all | solution.py:285
  35.9 2.9 %collective-permute-start.2 = (bf16[192,768]{1,0:T(8,128)(2,1)S(1)}, bf16[192,768]{1,0:T(8,128)(2,1)S(1)}, u32[]{:S(2)}, u32[]{:S(2)}) collective-permute-start(bf16[192,768]{1,0:T(8,128)(2,1)S(1)} %bitcast.10), channel_id=1, source_target_pairs={{24,0},{0,8},{8,16},{16,24},{25,1},{1,9},{9,17},{17,25},{26,2},{2,... | collective-permute-start | bytes 884744 | tf_op jit(solution)/shard_map/ppermute | solution.py:329
  38.8 4.3 %collective-permute-start.1 = (bf16[192,768]{1,0:T(8,128)(2,1)S(1)}, bf16[192,768]{1,0:T(8,128)(2,1)S(1)}, u32[]{:S(2)}, u32[]{:S(2)}) collective-permute-start(bf16[192,768]{1,0:T(8,128)(2,1)S(1)} %bitcast.11), channel_id=1, source_target_pairs={{16,0},{24,8},{0,16},{8,24},{17,1},{25,9},{1,17},{9,25},{18,2},{26... | collective-permute-start | bytes 884744 | tf_op jit(solution)/shard_map/ppermute | solution.py:329
  43.2 2.0 %all-to-all-done.1 = s32[64,1,128]{2,1,0:T(1,128)S(1)} async-done(((s32[64,1,128]{2,1,0:T(1,128)}), s32[64,1,128]{2,1,0:T(1,128)S(1)}, u32[]{:S(2)}, u32[]{:S(2)}) %all-to-all-start.1) | async-done | bytes 32800 | tf_op jit(solution)/shard_map/all_to_all | solution.py:285
  45.1 1.8 %slice_reduce_fusion.flags_ref = s32[64]{0:T(128)} fusion(s32[64,1,128]{2,1,0:T(1,128)S(1)} %all-to-all-done.1), kind=kLoop, calls=%fused_computation.6 | loop fusion | bytes 512 | tf_op jit(solution)/shard_map/slice | solution.py:330
  47.0 0.0 collective-permute-done
  47.0 0.9 pad_maximum_fusion.1
  47.8 0.0 collective-permute-done.2
  47.8 5.2 %collective-permute-done.1 = bf16[192,768]{1,0:T(8,128)(2,1)S(1)} collective-permute-done((bf16[192,768]{1,0:T(8,128)(2,1)S(1)}, bf16[192,768]{1,0:T(8,128)(2,1)S(1)}, u32[]{:S(2)}, u32[]{:S(2)}) %collective-permute-start.1) | collective-permute-done | bytes 294944 | tf_op jit(solution)/shard_map/ppermute | solution.py:329
  53.0 0.1 pad_maximum_fusion.o0
  53.1 1.0 pad_maximum_fusion.2
  54.0 3.6 %pack.1 = bf16[64,8,1536]{2,1,0:T(8,128)(2,1)} custom-call(s32[64]{0:T(128)} %slice_reduce_fusion.flags_ref, bf16[128,1536]{1,0:T(8,128)(2,1)} %cot_ref.1, bf16[64,8,1536]{2,1,0:T(8,128)(2,1)} %get-tuple-element.23.act_ref), custom_call_target="tpu_custom_call" | custom-call | bytes 1966080 | tf_op jit(solution)/shard_map/pack/pallas_call | solution.py:344
  57.6 9.0 %all-to-all-start.2 = ((bf16[64,8,1536]{2,1,0:T(8,128)(2,1)}), bf16[64,8,1536]{2,1,0:T(8,128)(2,1)S(1)}, u32[]{:S(2)}, u32[]{:S(2)}) async-start(bf16[64,8,1536]{2,1,0:T(8,128)(2,1)} %pack.1), calls=%async_computation.2 | async-start | bytes 3145728 | tf_op jit(solution)/shard_map/all_to_all | solution.py:285
  66.7 3.0 %collective-permute-start.4 = (bf16[384,768]{1,0:T(8,128)(2,1)}, bf16[384,768]{1,0:T(8,128)(2,1)S(1)}, u32[]{:S(2)}, u32[]{:S(2)}) collective-permute-start(bf16[384,768]{1,0:T(8,128)(2,1)} %pad_maximum_fusion.1), channel_id=1, source_target_pairs={{0,32},{32,128},{128,160},{160,256},{256,288},{288,384},{384,416},... | collective-permute-start | bytes 1769480 | tf_op jit(solution)/shard_map/ppermute | solution.py:338
  69.7 8.6 %collective-permute-start.5 = (bf16[384,768]{1,0:T(8,128)(2,1)}, bf16[384,768]{1,0:T(8,128)(2,1)}, u32[]{:S(2)}, u32[]{:S(2)}) collective-permute-start(bf16[384,768]{1,0:T(8,128)(2,1)} %pad_maximum_fusion.2), channel_id=1, source_target_pairs={{32,0},{128,32},{160,128},{256,160},{288,256},{384,288},{416,384},... | collective-permute-start | bytes 1769480 | tf_op jit(solution)/shard_map/ppermute | solution.py:339
  78.3 5.0 %collective-permute-start.3 = (bf16[768,768]{1,0:T(8,128)(2,1)S(1)}, bf16[768,768]{1,0:T(8,128)(2,1)}, u32[]{:S(2)}, u32[]{:S(2)}) collective-permute-start(bf16[768,768]{1,0:T(8,128)(2,1)S(1)} %pad_maximum_fusion.o0), channel_id=1, source_target_pairs={{0,64},{64,0},{1,65},{65,1},{2,66},{66,2},{3,67},{67,3},{4,68},{68... | collective-permute-start | bytes 3538952 | tf_op jit(solution)/shard_map/ppermute | solution.py:340
  83.3 6.6 %collective-permute-done.4.c00 = bf16[384,768]{1,0:T(8,128)(2,1)S(1)} collective-permute-done((bf16[384,768]{1,0:T(8,128)(2,1)}, bf16[384,768]{1,0:T(8,128)(2,1)S(1)}, u32[]{:S(2)}, u32[]{:S(2)}) %collective-permute-start.4) | collective-permute-done | bytes 589856 | tf_op jit(solution)/shard_map/ppermute | solution.py:338
  89.9 6.2 %collective-permute-start.6 = (bf16[384,768]{1,0:T(8,128)(2,1)S(1)}, bf16[384,768]{1,0:T(8,128)(2,1)}, u32[]{:S(2)}, u32[]{:S(2)}) collective-permute-start(bf16[384,768]{1,0:T(8,128)(2,1)S(1)} %collective-permute-done.4.c00), channel_id=1, source_target_pairs={{0,64},{64,0},{1,65},{65,1},{2,66},{66,2},{3,67},{67,3},{4,68},{68... | collective-permute-start | bytes 1769480 | tf_op jit(solution)/shard_map/ppermute | solution.py:341
  96.2 0.0 collective-permute-done.5.c01
  96.2 5.7 %collective-permute-start.7 = (bf16[384,768]{1,0:T(8,128)(2,1)}, bf16[384,768]{1,0:T(8,128)(2,1)}, u32[]{:S(2)}, u32[]{:S(2)}) collective-permute-start(bf16[384,768]{1,0:T(8,128)(2,1)} %collective-permute-done.5.c01), channel_id=1, source_target_pairs={{0,64},{64,0},{1,65},{65,1},{2,66},{66,2},{3,67},{67,3},{4,68},{68... | collective-permute-start | bytes 1769480 | tf_op jit(solution)/shard_map/ppermute | solution.py:342
  101.9 0.7 pad_add_fusion.place_ref
  102.5 0.0 collective-permute-done.6.c10
  102.5 1.3 collective-permute-done.7.c11
  103.8 0.0 collective-permute-done.3.o1
  103.8 1.2 copy-done
  105.0 13.6 %backward.1 = (bf16[192,1536]{1,0:T(8,128)(2,1)}, f32[16,1,1536]{2,1,0:T(1,128)}) custom-call(s32[48]{0:T(128)} %bitcast.17, s32[3]{0:T(128)} %pad_add_fusion.place_ref, s32[64]{0:T(128)} %order_ref.3, f32[15,1536]{1,0:T(8,128)} %kernel_ref.3, f32[1,1536]{1,0:T(1,128)} %broadcast_in_dim.11.gain_ref, f32[192,128]{1,0:T(8,128)} %get-tuple-element.27.inv_ref, ...), custom_call_target="tpu_custom_call" | custom-call | flops 7700742144 | bytes 9437184 | tf_op jit(solution)/shard_map/backward/pallas_call | solution.py:350
  118.6 13.8 %all_to_all.30 = f32[16,1,1536]{2,1,0:T(1,128)S(1)} all-to-all(f32[16,1,1536]{2,1,0:T(1,128)} %get-tuple-element.32), channel_id=1, replica_groups=mesh['zh'=4,'c'=2,'zl'=2,'x'=4,'y'=8] {'c','zl','x'}, dimensions={0} | all-to-all | bytes 196608 | tf_op jit(solution)/shard_map/all_to_all | solution.py:285
  132.4 0.1 reduce_sum.18
  132.5 0.1 broadcast_in_dim.13
  132.6 23.0 %all_to_all.31 = f32[32,1,1536]{2,1,0:T(1,128)S(1)} all-to-all(f32[32,1,1536]{2,1,0:T(1,128)S(1)} %broadcast_in_dim.13), channel_id=1, replica_groups=mesh['zh'=4,'c'=2,'zl'=2,'x'=4,'y'=8] {'zh','y'}, dimensions={0} | all-to-all | bytes 393216 | tf_op jit(solution)/shard_map/all_to_all | solution.py:285
  155.6 0.1 reduce_sum.19
  155.7 0.7 broadcast_in_dim.14
  156.4 6.3 %all-to-all-start.5 = ((f32[16,1,1536]{2,1,0:T(1,128)}), f32[16,1,1536]{2,1,0:T(1,128)S(1)}, u32[]{:S(2)}, u32[]{:S(2)}) async-start(f32[16,1,1536]{2,1,0:T(1,128)} %broadcast_in_dim.14), calls=%async_computation.5 | async-start | bytes 196608 | tf_op jit(solution)/shard_map/all_to_all | solution.py:285
  162.7 5.3 %project.1 = bf16[128,1536]{1,0:T(8,128)(2,1)} custom-call(s32[64]{0:T(128)} %slice_reduce_fusion.flags_ref, s32[3]{0:T(128)} %pad_add_fusion.place_ref, s32[64]{0:T(128)} %order_ref.3, bf16[64,8,1536]{2,1,0:T(8,128)(2,1)} %copy-done, bf16[768,768]{1,0:T(8,128)(2,1)} %copy-done.1, bf16[768,768]{1,0:T(8,128)(2,1)} %collective-permute-done.3.o1, ...), custom_call_target="tpu_custom_call" | custom-call | flops 603979776 | bytes 5505024 | tf_op jit(solution)/shard_map/project/pallas_call | solution.py:384
  168.0 0.7 all-to-all-done.5
  168.7 0.7 copy.20
  169.4 0.6 slice_reduce_fusion.1
  (14 shorter events, 0.1 us)
Async XLA Ops:
  0.6 9.7 %copy-start.5 = (s32[1,48]{1,0:T(1,128)S(1)}, s32[1,48]{1,0:T(1,128)}, u32[]{:S(2)}) copy-start(s32[1,48]{1,0:T(1,128)} %param.13) | copy-start | bytes 580
  0.6 9.8 %copy-start.4 = (f32[1536]{0:T(1024)S(1)}, f32[1536]{0:T(1024)}, u32[]{:S(2)}) copy-start(f32[1536]{0:T(1024)} %param.15) | copy-start | bytes 18436
  1.9 19.1 %copy-start.3 = (f32[24,1536]{1,0:T(8,128)}, f32[24,1536]{1,0:T(8,128)S(1)}, u32[]{:S(2)}) copy-start(f32[24,1536]{1,0:T(8,128)S(1)} %multiply_subtract_fusion) | copy-start | bytes 442372
  2.7 18.3 %all-to-all-start = ((bf16[8,24,768]{2,1,0:T(8,128)(2,1)}), bf16[8,24,768]{2,1,0:T(8,128)(2,1)S(1)}, u32[]{:S(2)}, u32[]{:S(2)}) async-start(bf16[8,24,768]{2,1,0:T(8,128)(2,1)} %broadcast_in_dim.10), calls=%async_computation | async-start | bytes 589824 | tf_op jit(solution)/shard_map/all_to_all | solution.py:285
  21.8 25.2 %collective-permute-start = (bf16[192,768]{1,0:T(8,128)(2,1)S(1)}, bf16[192,768]{1,0:T(8,128)(2,1)S(1)}, u32[]{:S(2)}, u32[]{:S(2)}) collective-permute-start(bf16[192,768]{1,0:T(8,128)(2,1)S(1)} %bitcast.9), channel_id=1, source_target_pairs={{8,0},{16,8},{24,16},{0,24},{9,1},{17,9},{25,17},{1,25},{10,2},{18... | collective-permute-start | bytes 884744 | tf_op jit(solution)/shard_map/ppermute | solution.py:329
  26.6 18.5 %all-to-all-start.1 = ((s32[64,1,128]{2,1,0:T(1,128)}), s32[64,1,128]{2,1,0:T(1,128)S(1)}, u32[]{:S(2)}, u32[]{:S(2)}) async-start(s32[64,1,128]{2,1,0:T(1,128)} %broadcast_in_dim.12), calls=%async_computation.1 | async-start | bytes 65536 | tf_op jit(solution)/shard_map/all_to_all | solution.py:285
  35.9 11.9 %collective-permute-start.2 = (bf16[192,768]{1,0:T(8,128)(2,1)S(1)}, bf16[192,768]{1,0:T(8,128)(2,1)S(1)}, u32[]{:S(2)}, u32[]{:S(2)}) collective-permute-start(bf16[192,768]{1,0:T(8,128)(2,1)S(1)} %bitcast.10), channel_id=1, source_target_pairs={{24,0},{0,8},{8,16},{16,24},{25,1},{1,9},{9,17},{17,25},{26,2},{2,... | collective-permute-start | bytes 884744 | tf_op jit(solution)/shard_map/ppermute | solution.py:329
  38.8 14.1 %collective-permute-start.1 = (bf16[192,768]{1,0:T(8,128)(2,1)S(1)}, bf16[192,768]{1,0:T(8,128)(2,1)S(1)}, u32[]{:S(2)}, u32[]{:S(2)}) collective-permute-start(bf16[192,768]{1,0:T(8,128)(2,1)S(1)} %bitcast.11), channel_id=1, source_target_pairs={{16,0},{24,8},{0,16},{8,24},{17,1},{25,9},{1,17},{9,25},{18,2},{26... | collective-permute-start | bytes 884744 | tf_op jit(solution)/shard_map/ppermute | solution.py:329
  53.0 25.2 %copy-start.1 = (bf16[768,768]{1,0:T(8,128)(2,1)}, bf16[768,768]{1,0:T(8,128)(2,1)S(1)}, u32[]{:S(2)}) copy-start(bf16[768,768]{1,0:T(8,128)(2,1)S(1)} %pad_maximum_fusion.o0) | copy-start | bytes 3538948
  57.6 46.2 %all-to-all-start.2 = ((bf16[64,8,1536]{2,1,0:T(8,128)(2,1)}), bf16[64,8,1536]{2,1,0:T(8,128)(2,1)S(1)}, u32[]{:S(2)}, u32[]{:S(2)}) async-start(bf16[64,8,1536]{2,1,0:T(8,128)(2,1)} %pack.1), calls=%async_computation.2 | async-start | bytes 3145728 | tf_op jit(solution)/shard_map/all_to_all | solution.py:285
  66.7 23.2 %collective-permute-start.4 = (bf16[384,768]{1,0:T(8,128)(2,1)}, bf16[384,768]{1,0:T(8,128)(2,1)S(1)}, u32[]{:S(2)}, u32[]{:S(2)}) collective-permute-start(bf16[384,768]{1,0:T(8,128)(2,1)} %pad_maximum_fusion.1), channel_id=1, source_target_pairs={{0,32},{32,128},{128,160},{160,256},{256,288},{288,384},{384,416},... | collective-permute-start | bytes 1769480 | tf_op jit(solution)/shard_map/ppermute | solution.py:338
  69.7 26.5 %collective-permute-start.5 = (bf16[384,768]{1,0:T(8,128)(2,1)}, bf16[384,768]{1,0:T(8,128)(2,1)}, u32[]{:S(2)}, u32[]{:S(2)}) collective-permute-start(bf16[384,768]{1,0:T(8,128)(2,1)} %pad_maximum_fusion.2), channel_id=1, source_target_pairs={{32,0},{128,32},{160,128},{256,160},{288,256},{384,288},{416,384},... | collective-permute-start | bytes 1769480 | tf_op jit(solution)/shard_map/ppermute | solution.py:339
  78.3 25.5 %collective-permute-start.3 = (bf16[768,768]{1,0:T(8,128)(2,1)S(1)}, bf16[768,768]{1,0:T(8,128)(2,1)}, u32[]{:S(2)}, u32[]{:S(2)}) collective-permute-start(bf16[768,768]{1,0:T(8,128)(2,1)S(1)} %pad_maximum_fusion.o0), channel_id=1, source_target_pairs={{0,64},{64,0},{1,65},{65,1},{2,66},{66,2},{3,67},{67,3},{4,68},{68... | collective-permute-start | bytes 3538952 | tf_op jit(solution)/shard_map/ppermute | solution.py:340
  89.9 13.9 %copy-start.2 = (bf16[384,768]{1,0:T(8,128)(2,1)}, bf16[384,768]{1,0:T(8,128)(2,1)S(1)}, u32[]{:S(2)}) copy-start(bf16[384,768]{1,0:T(8,128)(2,1)S(1)} %collective-permute-done.4.c00) | copy-start | bytes 1769476
  89.9 12.6 %collective-permute-start.6 = (bf16[384,768]{1,0:T(8,128)(2,1)S(1)}, bf16[384,768]{1,0:T(8,128)(2,1)}, u32[]{:S(2)}, u32[]{:S(2)}) collective-permute-start(bf16[384,768]{1,0:T(8,128)(2,1)S(1)} %collective-permute-done.4.c00), channel_id=1, source_target_pairs={{0,64},{64,0},{1,65},{65,1},{2,66},{66,2},{3,67},{67,3},{4,68},{68... | collective-permute-start | bytes 1769480 | tf_op jit(solution)/shard_map/ppermute | solution.py:341
  96.2 7.7 %collective-permute-start.7 = (bf16[384,768]{1,0:T(8,128)(2,1)}, bf16[384,768]{1,0:T(8,128)(2,1)}, u32[]{:S(2)}, u32[]{:S(2)}) collective-permute-start(bf16[384,768]{1,0:T(8,128)(2,1)} %collective-permute-done.5.c01), channel_id=1, source_target_pairs={{0,64},{64,0},{1,65},{65,1},{2,66},{66,2},{3,67},{67,3},{4,68},{68... | collective-permute-start | bytes 1769480 | tf_op jit(solution)/shard_map/ppermute | solution.py:342
  103.8 1.2 copy-start
  156.4 12.3 %all-to-all-start.5 = ((f32[16,1,1536]{2,1,0:T(1,128)}), f32[16,1,1536]{2,1,0:T(1,128)S(1)}, u32[]{:S(2)}, u32[]{:S(2)}) async-start(f32[16,1,1536]{2,1,0:T(1,128)} %broadcast_in_dim.14), calls=%async_computation.5 | async-start | bytes 196608 | tf_op jit(solution)/shard_map/all_to_all | solution.py:285

commit v4 on v3

--- a/solution.py
+++ b/solution.py
@@ -10,6 +10,7 @@
 ROWS = 128
 BLK = 4
 CHUNK = 256
+EMPTY = -2.0
 DP = ("zl", "x", "y")
 NEAR = ("c", "zl", "x")
 FAR = ("zh", "y")
@@ -91,12 +92,13 @@
     lax.fori_loop(0, height // step, norm, 0)
     copies[1].start()
     copies[2].start()
+    slots_ref[:, :, 0:128] = jnp.full((slots_ref.shape[0], BLK, 128), EMPTY, BF16)
     for b in range(height // BLK):
         where = dest_ref[b]
 
         @pl.when(where >= 0)
         def _():
-            slots_ref[where, 0:BLK, :] = act_ref[b * BLK : (b + 1) * BLK, :].astype(BF16)
+            slots_ref[where] = act_ref[b * BLK : (b + 1) * BLK, :].astype(BF16)
 
     for copy in copies:
         copy.wait()
@@ -118,44 +120,40 @@
     lax.fori_loop(0, flags_ref.shape[0], look, jnp.int32(0))
 
 
-def pack_kernel(flags_ref, cot_ref, act_ref, slots_ref, table_ref):
+def scatter_kernel(flags_ref, cot_ref, slots_ref, table_ref):
     find_senders(flags_ref, table_ref)
-    slots_ref[...] = act_ref[...]
     for k in range(cot_ref.shape[0] // BLK):
         base = k // 4 * 16
         rows = cot_ref[base : base + 16, :].astype(F32)
         low = k % 4 * BLK
-        slots_ref[table_ref[k], BLK : 2 * BLK, :] = rows[low : low + BLK, :].astype(BF16)
-
-
-def load_weight(place_ref, own, cross, weight_ref, sems):
-    size, width = own[0].shape
-    part = size // 2
-    core = place_ref[1]
-    copies = []
-    for h in range(2):
-        start = core * width if h == 0 else (1 - core) * width
-        at = pl.ds(pl.multiple_of(start, 128), width)
-        pairs = [(own[h], 0, size), (cross[h][0], size, part), (cross[h][1], size + part, part)]
-        for source, row, count in pairs:
-            copies.append(
-                pltpu.make_async_copy(source, weight_ref.at[pl.ds(row, count), at], sems.at[len(copies)])
-            )
+        slots_ref[table_ref[k]] = rows[low : low + BLK, :].astype(BF16)
+
+
+def load_weight(place_ref, pieces, weight_ref, sems):
+    width = pieces[0].shape[1]
+    core = place_ref[0]
+    copies, row = [], 0
+    for i, piece in enumerate(pieces):
+        start = core * width if i < len(pieces) // 2 else (1 - core) * width
+        row = row % weight_ref.shape[0]
+        target = weight_ref.at[pl.ds(row, piece.shape[0]), pl.ds(pl.multiple_of(start, 128), width)]
+        copies.append(pltpu.make_async_copy(piece, target, sems.at[i]))
+        row += piece.shape[0]
     for copy in copies:
         copy.start()
     return copies
 
 
 def block_place(place_ref, owner, blocks):
-    nx, ny = NX, blocks // (2 * NX)
-    other = jnp.where(owner // (ny * nx) != place_ref[0], blocks // 2, 0)
-    return other + (owner // ny % nx - place_ref[2] + nx) % nx * ny + owner % ny
+    ny = blocks // (2 * NX)
+    oz, ox, oy = owner // (ny * NX), owner // ny % NX, owner % ny
+    return ((ox - place_ref[1] + NX) % NX * 2 + oz) * ny + oy
 
 
 def backward_kernel(
     dest_ref, place_ref, order_ref,
     kernel_ref, gain_ref, inv_ref, slots_ref,
-    frames_hbm, unit_hbm, factor_hbm, shift_hbm, o0, o1, c00, c01, c10, c11,
+    frames_hbm, unit_hbm, factor_hbm, shift_hbm, p0, p1, p2, p3, p4, q0, q1, q2, q3, q4,
     frame_ref, term_ref,
     frames_ref, unit_ref, factor_ref, shift_ref,
     home_ref, homeb_ref, weight_ref, raw_ref, sorted_ref, grad_ref, moved_ref, sum_ref, sems,
@@ -164,14 +162,14 @@
     height, columns = frames_ref.shape
     blocks = order_ref.shape[0]
     size = columns // blocks
-    copies = load_weight(place_ref, (o0, o1), ((c00, c01), (c10, c11)), weight_ref, sems)
+    copies = load_weight(place_ref, (p0, p1, p2, p3, p4, q0, q1, q2, q3, q4), weight_ref, sems)
     saved = [(unit_hbm, unit_ref), (factor_hbm, factor_ref), (shift_hbm, shift_ref), (frames_hbm, frames_ref)]
     late = [pltpu.make_async_copy(a, b, sems.at[len(copies) + i]) for i, (a, b) in enumerate(saved)]
     for copy in late:
         copy.start()
     for b in range(height // BLK):
         where = dest_ref[b]
-        rows = slots_ref[jnp.maximum(where, 0), BLK : 2 * BLK, :].astype(F32)
+        rows = slots_ref[jnp.maximum(where, 0)].astype(F32)
         home_ref[b * BLK : (b + 1) * BLK, :] = jnp.where(where >= 0, rows, 0.0)
     homeb_ref[...] = home_ref[...].astype(BF16)
     for copy in copies:
@@ -242,16 +240,16 @@
 
 def project_kernel(
     flags_ref, place_ref, order_ref,
-    slots_ref, o0, o1, c00, c01, c10, c11,
+    slots_ref, p0, p1, p2, p3, p4, q0, q1, q2, q3, q4,
     out_ref,
     table_ref, rows_ref, turned_ref, weight_ref, sems,
 ):
     blocks = order_ref.shape[0]
     size = weight_ref.shape[0] // blocks
-    copies = load_weight(place_ref, (o0, o1), ((c00, c01), (c10, c11)), weight_ref, sems)
+    copies = load_weight(place_ref, (p0, p1, p2, p3, p4, q0, q1, q2, q3, q4), weight_ref, sems)
     find_senders(flags_ref, table_ref)
     for k in range(rows_ref.shape[0] // BLK):
-        rows_ref[k * BLK : (k + 1) * BLK, :] = slots_ref[table_ref[k], 0:BLK, :].astype(F32)
+        rows_ref[k * BLK : (k + 1) * BLK, :] = slots_ref[table_ref[k]].astype(F32)
     turned = rows_ref[...].T
     for b in range(blocks):
         at = pl.multiple_of(block_place(place_ref, order_ref[b], blocks) * size, 8)
@@ -290,18 +288,18 @@
     taps = kernel.shape[0]
     owners = bucket_order.shape[0]
     half = columns // 2
-    core, zl, x = lax.axis_index("c"), lax.axis_index("zl"), lax.axis_index("x")
+    core, x = lax.axis_index("c"), lax.axis_index("x")
     dest = destination[0]
     lens = lengths[0]
-    place = jnp.stack([zl, core, x]).astype(jnp.int32)
+    place = jnp.stack([core, x]).astype(jnp.int32)
     gain = norm_gain[None, :]
 
     updated = adam_step(master, moment, second, gradient)
     bucket = lax.dynamic_slice_in_dim(updated, core * half, half, axis=1).astype(BF16)
-    ny = lax.axis_size("y")
-    line = exchange(jnp.broadcast_to(bucket[None], (ny, *bucket.shape)), "y").reshape(-1, half)
-
-    slots = jax.ShapeDtypeStruct((owners, 2 * BLK, columns), BF16)
+    near = lax.axis_size(("zl", "y"))
+    line = exchange(jnp.broadcast_to(bucket[None], (near, *bucket.shape)), ("zl", "y")).reshape(-1, half)
+
+    slots = jax.ShapeDtypeStruct((owners, BLK, columns), BF16)
     whole = jax.ShapeDtypeStruct((height, columns), F32)
     shifts = jax.ShapeDtypeStruct((taps * height, height), BF16)
     sent, inv, unit, factor, shifts = call(
@@ -321,35 +319,31 @@
         16 * height * columns,
         [VM] * 2 + [HB] * 3,
     )(lens, dest, frames, kernel, gain)
-    sends = jnp.any(dest[None, :] == jnp.arange(owners, dtype=jnp.int32)[:, None], axis=1).astype(jnp.int32)
-    sends = jnp.broadcast_to(sends[:, None, None], (owners, 1, 128))
-    line, sent, sends = lax.optimization_barrier((line, sent, sends))
+    line, sent = lax.optimization_barrier((line, sent))
+    act_slots = exchange(sent, DP)
 
     nx = lax.axis_size("x")
-    by_x = [line] + [lax.ppermute(line, "x", [((i + k) % nx, i) for i in range(nx)]) for k in range(1, nx)]
-    flags = exchange(sends, DP)[:, 0, 0]
-    nz = lax.axis_size("zh") * lax.axis_size("zl")
-    up = [(i, (i + 1) % nz) for i in range(nz)]
-    down = [((i + 1) % nz, i) for i in range(nz)]
+    ahead = [((i + 1) % nx, i) for i in range(nx)]
+    behind = [(i, (i + 1) % nx) for i in range(nx)]
     swap = [(0, 1), (1, 0)]
-    low, high = jnp.concatenate(by_x[: nx // 2]), jnp.concatenate(by_x[nx // 2 :])
-    own = jnp.concatenate(by_x)
-    low, high, own, flags = lax.optimization_barrier((low, high, own, flags))
-    c00 = lax.ppermute(low, ("zh", "zl"), up)
-    c01 = lax.ppermute(high, ("zh", "zl"), down)
-    own1 = lax.ppermute(own, "c", swap)
-    c10 = lax.ppermute(c00, "c", swap)
-    c11 = lax.ppermute(c01, "c", swap)
-
-    (packed,) = call(
-        pack_kernel, [SM, VM, VM], [slots], [pltpu.SMEM((owners,), jnp.int32)], 60, "pack", 0, 10 * cotangent.size
-    )(flags, cotangent, sent)
-    both_slots = exchange(packed, DP)
-
-    pieces = (own, own1, c00, c01, c10, c11)
+    flags = (act_slots[:, 0, 0] > EMPTY / 2).astype(jnp.int32)
+    next_x, last_x = lax.ppermute(line, "x", ahead), lax.ppermute(line, "x", behind)
+    line_c = lax.ppermute(line, "c", swap)
+    flags, next_x, last_x, line_c = lax.optimization_barrier((flags, next_x, last_x, line_c))
+    part = line.shape[0] // 2
+    far_low = lax.ppermute(next_x[:part], "x", ahead)
+    far_high = lax.ppermute(last_x[part:], "x", behind)
+    half_pieces = [line, next_x, far_low, far_high, last_x]
+    pieces = half_pieces + [line_c] + [lax.ppermute(piece, "c", swap) for piece in half_pieces[1:]]
+
+    (cot_sent,) = call(
+        scatter_kernel, [SM, VM], [slots], [pltpu.SMEM((owners,), jnp.int32)], 60, "scatter", 0, 6 * cotangent.size
+    )(flags, cotangent)
+    cot_slots = exchange(cot_sent, DP)
+
     frame_grad, term = call(
         backward_kernel,
-        [SM] * 3 + [VM] * 4 + [HB] * 4 + [AN] * 6,
+        [SM] * 3 + [VM] * 4 + [HB] * 4 + [AN] * 10,
         [
             jax.ShapeDtypeStruct((height, columns), BF16),
             jax.ShapeDtypeStruct((taps + 1, 1, columns), F32),
@@ -367,13 +361,13 @@
             pltpu.VMEM((height, columns), BF16),
             pltpu.VMEM((taps * height, CHUNK), F32),
             pltpu.VMEM((taps, 8, CHUNK), F32),
-            pltpu.SemaphoreType.DMA((10,)),
+            pltpu.SemaphoreType.DMA((14,)),
         ],
         60,
         "backward",
         8 * taps * height * height * columns + 2 * height * columns * columns,
         16 * height * columns + 2 * columns * columns,
-    )(dest, place, bucket_order, kernel, gain, inv, both_slots, frames, unit, factor, shifts, *pieces)
+    )(dest, place, bucket_order, kernel, gain, inv, cot_slots, frames, unit, factor, shifts, *pieces)
 
     mine = jnp.sum(exchange(term, NEAR), axis=0, keepdims=True)
     far = lax.axis_size(FAR)
@@ -383,20 +377,20 @@
 
     (projected,) = call(
         project_kernel,
-        [SM] * 3 + [VM] + [AN] * 6,
+        [SM] * 3 + [VM] + [AN] * 10,
         [jax.ShapeDtypeStruct(cotangent.shape, BF16)],
         [
             pltpu.SMEM((owners,), jnp.int32),
             pltpu.VMEM(cotangent.shape, F32),
             pltpu.VMEM(cotangent.shape[::-1], F32),
             pltpu.VMEM((columns, columns), BF16),
-            pltpu.SemaphoreType.DMA((6,)),
+            pltpu.SemaphoreType.DMA((10,)),
         ],
         60,
         "project",
         2 * cotangent.size * columns,
         4 * cotangent.size + 2 * columns * columns,
-    )(flags, place, bucket_order, both_slots, *pieces)
+    )(flags, place, bucket_order, act_slots, *pieces)
     return projected, frame_grad, sums[:taps], sums[taps], updated
 
 

time: 171 us -> 167 us (0.977)
  starting transfers between devices: 72.9 us -> 62.9 us
  waiting for transfers between devices: 15.7 us -> 25.7 us
    all_to_all x4, waiting for transfers between devices: 2.64 us -> 17.5 us  [exchange(): return lax.all_to_all(x, axes, split_axis=0, concat_axis=0, tiled=True)]
    ppermute x8 -> x9, starting transfers between devices: 40.7 us -> 28 us  [the longest x4 11.8 us: body(): lax.ppermute(piece, 'c', swap)]
    ppermute x8 -> x9, waiting for transfers between devices: 13 us -> 8.24 us  [the longest x1 3.98 us: body(): lax.ppermute(line, 'x', behind)]
    all_to_all x4, starting transfers between devices: 32.2 us -> 34.9 us  [exchange(): return lax.all_to_all(x, axes, split_axis=0, concat_axis=0, tiled=True)]
    concatenate x3 -> x0, other arithmetic: 1.89 us -> none  [the longest x1 0.96 us: body(): jnp.concatenate(by_x[nx // 2:])]
    slice x1 -> x2, local copies, waits for them, and re-layouts: 1.81 us -> 0.04 us  [the longest x1 0.02 us: body(): far_high = lax.ppermute(last_x[part:], 'x', behind)]
    convert_element_type x1, other arithmetic: 0.01 us -> 1.75 us  [body(): flags = (act_slots[:, 0, 0] > EMPTY / 2).astype(jnp.int32)]
  transfers between devices with their start and end apart: 12 -> 13, of which waited for: 5 -> 7; matrix products, arithmetic and copies ran while one was open for 2% -> 2% of each run, Pallas kernels for 9% -> 9%
where the time goes in v4:
time: 167 us
  starting transfers between devices  62.9 us (38%)
  blocking collectives  36.7 us (22%)
  Pallas kernels  30.8 us (18%)
  waiting for transfers between devices  25.7 us (15%)
  local copies, waits for them, and re-layouts  5.63 us (3%)
  other arithmetic  3.83 us (2%)
    all_to_all x2, blocking collectives, exchange(): return lax.all_to_all(x, axes, split_axis=0, concat_axis=0, tiled=True)  36.7 us
    all_to_all x4, starting transfers between devices, exchange(): return lax.all_to_all(x, axes, split_axis=0, concat_axis=0, tiled=True)  34.9 us
    all_to_all x4, waiting for transfers between devices, exchange(): return lax.all_to_all(x, axes, split_axis=0, concat_axis=0, tiled=True)  17.5 us
    pallas_call x1, Pallas kernels, body(): call(backward_kernel, [SM] * 3 + [VM] * 4 + [HB] * 4 + [AN] * 10, [jax.Sh...  13.2 us
    ppermute x4, starting transfers between devices, body(): lax.ppermute(piece, 'c', swap)  11.8 us
    pallas_call x1, Pallas kernels, body(): call(forward_kernel, [SM, SM, VM, VM, VM], [slots, jax.ShapeDtypeStruct((...  9.65 us
    pallas_call x1, Pallas kernels, body(): call(project_kernel, [SM] * 3 + [VM] + [AN] * 10, [jax.ShapeDtypeStruct(c...  5.08 us
    ppermute x1, waiting for transfers between devices, body(): lax.ppermute(line, 'x', behind)  3.98 us
  transfers between devices with their start and end apart: 13, of which 7 were waited for; matrix products, arithmetic and copies ran while one was open for 2% of the time, Pallas kernels for 9%

profile of v4, /device:TPU:1, one launch (start us, length us, event | category | flops | bytes accessed | tf_op | source)
XLA Modules:
  0.0 166.5 jit_solution(2111560496149751775)
XLA Ops:
  0.6 1.2 multiply_subtract_fusion
  1.9 0.0 copy-start.9
  1.9 0.7 copy-done.9
  2.6 0.9 broadcast_in_dim.8
  3.4 9.6 %all-to-all-start = ((bf16[16,24,768]{2,1,0:T(8,128)(2,1)}), bf16[16,24,768]{2,1,0:T(8,128)(2,1)S(1)}, u32[]{:S(2)}, u32[]{:S(2)}) async-start(bf16[16,24,768]{2,1,0:T(8,128)(2,1)} %broadcast_in_dim.8), calls=%async_computation | async-start | bytes 1179648 | tf_op jit(solution)/shard_map/all_to_all | solution.py:283
  13.0 0.6 broadcast_in_dim.9.gain_ref
  13.6 9.7 %forward.1 = (bf16[64,4,1536]{2,1,0:T(4,128)(2,1)}, f32[192,128]{1,0:T(8,128)}, f32[192,1536]{1,0:T(8,128)}, f32[192,1536]{1,0:T(8,128)}, bf16[2880,192]{1,0:T(8,128)(2,1)}) custom-call(s32[8]{0:T(128)} %bitcast.14, s32[48]{0:T(128)} %bitcast.15, bf16[192,1536]{1,0:T(8,128)(2,1)} %frames_hbm.1, f32[15,1536]{1,0:T(8,128)} %kernel_ref.3, ...), custom_call_target="tpu_custom_call" | custom-call | flops 6794772480 | bytes 4718592 | tf_op jit(solution)/shard_map/forward/pallas_call | solution.py:305
  23.3 4.8 %all-to-all-done = bf16[16,24,768]{2,1,0:T(8,128)(2,1)S(1)} async-done(((bf16[16,24,768]{2,1,0:T(8,128)(2,1)}), bf16[16,24,768]{2,1,0:T(8,128)(2,1)S(1)}, u32[]{:S(2)}, u32[]{:S(2)}) %all-to-all-start) | async-done | bytes 589856 | tf_op jit(solution)/shard_map/all_to_all | solution.py:283
  28.0 9.6 %all-to-all-start.1 = ((bf16[64,4,1536]{2,1,0:T(4,128)(2,1)}), bf16[64,4,1536]{2,1,0:T(4,128)(2,1)S(1)}, u32[]{:S(2)}, u32[]{:S(2)}) async-start(bf16[64,4,1536]{2,1,0:T(4,128)(2,1)} %get-tuple-element.19), calls=%async_computation.1 | async-start | bytes 1572864 | tf_op jit(solution)/shard_map/all_to_all | solution.py:283
  37.6 3.2 %collective-permute-start.2 = (bf16[384,768]{1,0:T(8,128)(2,1)S(1)}, bf16[384,768]{1,0:T(8,128)(2,1)S(1)}, u32[]{:S(2)}, u32[]{:S(2)}) collective-permute-start(bf16[384,768]{1,0:T(8,128)(2,1)S(1)} %bitcast.8), channel_id=1, source_target_pairs={{0,64},{64,0},{1,65},{65,1},{2,66},{66,2},{3,67},{67,3},{4,68},{68... | collective-permute-start | bytes 1769480 | tf_op jit(solution)/shard_map/ppermute | solution.py:331
  40.9 3.2 %collective-permute-start.1 = (bf16[384,768]{1,0:T(8,128)(2,1)S(1)}, bf16[384,768]{1,0:T(8,128)(2,1)S(1)}, u32[]{:S(2)}, u32[]{:S(2)}) collective-permute-start(bf16[384,768]{1,0:T(8,128)(2,1)S(1)} %bitcast.9), channel_id=1, source_target_pairs={{0,8},{8,16},{16,24},{24,0},{1,9},{9,17},{17,25},{25,1},{2,10},{10... | collective-permute-start | bytes 1769480 | tf_op jit(solution)/shard_map/ppermute | solution.py:330
  44.1 3.3 %collective-permute-start = (bf16[384,768]{1,0:T(8,128)(2,1)S(1)}, bf16[384,768]{1,0:T(8,128)(2,1)S(1)}, u32[]{:S(2)}, u32[]{:S(2)}) collective-permute-start(bf16[384,768]{1,0:T(8,128)(2,1)S(1)} %bitcast.10), channel_id=1, source_target_pairs={{8,0},{16,8},{24,16},{0,24},{9,1},{17,9},{25,17},{1,25},{10,2},{18... | collective-permute-start | bytes 1769480 | tf_op jit(solution)/shard_map/ppermute | solution.py:330
  47.4 11.8 %all-to-all-done.1.slots_ref = bf16[64,4,1536]{2,1,0:T(4,128)(2,1)S(1)} async-done(((bf16[64,4,1536]{2,1,0:T(4,128)(2,1)}), bf16[64,4,1536]{2,1,0:T(4,128)(2,1)S(1)}, u32[]{:S(2)}, u32[]{:S(2)}) %all-to-all-start.1) | async-done | bytes 786464 | tf_op jit(solution)/shard_map/all_to_all | solution.py:283
  59.2 1.8 %fusion.flags_ref = s32[64]{0:T(128)} fusion(bf16[64,4,1536]{2,1,0:T(4,128)(2,1)S(1)} %all-to-all-done.1.slots_ref), kind=kLoop, calls=%fused_computation.4 | loop fusion | flops 128 | bytes 384 | tf_op jit(solution)/shard_map/convert_element_type | solution.py:329
  60.9 0.0 collective-permute-done.2.q0
  60.9 4.0 %collective-permute-done.1.p4 = bf16[384,768]{1,0:T(8,128)(2,1)S(1)} collective-permute-done((bf16[384,768]{1,0:T(8,128)(2,1)S(1)}, bf16[384,768]{1,0:T(8,128)(2,1)S(1)}, u32[]{:S(2)}, u32[]{:S(2)}) %collective-permute-start.1) | collective-permute-done | bytes 589856 | tf_op jit(solution)/shard_map/ppermute | solution.py:330
  64.9 0.3 collective-permute-done.p1
  65.2 2.8 %scatter.1 = bf16[64,4,1536]{2,1,0:T(4,128)(2,1)} custom-call(s32[64]{0:T(128)} %fusion.flags_ref, bf16[128,1536]{1,0:T(8,128)(2,1)} %cot_ref.1), custom_call_target="tpu_custom_call" | custom-call | bytes 1179648 | tf_op jit(solution)/shard_map/scatter/pallas_call | solution.py:339
  68.1 9.5 %all-to-all-start.2 = ((bf16[64,4,1536]{2,1,0:T(4,128)(2,1)}), bf16[64,4,1536]{2,1,0:T(4,128)(2,1)S(1)}, u32[]{:S(2)}, u32[]{:S(2)}) async-start(bf16[64,4,1536]{2,1,0:T(4,128)(2,1)} %scatter.1), calls=%async_computation.2 | async-start | bytes 1572864 | tf_op jit(solution)/shard_map/all_to_all | solution.py:283
  77.6 2.9 %collective-permute-start.4 = (bf16[192,768]{1,0:T(8,128)(2,1)S(1)}, bf16[192,768]{1,0:T(8,128)(2,1)S(1)}, u32[]{:S(2)}, u32[]{:S(2)}) collective-permute-start(bf16[192,768]{1,0:T(8,128)(2,1)S(1)} %slice.21), channel_id=1, source_target_pairs={{0,8},{8,16},{16,24},{24,0},{1,9},{9,17},{17,25},{25,1},{2,10},{10... | collective-permute-start | bytes 884744 | tf_op jit(solution)/shard_map/ppermute | solution.py:335
  80.6 3.6 %collective-permute-start.3 = (bf16[192,768]{1,0:T(8,128)(2,1)S(1)}, bf16[192,768]{1,0:T(8,128)(2,1)}, u32[]{:S(2)}, u32[]{:S(2)}) collective-permute-start(bf16[192,768]{1,0:T(8,128)(2,1)S(1)} %slice.20), channel_id=1, source_target_pairs={{8,0},{16,8},{24,16},{0,24},{9,1},{17,9},{25,17},{1,25},{10,2},{18... | collective-permute-start | bytes 884744 | tf_op jit(solution)/shard_map/ppermute | solution.py:334
  84.2 3.6 %collective-permute-start.5 = (bf16[384,768]{1,0:T(8,128)(2,1)S(1)}, bf16[384,768]{1,0:T(8,128)(2,1)S(1)}, u32[]{:S(2)}, u32[]{:S(2)}) collective-permute-start(bf16[384,768]{1,0:T(8,128)(2,1)S(1)} %collective-permute-done.p1), channel_id=1, source_target_pairs={{0,64},{64,0},{1,65},{65,1},{2,66},{66,2},{3,67},{67,3},{4,68},{68... | collective-permute-start | bytes 1769480 | tf_op jit(solution)/shard_map/ppermute | solution.py:337
  87.8 1.9 %collective-permute-start.8 = (bf16[384,768]{1,0:T(8,128)(2,1)S(1)}, bf16[384,768]{1,0:T(8,128)(2,1)S(1)}, u32[]{:S(2)}, u32[]{:S(2)}) collective-permute-start(bf16[384,768]{1,0:T(8,128)(2,1)S(1)} %collective-permute-done.1.p4), channel_id=1, source_target_pairs={{0,64},{64,0},{1,65},{65,1},{2,66},{66,2},{3,67},{67,3},{4,68},{68... | collective-permute-start | bytes 1769480 | tf_op jit(solution)/shard_map/ppermute | solution.py:337
  89.7 3.0 %collective-permute-done.4.p3 = bf16[192,768]{1,0:T(8,128)(2,1)S(1)} collective-permute-done((bf16[192,768]{1,0:T(8,128)(2,1)S(1)}, bf16[192,768]{1,0:T(8,128)(2,1)S(1)}, u32[]{:S(2)}, u32[]{:S(2)}) %collective-permute-start.4) | collective-permute-done | bytes 294944 | tf_op jit(solution)/shard_map/ppermute | solution.py:335
  92.7 3.9 %collective-permute-start.7 = (bf16[192,768]{1,0:T(8,128)(2,1)S(1)}, bf16[192,768]{1,0:T(8,128)(2,1)}, u32[]{:S(2)}, u32[]{:S(2)}) collective-permute-start(bf16[192,768]{1,0:T(8,128)(2,1)S(1)} %collective-permute-done.4.p3), channel_id=1, source_target_pairs={{0,64},{64,0},{1,65},{65,1},{2,66},{66,2},{3,67},{67,3},{4,68},{68... | collective-permute-start | bytes 884744 | tf_op jit(solution)/shard_map/ppermute | solution.py:337
  96.7 0.0 collective-permute-done.3.p2
  96.7 2.3 %collective-permute-start.6 = (bf16[192,768]{1,0:T(8,128)(2,1)}, bf16[192,768]{1,0:T(8,128)(2,1)}, u32[]{:S(2)}, u32[]{:S(2)}) collective-permute-start(bf16[192,768]{1,0:T(8,128)(2,1)} %collective-permute-done.3.p2), channel_id=1, source_target_pairs={{0,64},{64,0},{1,65},{65,1},{2,66},{66,2},{3,67},{67,3},{4,68},{68... | collective-permute-start | bytes 884744 | tf_op jit(solution)/shard_map/ppermute | solution.py:337
  99.0 0.6 pad_add_fusion.place_ref
  99.7 0.0 collective-permute-done.7.q3
  99.7 0.9 collective-permute-done.6.q2
  100.5 0.0 collective-permute-done.5.q1
  100.5 0.0 collective-permute-done.8.q4
  100.6 0.0 all-to-all-done.2.slots_ref
  100.6 0.8 copy-done.6
  101.4 0.2 copy-done.7
  101.6 0.3 copy-done.4
  102.0 13.2 %backward.1 = (bf16[192,1536]{1,0:T(8,128)(2,1)}, f32[16,1,1536]{2,1,0:T(1,128)}) custom-call(s32[48]{0:T(128)} %bitcast.16, s32[2]{0:T(128)} %pad_add_fusion.place_ref, s32[64]{0:T(128)} %order_ref.3, f32[15,1536]{1,0:T(8,128)} %kernel_ref.3, f32[1,1536]{1,0:T(1,128)} %broadcast_in_dim.9.gain_ref, f32[192,128]{1,0:T(8,128)} %get-tuple-element.25.inv_ref, ...), custom_call_target="tpu_custom_call" | custom-call | flops 7700742144 | bytes 9437184 | tf_op jit(solution)/shard_map/backward/pallas_call | solution.py:344
  115.2 11.4 %all_to_all.30 = f32[16,1,1536]{2,1,0:T(1,128)S(1)} all-to-all(f32[16,1,1536]{2,1,0:T(1,128)} %get-tuple-element.30), channel_id=1, replica_groups=mesh['zh'=4,'c'=2,'zl'=2,'x'=4,'y'=8] {'c','zl','x'}, dimensions={0} | all-to-all | bytes 196608 | tf_op jit(solution)/shard_map/all_to_all | solution.py:283
  126.6 0.1 reduce_sum.18
  126.7 0.1 broadcast_in_dim.10
  126.8 25.3 %all_to_all.31 = f32[32,1,1536]{2,1,0:T(1,128)S(1)} all-to-all(f32[32,1,1536]{2,1,0:T(1,128)S(1)} %broadcast_in_dim.10), channel_id=1, replica_groups=mesh['zh'=4,'c'=2,'zl'=2,'x'=4,'y'=8] {'zh','y'}, dimensions={0} | all-to-all | bytes 393216 | tf_op jit(solution)/shard_map/all_to_all | solution.py:283
  152.1 0.1 reduce_sum.19
  152.3 0.7 broadcast_in_dim.11
  153.0 6.3 %all-to-all-start.5 = ((f32[16,1,1536]{2,1,0:T(1,128)}), f32[16,1,1536]{2,1,0:T(1,128)S(1)}, u32[]{:S(2)}, u32[]{:S(2)}) async-start(f32[16,1,1536]{2,1,0:T(1,128)} %broadcast_in_dim.11), calls=%async_computation.5 | async-start | bytes 196608 | tf_op jit(solution)/shard_map/all_to_all | solution.py:283
  159.2 5.1 %project.1 = bf16[128,1536]{1,0:T(8,128)(2,1)} custom-call(s32[64]{0:T(128)} %fusion.flags_ref, s32[2]{0:T(128)} %pad_add_fusion.place_ref, s32[64]{0:T(128)} %order_ref.3, bf16[64,4,1536]{2,1,0:T(4,128)(2,1)} %copy-done, bf16[384,768]{1,0:T(8,128)(2,1)} %bitcast.12, bf16[384,768]{1,0:T(8,128)(2,1)} %copy-done.3, ...), custom_call_target="tpu_custom_call" | custom-call | flops 603979776 | bytes 5505024 | tf_op jit(solution)/shard_map/project/pallas_call | solution.py:378
  164.3 0.9 all-to-all-done.5
  165.2 0.7 copy.20
  165.9 0.6 slice_reduce_fusion
  (22 shorter events, 0.1 us)
Async XLA Ops:
  0.6 12.4 %copy-start.10 = (f32[1536]{0:T(1024)S(1)}, f32[1536]{0:T(1024)}, u32[]{:S(2)}) copy-start(f32[1536]{0:T(1024)} %param.15) | copy-start | bytes 18436
  1.9 0.7 copy-start.9
  3.4 24.6 %all-to-all-start = ((bf16[16,24,768]{2,1,0:T(8,128)(2,1)}), bf16[16,24,768]{2,1,0:T(8,128)(2,1)S(1)}, u32[]{:S(2)}, u32[]{:S(2)}) async-start(bf16[16,24,768]{2,1,0:T(8,128)(2,1)} %broadcast_in_dim.8), calls=%async_computation | async-start | bytes 1179648 | tf_op jit(solution)/shard_map/all_to_all | solution.py:283
  28.0 40.1 %copy-start.1 = (bf16[16,24,768]{2,1,0:T(8,128)(2,1)}, bf16[16,24,768]{2,1,0:T(8,128)(2,1)S(1)}, u32[]{:S(2)}) copy-start(bf16[16,24,768]{2,1,0:T(8,128)(2,1)S(1)} %all-to-all-done) | copy-start | bytes 1769476
  28.0 31.1 %all-to-all-start.1 = ((bf16[64,4,1536]{2,1,0:T(4,128)(2,1)}), bf16[64,4,1536]{2,1,0:T(4,128)(2,1)S(1)}, u32[]{:S(2)}, u32[]{:S(2)}) async-start(bf16[64,4,1536]{2,1,0:T(4,128)(2,1)} %get-tuple-element.19), calls=%async_computation.1 | async-start | bytes 1572864 | tf_op jit(solution)/shard_map/all_to_all | solution.py:283
  37.6 23.3 %collective-permute-start.2 = (bf16[384,768]{1,0:T(8,128)(2,1)S(1)}, bf16[384,768]{1,0:T(8,128)(2,1)S(1)}, u32[]{:S(2)}, u32[]{:S(2)}) collective-permute-start(bf16[384,768]{1,0:T(8,128)(2,1)S(1)} %bitcast.8), channel_id=1, source_target_pairs={{0,64},{64,0},{1,65},{65,1},{2,66},{66,2},{3,67},{67,3},{4,68},{68... | collective-permute-start | bytes 1769480 | tf_op jit(solution)/shard_map/ppermute | solution.py:331
  40.9 24.0 %collective-permute-start.1 = (bf16[384,768]{1,0:T(8,128)(2,1)S(1)}, bf16[384,768]{1,0:T(8,128)(2,1)S(1)}, u32[]{:S(2)}, u32[]{:S(2)}) collective-permute-start(bf16[384,768]{1,0:T(8,128)(2,1)S(1)} %bitcast.9), channel_id=1, source_target_pairs={{0,8},{8,16},{16,24},{24,0},{1,9},{9,17},{17,25},{25,1},{2,10},{10... | collective-permute-start | bytes 1769480 | tf_op jit(solution)/shard_map/ppermute | solution.py:330
  44.1 21.1 %collective-permute-start = (bf16[384,768]{1,0:T(8,128)(2,1)S(1)}, bf16[384,768]{1,0:T(8,128)(2,1)S(1)}, u32[]{:S(2)}, u32[]{:S(2)}) collective-permute-start(bf16[384,768]{1,0:T(8,128)(2,1)S(1)} %bitcast.10), channel_id=1, source_target_pairs={{8,0},{16,8},{24,16},{0,24},{9,1},{17,9},{25,17},{1,25},{10,2},{18... | collective-permute-start | bytes 1769480 | tf_op jit(solution)/shard_map/ppermute | solution.py:330
  59.2 8.9 %copy-start = (bf16[64,4,1536]{2,1,0:T(4,128)(2,1)}, bf16[64,4,1536]{2,1,0:T(4,128)(2,1)S(1)}, u32[]{:S(2)}) copy-start(bf16[64,4,1536]{2,1,0:T(4,128)(2,1)S(1)} %all-to-all-done.1.slots_ref) | copy-start | bytes 2359300
  60.9 7.2 %copy-start.5 = (bf16[384,768]{1,0:T(8,128)(2,1)}, bf16[384,768]{1,0:T(8,128)(2,1)S(1)}, u32[]{:S(2)}) copy-start(bf16[384,768]{1,0:T(8,128)(2,1)S(1)} %collective-permute-done.2.q0) | copy-start | bytes 1769476
  64.9 22.9 %copy-start.2 = (bf16[384,768]{1,0:T(8,128)(2,1)}, bf16[384,768]{1,0:T(8,128)(2,1)S(1)}, u32[]{:S(2)}) copy-start(bf16[384,768]{1,0:T(8,128)(2,1)S(1)} %collective-permute-done.1.p4) | copy-start | bytes 1769476
  65.2 18.9 %copy-start.3 = (bf16[384,768]{1,0:T(8,128)(2,1)}, bf16[384,768]{1,0:T(8,128)(2,1)S(1)}, u32[]{:S(2)}) copy-start(bf16[384,768]{1,0:T(8,128)(2,1)S(1)} %collective-permute-done.p1) | copy-start | bytes 1769476
  68.1 32.5 %all-to-all-start.2 = ((bf16[64,4,1536]{2,1,0:T(4,128)(2,1)}), bf16[64,4,1536]{2,1,0:T(4,128)(2,1)S(1)}, u32[]{:S(2)}, u32[]{:S(2)}) async-start(bf16[64,4,1536]{2,1,0:T(4,128)(2,1)} %scatter.1), calls=%async_computation.2 | async-start | bytes 1572864 | tf_op jit(solution)/shard_map/all_to_all | solution.py:283
  77.6 15.1 %collective-permute-start.4 = (bf16[192,768]{1,0:T(8,128)(2,1)S(1)}, bf16[192,768]{1,0:T(8,128)(2,1)S(1)}, u32[]{:S(2)}, u32[]{:S(2)}) collective-permute-start(bf16[192,768]{1,0:T(8,128)(2,1)S(1)} %slice.21), channel_id=1, source_target_pairs={{0,8},{8,16},{16,24},{24,0},{1,9},{9,17},{17,25},{25,1},{2,10},{10... | collective-permute-start | bytes 884744 | tf_op jit(solution)/shard_map/ppermute | solution.py:335
  80.6 16.1 %collective-permute-start.3 = (bf16[192,768]{1,0:T(8,128)(2,1)S(1)}, bf16[192,768]{1,0:T(8,128)(2,1)}, u32[]{:S(2)}, u32[]{:S(2)}) collective-permute-start(bf16[192,768]{1,0:T(8,128)(2,1)S(1)} %slice.20), channel_id=1, source_target_pairs={{8,0},{16,8},{24,16},{0,24},{9,1},{17,9},{25,17},{1,25},{10,2},{18... | collective-permute-start | bytes 884744 | tf_op jit(solution)/shard_map/ppermute | solution.py:334
  84.2 16.4 %collective-permute-start.5 = (bf16[384,768]{1,0:T(8,128)(2,1)S(1)}, bf16[384,768]{1,0:T(8,128)(2,1)S(1)}, u32[]{:S(2)}, u32[]{:S(2)}) collective-permute-start(bf16[384,768]{1,0:T(8,128)(2,1)S(1)} %collective-permute-done.p1), channel_id=1, source_target_pairs={{0,64},{64,0},{1,65},{65,1},{2,66},{66,2},{3,67},{67,3},{4,68},{68... | collective-permute-start | bytes 1769480 | tf_op jit(solution)/shard_map/ppermute | solution.py:337
  87.8 12.8 %collective-permute-start.8 = (bf16[384,768]{1,0:T(8,128)(2,1)S(1)}, bf16[384,768]{1,0:T(8,128)(2,1)S(1)}, u32[]{:S(2)}, u32[]{:S(2)}) collective-permute-start(bf16[384,768]{1,0:T(8,128)(2,1)S(1)} %collective-permute-done.1.p4), channel_id=1, source_target_pairs={{0,64},{64,0},{1,65},{65,1},{2,66},{66,2},{3,67},{67,3},{4,68},{68... | collective-permute-start | bytes 1769480 | tf_op jit(solution)/shard_map/ppermute | solution.py:337
  92.7 7.9 %copy-start.8 = (bf16[192,768]{1,0:T(8,128)(2,1)}, bf16[192,768]{1,0:T(8,128)(2,1)S(1)}, u32[]{:S(2)}) copy-start(bf16[192,768]{1,0:T(8,128)(2,1)S(1)} %collective-permute-done.4.p3) | copy-start | bytes 884740
  92.7 7.0 %collective-permute-start.7 = (bf16[192,768]{1,0:T(8,128)(2,1)S(1)}, bf16[192,768]{1,0:T(8,128)(2,1)}, u32[]{:S(2)}, u32[]{:S(2)}) collective-permute-start(bf16[192,768]{1,0:T(8,128)(2,1)S(1)} %collective-permute-done.4.p3), channel_id=1, source_target_pairs={{0,64},{64,0},{1,65},{65,1},{2,66},{66,2},{3,67},{67,3},{4,68},{68... | collective-permute-start | bytes 884744 | tf_op jit(solution)/shard_map/ppermute | solution.py:337
  96.7 3.9 %collective-permute-start.6 = (bf16[192,768]{1,0:T(8,128)(2,1)}, bf16[192,768]{1,0:T(8,128)(2,1)}, u32[]{:S(2)}, u32[]{:S(2)}) collective-permute-start(bf16[192,768]{1,0:T(8,128)(2,1)} %collective-permute-done.3.p2), channel_id=1, source_target_pairs={{0,64},{64,0},{1,65},{65,1},{2,66},{66,2},{3,67},{67,3},{4,68},{68... | collective-permute-start | bytes 884744 | tf_op jit(solution)/shard_map/ppermute | solution.py:337
  100.5 0.9 copy-start.6
  100.6 1.1 copy-start.7
  100.6 1.4 copy-start.4
  153.0 12.3 %all-to-all-start.5 = ((f32[16,1,1536]{2,1,0:T(1,128)}), f32[16,1,1536]{2,1,0:T(1,128)S(1)}, u32[]{:S(2)}, u32[]{:S(2)}) async-start(f32[16,1,1536]{2,1,0:T(1,128)} %broadcast_in_dim.11), calls=%async_computation.5 | async-start | bytes 196608 | tf_op jit(solution)/shard_map/all_to_all | solution.py:283

commit v5 on v4

--- a/solution.py
+++ b/solution.py
@@ -130,18 +130,21 @@
 
 
 def load_weight(place_ref, pieces, weight_ref, sems):
+    count = len(pieces) // 2
     width = pieces[0].shape[1]
     core = place_ref[0]
-    copies, row = [], 0
-    for i, piece in enumerate(pieces):
-        start = core * width if i < len(pieces) // 2 else (1 - core) * width
-        row = row % weight_ref.shape[0]
-        target = weight_ref.at[pl.ds(row, piece.shape[0]), pl.ds(pl.multiple_of(start, 128), width)]
-        copies.append(pltpu.make_async_copy(piece, target, sems.at[i]))
-        row += piece.shape[0]
-    for copy in copies:
-        copy.start()
-    return copies
+    groups, row = [], 0
+    for i in range(count):
+        rows = pieces[i].shape[0]
+        copies = []
+        for h in range(2):
+            start = core * width if h == 0 else (1 - core) * width
+            target = weight_ref.at[pl.ds(row, rows), pl.ds(pl.multiple_of(start, 128), width)]
+            copies.append(pltpu.make_async_copy(pieces[h * count + i], target, sems.at[2 * i + h]))
+            copies[h].start()
+        groups.append((row, rows, copies))
+        row += rows
+    return groups
 
 
 def block_place(place_ref, owner, blocks):
@@ -162,9 +165,9 @@
     height, columns = frames_ref.shape
     blocks = order_ref.shape[0]
     size = columns // blocks
-    copies = load_weight(place_ref, (p0, p1, p2, p3, p4, q0, q1, q2, q3, q4), weight_ref, sems)
+    groups = load_weight(place_ref, (p0, p1, p2, p3, p4, q0, q1, q2, q3, q4), weight_ref, sems)
     saved = [(unit_hbm, unit_ref), (factor_hbm, factor_ref), (shift_hbm, shift_ref), (frames_hbm, frames_ref)]
-    late = [pltpu.make_async_copy(a, b, sems.at[len(copies) + i]) for i, (a, b) in enumerate(saved)]
+    late = [pltpu.make_async_copy(a, b, sems.at[2 * len(groups) + i]) for i, (a, b) in enumerate(saved)]
     for copy in late:
         copy.start()
     for b in range(height // BLK):
@@ -172,24 +175,19 @@
         rows = slots_ref[jnp.maximum(where, 0)].astype(F32)
         home_ref[b * BLK : (b + 1) * BLK, :] = jnp.where(where >= 0, rows, 0.0)
     homeb_ref[...] = home_ref[...].astype(BF16)
-    for copy in copies:
-        copy.wait()
-
-    def back(i, carry):
-        at = pl.ds(pl.multiple_of(i * 2 * CHUNK, CHUNK), 2 * CHUNK)
-        raw_ref[at, :] = lax.dot_general(
-            weight_ref[at, :], homeb_ref[...], (((1,), (1,)), ((), ())), preferred_element_type=F32
+    for row, rows, copies in groups:
+        for copy in copies:
+            copy.wait()
+        raw_ref[row : row + rows, :] = lax.dot_general(
+            weight_ref[row : row + rows, :], homeb_ref[...], (((1,), (1,)), ((), ())), preferred_element_type=F32
         )
-        return carry
-
-    lax.fori_loop(0, columns // (2 * CHUNK), back, 0)
     for b in range(blocks):
         at = pl.multiple_of(block_place(place_ref, order_ref[b], blocks) * size, 8)
         sorted_ref[b * size : (b + 1) * size, :] = raw_ref[pl.ds(at, size), :]
 
     def turn(i, carry):
         at = pl.ds(pl.multiple_of(i * CHUNK, CHUNK), CHUNK)
-        home_ref[:, at] = sorted_ref[at, :].T.astype(BF16).astype(F32)
+        home_ref[:, at] = sorted_ref[at, :].astype(BF16).T.astype(F32)
         return carry
 
     lax.fori_loop(0, columns // CHUNK, turn, 0)
@@ -246,7 +244,7 @@
 ):
     blocks = order_ref.shape[0]
     size = weight_ref.shape[0] // blocks
-    copies = load_weight(place_ref, (p0, p1, p2, p3, p4, q0, q1, q2, q3, q4), weight_ref, sems)
+    groups = load_weight(place_ref, (p0, p1, p2, p3, p4, q0, q1, q2, q3, q4), weight_ref, sems)
     find_senders(flags_ref, table_ref)
     for k in range(rows_ref.shape[0] // BLK):
         rows_ref[k * BLK : (k + 1) * BLK, :] = slots_ref[table_ref[k]].astype(F32)
@@ -255,8 +253,9 @@
         at = pl.multiple_of(block_place(place_ref, order_ref[b], blocks) * size, 8)
         turned_ref[pl.ds(at, size), :] = turned[b * size : (b + 1) * size, :]
     rows = turned_ref[...].T.astype(BF16)
-    for copy in copies:
-        copy.wait()
+    for _, _, copies in groups:
+        for copy in copies:
+            copy.wait()
     out_ref[...] = jnp.dot(rows, weight_ref[...], preferred_element_type=F32).astype(BF16)
 
 
@@ -329,17 +328,16 @@
     flags = (act_slots[:, 0, 0] > EMPTY / 2).astype(jnp.int32)
     next_x, last_x = lax.ppermute(line, "x", ahead), lax.ppermute(line, "x", behind)
     line_c = lax.ppermute(line, "c", swap)
-    flags, next_x, last_x, line_c = lax.optimization_barrier((flags, next_x, last_x, line_c))
+    (cot_sent,) = call(
+        scatter_kernel, [SM, VM], [slots], [pltpu.SMEM((owners,), jnp.int32)], 60, "scatter", 0, 6 * cotangent.size
+    )(flags, cotangent)
+    cot_sent, next_x, last_x, line_c = lax.optimization_barrier((cot_sent, next_x, last_x, line_c))
+    cot_slots = exchange(cot_sent, DP)
     part = line.shape[0] // 2
     far_low = lax.ppermute(next_x[:part], "x", ahead)
     far_high = lax.ppermute(last_x[part:], "x", behind)
     half_pieces = [line, next_x, far_low, far_high, last_x]
     pieces = half_pieces + [line_c] + [lax.ppermute(piece, "c", swap) for piece in half_pieces[1:]]
-
-    (cot_sent,) = call(
-        scatter_kernel, [SM, VM], [slots], [pltpu.SMEM((owners,), jnp.int32)], 60, "scatter", 0, 6 * cotangent.size
-    )(flags, cotangent)
-    cot_slots = exchange(cot_sent, DP)
 
     frame_grad, term = call(
         backward_kernel,

time: 167 us -> 165 us (0.988)
    ppermute x1, waiting for transfers between devices: 0.01 us -> 6.7 us  [body(): far_low = lax.ppermute(next_x[:part], 'x', ahead)]
    ppermute x1, waiting for transfers between devices: 3.98 us -> 0.57 us  [body(): lax.ppermute(line, 'x', behind)]
  transfers between devices with their start and end apart: 13 -> 13, of which waited for: 7 -> 7; matrix products, arithmetic and copies ran while one was open for 2% -> 2% of each run, Pallas kernels for 9% -> 11%
where the time goes in v5:
time: 165 us; the launch traced here: 164 us
  starting transfers between devices  61.3 us (37%)
  blocking collectives  35.3 us (21%)
  Pallas kernels  29.9 us (18%)
  waiting for transfers between devices  27 us (16%)
  local copies, waits for them, and re-layouts  5.45 us (3%)
  other arithmetic  3.83 us (2%)
    all_to_all x2, blocking collectives, exchange(): return lax.all_to_all(x, axes, split_axis=0, concat_axis=0, tiled=True)  35.3 us
    all_to_all x4, starting transfers between devices, exchange(): return lax.all_to_all(x, axes, split_axis=0, concat_axis=0, tiled=True)  33.6 us
    all_to_all x4, waiting for transfers between devices, exchange(): return lax.all_to_all(x, axes, split_axis=0, concat_axis=0, tiled=True)  17.3 us
    pallas_call x1, Pallas kernels, body(): call(backward_kernel, [SM] * 3 + [VM] * 4 + [HB] * 4 + [AN] * 10, [jax.Sh...  12.5 us
    ppermute x4, starting transfers between devices, body(): lax.ppermute(piece, 'c', swap)  11.5 us
    pallas_call x1, Pallas kernels, body(): call(forward_kernel, [SM, SM, VM, VM, VM], [slots, jax.ShapeDtypeStruct((...  9.65 us
    ppermute x1, waiting for transfers between devices, body(): far_low = lax.ppermute(next_x[:part], 'x', ahead)  6.7 us
    pallas_call x1, Pallas kernels, body(): call(project_kernel, [SM] * 3 + [VM] + [AN] * 10, [jax.ShapeDtypeStruct(c...  5.07 us
  transfers between devices with their start and end apart: 13, of which 7 were waited for; matrix products, arithmetic and copies ran while one was open for 2% of the time, Pallas kernels for 11%

profile of v5, /device:TPU:1, one launch (start us, length us, event | category | flops | bytes accessed | tf_op | source)
XLA Modules:
  0.0 163.7 jit_solution(17306365825040667029)
XLA Ops:
  0.6 1.2 multiply_subtract_fusion
  1.9 0.0 copy-start.9
  1.9 0.7 copy-done.9
  2.6 0.9 broadcast_in_dim.8
  3.4 9.6 %all-to-all-start = ((bf16[16,24,768]{2,1,0:T(8,128)(2,1)}), bf16[16,24,768]{2,1,0:T(8,128)(2,1)S(1)}, u32[]{:S(2)}, u32[]{:S(2)}) async-start(bf16[16,24,768]{2,1,0:T(8,128)(2,1)} %broadcast_in_dim.8), calls=%async_computation | async-start | bytes 1179648 | tf_op jit(solution)/shard_map/all_to_all | solution.py:282
  13.0 0.6 broadcast_in_dim.9.gain_ref
  13.6 9.7 %forward.1 = (bf16[64,4,1536]{2,1,0:T(4,128)(2,1)}, f32[192,128]{1,0:T(8,128)}, f32[192,1536]{1,0:T(8,128)}, f32[192,1536]{1,0:T(8,128)}, bf16[2880,192]{1,0:T(8,128)(2,1)}) custom-call(s32[8]{0:T(128)} %bitcast.14, s32[48]{0:T(128)} %bitcast.15, bf16[192,1536]{1,0:T(8,128)(2,1)} %frames_hbm.1, f32[15,1536]{1,0:T(8,128)} %kernel_ref.3, ...), custom_call_target="tpu_custom_call" | custom-call | flops 6794772480 | bytes 4718592 | tf_op jit(solution)/shard_map/forward/pallas_call | solution.py:304
  23.3 4.8 %all-to-all-done = bf16[16,24,768]{2,1,0:T(8,128)(2,1)S(1)} async-done(((bf16[16,24,768]{2,1,0:T(8,128)(2,1)}), bf16[16,24,768]{2,1,0:T(8,128)(2,1)S(1)}, u32[]{:S(2)}, u32[]{:S(2)}) %all-to-all-start) | async-done | bytes 589856 | tf_op jit(solution)/shard_map/all_to_all | solution.py:282
  28.0 9.6 %all-to-all-start.1 = ((bf16[64,4,1536]{2,1,0:T(4,128)(2,1)}), bf16[64,4,1536]{2,1,0:T(4,128)(2,1)S(1)}, u32[]{:S(2)}, u32[]{:S(2)}) async-start(bf16[64,4,1536]{2,1,0:T(4,128)(2,1)} %get-tuple-element.19), calls=%async_computation.1 | async-start | bytes 1572864 | tf_op jit(solution)/shard_map/all_to_all | solution.py:282
  37.6 4.2 %collective-permute-start = (bf16[384,768]{1,0:T(8,128)(2,1)S(1)}, bf16[384,768]{1,0:T(8,128)(2,1)S(1)}, u32[]{:S(2)}, u32[]{:S(2)}) collective-permute-start(bf16[384,768]{1,0:T(8,128)(2,1)S(1)} %bitcast.8), channel_id=1, source_target_pairs={{8,0},{16,8},{24,16},{0,24},{9,1},{17,9},{25,17},{1,25},{10,2},{18... | collective-permute-start | bytes 1769480 | tf_op jit(solution)/shard_map/ppermute | solution.py:329
  41.8 1.9 %collective-permute-start.1 = (bf16[384,768]{1,0:T(8,128)(2,1)S(1)}, bf16[384,768]{1,0:T(8,128)(2,1)S(1)}, u32[]{:S(2)}, u32[]{:S(2)}) collective-permute-start(bf16[384,768]{1,0:T(8,128)(2,1)S(1)} %bitcast.9), channel_id=1, source_target_pairs={{0,8},{8,16},{16,24},{24,0},{1,9},{9,17},{17,25},{25,1},{2,10},{10... | collective-permute-start | bytes 1769480 | tf_op jit(solution)/shard_map/ppermute | solution.py:329
  43.8 3.8 %collective-permute-start.2 = (bf16[384,768]{1,0:T(8,128)(2,1)S(1)}, bf16[384,768]{1,0:T(8,128)(2,1)S(1)}, u32[]{:S(2)}, u32[]{:S(2)}) collective-permute-start(bf16[384,768]{1,0:T(8,128)(2,1)S(1)} %bitcast.10), channel_id=1, source_target_pairs={{0,64},{64,0},{1,65},{65,1},{2,66},{66,2},{3,67},{67,3},{4,68},{68... | collective-permute-start | bytes 1769480 | tf_op jit(solution)/shard_map/ppermute | solution.py:330
  47.6 11.6 %all-to-all-done.1.slots_ref = bf16[64,4,1536]{2,1,0:T(4,128)(2,1)S(1)} async-done(((bf16[64,4,1536]{2,1,0:T(4,128)(2,1)}), bf16[64,4,1536]{2,1,0:T(4,128)(2,1)S(1)}, u32[]{:S(2)}, u32[]{:S(2)}) %all-to-all-start.1) | async-done | bytes 786464 | tf_op jit(solution)/shard_map/all_to_all | solution.py:282
  59.2 1.8 %fusion.flags_ref = s32[64]{0:T(128)} fusion(bf16[64,4,1536]{2,1,0:T(4,128)(2,1)S(1)} %all-to-all-done.1.slots_ref), kind=kLoop, calls=%fused_computation.4 | loop fusion | flops 128 | bytes 384 | tf_op jit(solution)/shard_map/convert_element_type | solution.py:328
  60.9 2.6 %scatter.1 = bf16[64,4,1536]{2,1,0:T(4,128)(2,1)} custom-call(s32[64]{0:T(128)} %fusion.flags_ref, bf16[128,1536]{1,0:T(8,128)(2,1)} %cot_ref.1), custom_call_target="tpu_custom_call" | custom-call | bytes 1179648 | tf_op jit(solution)/shard_map/scatter/pallas_call | solution.py:331
  63.5 0.0 collective-permute-done.p1
  63.6 0.6 collective-permute-done.1.p4
  64.1 0.0 collective-permute-done.2.q0
  64.1 8.2 %all-to-all-start.2 = ((bf16[64,4,1536]{2,1,0:T(4,128)(2,1)}), bf16[64,4,1536]{2,1,0:T(4,128)(2,1)S(1)}, u32[]{:S(2)}, u32[]{:S(2)}) async-start(bf16[64,4,1536]{2,1,0:T(4,128)(2,1)} %scatter.1), calls=%async_computation.2 | async-start | bytes 1572864 | tf_op jit(solution)/shard_map/all_to_all | solution.py:282
  72.3 3.8 %collective-permute-start.5 = (bf16[384,768]{1,0:T(8,128)(2,1)S(1)}, bf16[384,768]{1,0:T(8,128)(2,1)S(1)}, u32[]{:S(2)}, u32[]{:S(2)}) collective-permute-start(bf16[384,768]{1,0:T(8,128)(2,1)S(1)} %collective-permute-done.p1), channel_id=1, source_target_pairs={{0,64},{64,0},{1,65},{65,1},{2,66},{66,2},{3,67},{67,3},{4,68},{68... | collective-permute-start | bytes 1769480 | tf_op jit(solution)/shard_map/ppermute | solution.py:340
  76.1 4.5 %collective-permute-start.3 = (bf16[192,768]{1,0:T(8,128)(2,1)S(1)}, bf16[192,768]{1,0:T(8,128)(2,1)}, u32[]{:S(2)}, u32[]{:S(2)}) collective-permute-start(bf16[192,768]{1,0:T(8,128)(2,1)S(1)} %slice.20), channel_id=1, source_target_pairs={{8,0},{16,8},{24,16},{0,24},{9,1},{17,9},{25,17},{1,25},{10,2},{18... | collective-permute-start | bytes 884744 | tf_op jit(solution)/shard_map/ppermute | solution.py:337
  80.6 1.9 %collective-permute-start.4 = (bf16[192,768]{1,0:T(8,128)(2,1)S(1)}, bf16[192,768]{1,0:T(8,128)(2,1)}, u32[]{:S(2)}, u32[]{:S(2)}) collective-permute-start(bf16[192,768]{1,0:T(8,128)(2,1)S(1)} %slice.21), channel_id=1, source_target_pairs={{0,8},{8,16},{16,24},{24,0},{1,9},{9,17},{17,25},{25,1},{2,10},{10... | collective-permute-start | bytes 884744 | tf_op jit(solution)/shard_map/ppermute | solution.py:338
  82.6 2.2 %collective-permute-start.8 = (bf16[384,768]{1,0:T(8,128)(2,1)S(1)}, bf16[384,768]{1,0:T(8,128)(2,1)S(1)}, u32[]{:S(2)}, u32[]{:S(2)}) collective-permute-start(bf16[384,768]{1,0:T(8,128)(2,1)S(1)} %collective-permute-done.1.p4), channel_id=1, source_target_pairs={{0,64},{64,0},{1,65},{65,1},{2,66},{66,2},{3,67},{67,3},{4,68},{68... | collective-permute-start | bytes 1769480 | tf_op jit(solution)/shard_map/ppermute | solution.py:340
  84.8 6.7 %collective-permute-done.3.p2 = bf16[192,768]{1,0:T(8,128)(2,1)} collective-permute-done((bf16[192,768]{1,0:T(8,128)(2,1)S(1)}, bf16[192,768]{1,0:T(8,128)(2,1)}, u32[]{:S(2)}, u32[]{:S(2)}) %collective-permute-start.3) | collective-permute-done | bytes 294944 | tf_op jit(solution)/shard_map/ppermute | solution.py:337
  91.5 2.8 %collective-permute-start.6 = (bf16[192,768]{1,0:T(8,128)(2,1)}, bf16[192,768]{1,0:T(8,128)(2,1)S(1)}, u32[]{:S(2)}, u32[]{:S(2)}) collective-permute-start(bf16[192,768]{1,0:T(8,128)(2,1)} %collective-permute-done.3.p2), channel_id=1, source_target_pairs={{0,64},{64,0},{1,65},{65,1},{2,66},{66,2},{3,67},{67,3},{4,68},{68... | collective-permute-start | bytes 884744 | tf_op jit(solution)/shard_map/ppermute | solution.py:340
  94.3 1.6 collective-permute-done.4.p3
  95.9 2.7 %collective-permute-start.7 = (bf16[192,768]{1,0:T(8,128)(2,1)}, bf16[192,768]{1,0:T(8,128)(2,1)}, u32[]{:S(2)}, u32[]{:S(2)}) collective-permute-start(bf16[192,768]{1,0:T(8,128)(2,1)} %collective-permute-done.4.p3), channel_id=1, source_target_pairs={{0,64},{64,0},{1,65},{65,1},{2,66},{66,2},{3,67},{67,3},{4,68},{68... | collective-permute-start | bytes 884744 | tf_op jit(solution)/shard_map/ppermute | solution.py:340
  98.6 0.6 pad_add_fusion.place_ref
  99.2 0.0 collective-permute-done.5.q1
  99.2 0.0 collective-permute-done.6.q2
  99.2 0.9 collective-permute-done.7.q3
  100.1 0.0 collective-permute-done.8.q4
  100.1 0.0 all-to-all-done.2.slots_ref
  100.1 0.1 copy-done.8
  100.2 0.8 copy-done.7
  101.0 0.3 copy-done.4
  101.3 12.5 %backward.1 = (bf16[192,1536]{1,0:T(8,128)(2,1)}, f32[16,1,1536]{2,1,0:T(1,128)}) custom-call(s32[48]{0:T(128)} %bitcast.16, s32[2]{0:T(128)} %pad_add_fusion.place_ref, s32[64]{0:T(128)} %order_ref.3, f32[15,1536]{1,0:T(8,128)} %kernel_ref.3, f32[1,1536]{1,0:T(1,128)} %broadcast_in_dim.9.gain_ref, f32[192,128]{1,0:T(8,128)} %get-tuple-element.24.inv_ref, ...), custom_call_target="tpu_custom_call" | custom-call | flops 7700742144 | bytes 9437184 | tf_op jit(solution)/shard_map/backward/pallas_call | solution.py:342
  113.8 9.7 %all_to_all.30 = f32[16,1,1536]{2,1,0:T(1,128)S(1)} all-to-all(f32[16,1,1536]{2,1,0:T(1,128)} %get-tuple-element.30), channel_id=1, replica_groups=mesh['zh'=4,'c'=2,'zl'=2,'x'=4,'y'=8] {'c','zl','x'}, dimensions={0} | all-to-all | bytes 196608 | tf_op jit(solution)/shard_map/all_to_all | solution.py:282
  123.5 0.1 reduce_sum.18
  123.6 0.1 broadcast_in_dim.10
  123.7 25.6 %all_to_all.31 = f32[32,1,1536]{2,1,0:T(1,128)S(1)} all-to-all(f32[32,1,1536]{2,1,0:T(1,128)S(1)} %broadcast_in_dim.10), channel_id=1, replica_groups=mesh['zh'=4,'c'=2,'zl'=2,'x'=4,'y'=8] {'zh','y'}, dimensions={0} | all-to-all | bytes 393216 | tf_op jit(solution)/shard_map/all_to_all | solution.py:282
  149.3 0.1 reduce_sum.19
  149.4 0.7 broadcast_in_dim.11
  150.1 6.3 %all-to-all-start.5 = ((f32[16,1,1536]{2,1,0:T(1,128)}), f32[16,1,1536]{2,1,0:T(1,128)S(1)}, u32[]{:S(2)}, u32[]{:S(2)}) async-start(f32[16,1,1536]{2,1,0:T(1,128)} %broadcast_in_dim.11), calls=%async_computation.5 | async-start | bytes 196608 | tf_op jit(solution)/shard_map/all_to_all | solution.py:282
  156.4 5.1 %project.1 = bf16[128,1536]{1,0:T(8,128)(2,1)} custom-call(s32[64]{0:T(128)} %fusion.flags_ref, s32[2]{0:T(128)} %pad_add_fusion.place_ref, s32[64]{0:T(128)} %order_ref.3, bf16[64,4,1536]{2,1,0:T(4,128)(2,1)} %copy-done, bf16[384,768]{1,0:T(8,128)(2,1)} %bitcast.12, bf16[384,768]{1,0:T(8,128)(2,1)} %copy-done.2, ...), custom_call_target="tpu_custom_call" | custom-call | flops 603979776 | bytes 5505024 | tf_op jit(solution)/shard_map/project/pallas_call | solution.py:376
  161.5 0.9 all-to-all-done.5
  162.4 0.7 copy.20
  163.1 0.6 slice_reduce_fusion
  (22 shorter events, 0.1 us)
Async XLA Ops:
  0.6 12.4 %copy-start.10 = (f32[1536]{0:T(1024)S(1)}, f32[1536]{0:T(1024)}, u32[]{:S(2)}) copy-start(f32[1536]{0:T(1024)} %param.15) | copy-start | bytes 18436
  1.9 0.7 copy-start.9
  3.4 24.6 %all-to-all-start = ((bf16[16,24,768]{2,1,0:T(8,128)(2,1)}), bf16[16,24,768]{2,1,0:T(8,128)(2,1)S(1)}, u32[]{:S(2)}, u32[]{:S(2)}) async-start(bf16[16,24,768]{2,1,0:T(8,128)(2,1)} %broadcast_in_dim.8), calls=%async_computation | async-start | bytes 1179648 | tf_op jit(solution)/shard_map/all_to_all | solution.py:282
  28.0 35.5 %copy-start.1 = (bf16[16,24,768]{2,1,0:T(8,128)(2,1)}, bf16[16,24,768]{2,1,0:T(8,128)(2,1)S(1)}, u32[]{:S(2)}) copy-start(bf16[16,24,768]{2,1,0:T(8,128)(2,1)S(1)} %all-to-all-done) | copy-start | bytes 1769476
  28.0 31.1 %all-to-all-start.1 = ((bf16[64,4,1536]{2,1,0:T(4,128)(2,1)}), bf16[64,4,1536]{2,1,0:T(4,128)(2,1)S(1)}, u32[]{:S(2)}, u32[]{:S(2)}) async-start(bf16[64,4,1536]{2,1,0:T(4,128)(2,1)} %get-tuple-element.19), calls=%async_computation.1 | async-start | bytes 1572864 | tf_op jit(solution)/shard_map/all_to_all | solution.py:282
  37.6 25.9 %collective-permute-start = (bf16[384,768]{1,0:T(8,128)(2,1)S(1)}, bf16[384,768]{1,0:T(8,128)(2,1)S(1)}, u32[]{:S(2)}, u32[]{:S(2)}) collective-permute-start(bf16[384,768]{1,0:T(8,128)(2,1)S(1)} %bitcast.8), channel_id=1, source_target_pairs={{8,0},{16,8},{24,16},{0,24},{9,1},{17,9},{25,17},{1,25},{10,2},{18... | collective-permute-start | bytes 1769480 | tf_op jit(solution)/shard_map/ppermute | solution.py:329
  41.8 22.3 %collective-permute-start.1 = (bf16[384,768]{1,0:T(8,128)(2,1)S(1)}, bf16[384,768]{1,0:T(8,128)(2,1)S(1)}, u32[]{:S(2)}, u32[]{:S(2)}) collective-permute-start(bf16[384,768]{1,0:T(8,128)(2,1)S(1)} %bitcast.9), channel_id=1, source_target_pairs={{0,8},{8,16},{16,24},{24,0},{1,9},{9,17},{17,25},{25,1},{2,10},{10... | collective-permute-start | bytes 1769480 | tf_op jit(solution)/shard_map/ppermute | solution.py:329
  43.8 20.4 %collective-permute-start.2 = (bf16[384,768]{1,0:T(8,128)(2,1)S(1)}, bf16[384,768]{1,0:T(8,128)(2,1)S(1)}, u32[]{:S(2)}, u32[]{:S(2)}) collective-permute-start(bf16[384,768]{1,0:T(8,128)(2,1)S(1)} %bitcast.10), channel_id=1, source_target_pairs={{0,64},{64,0},{1,65},{65,1},{2,66},{66,2},{3,67},{67,3},{4,68},{68... | collective-permute-start | bytes 1769480 | tf_op jit(solution)/shard_map/ppermute | solution.py:330
  59.2 5.0 %copy-start = (bf16[64,4,1536]{2,1,0:T(4,128)(2,1)}, bf16[64,4,1536]{2,1,0:T(4,128)(2,1)S(1)}, u32[]{:S(2)}) copy-start(bf16[64,4,1536]{2,1,0:T(4,128)(2,1)S(1)} %all-to-all-done.1.slots_ref) | copy-start | bytes 2359300
  63.5 17.0 %copy-start.2 = (bf16[384,768]{1,0:T(8,128)(2,1)}, bf16[384,768]{1,0:T(8,128)(2,1)S(1)}, u32[]{:S(2)}) copy-start(bf16[384,768]{1,0:T(8,128)(2,1)S(1)} %collective-permute-done.p1) | copy-start | bytes 1769476
  64.1 18.4 %copy-start.3 = (bf16[384,768]{1,0:T(8,128)(2,1)}, bf16[384,768]{1,0:T(8,128)(2,1)S(1)}, u32[]{:S(2)}) copy-start(bf16[384,768]{1,0:T(8,128)(2,1)S(1)} %collective-permute-done.1.p4) | copy-start | bytes 1769476
  64.1 16.5 %copy-start.5 = (bf16[384,768]{1,0:T(8,128)(2,1)}, bf16[384,768]{1,0:T(8,128)(2,1)S(1)}, u32[]{:S(2)}) copy-start(bf16[384,768]{1,0:T(8,128)(2,1)S(1)} %collective-permute-done.2.q0) | copy-start | bytes 1769476
  64.1 36.0 %all-to-all-start.2 = ((bf16[64,4,1536]{2,1,0:T(4,128)(2,1)}), bf16[64,4,1536]{2,1,0:T(4,128)(2,1)S(1)}, u32[]{:S(2)}, u32[]{:S(2)}) async-start(bf16[64,4,1536]{2,1,0:T(4,128)(2,1)} %scatter.1), calls=%async_computation.2 | async-start | bytes 1572864 | tf_op jit(solution)/shard_map/all_to_all | solution.py:282
  72.3 26.9 %collective-permute-start.5 = (bf16[384,768]{1,0:T(8,128)(2,1)S(1)}, bf16[384,768]{1,0:T(8,128)(2,1)S(1)}, u32[]{:S(2)}, u32[]{:S(2)}) collective-permute-start(bf16[384,768]{1,0:T(8,128)(2,1)S(1)} %collective-permute-done.p1), channel_id=1, source_target_pairs={{0,64},{64,0},{1,65},{65,1},{2,66},{66,2},{3,67},{67,3},{4,68},{68... | collective-permute-start | bytes 1769480 | tf_op jit(solution)/shard_map/ppermute | solution.py:340
  76.1 15.4 %collective-permute-start.3 = (bf16[192,768]{1,0:T(8,128)(2,1)S(1)}, bf16[192,768]{1,0:T(8,128)(2,1)}, u32[]{:S(2)}, u32[]{:S(2)}) collective-permute-start(bf16[192,768]{1,0:T(8,128)(2,1)S(1)} %slice.20), channel_id=1, source_target_pairs={{8,0},{16,8},{24,16},{0,24},{9,1},{17,9},{25,17},{1,25},{10,2},{18... | collective-permute-start | bytes 884744 | tf_op jit(solution)/shard_map/ppermute | solution.py:337
  80.6 15.3 %collective-permute-start.4 = (bf16[192,768]{1,0:T(8,128)(2,1)S(1)}, bf16[192,768]{1,0:T(8,128)(2,1)}, u32[]{:S(2)}, u32[]{:S(2)}) collective-permute-start(bf16[192,768]{1,0:T(8,128)(2,1)S(1)} %slice.21), channel_id=1, source_target_pairs={{0,8},{8,16},{16,24},{24,0},{1,9},{9,17},{17,25},{25,1},{2,10},{10... | collective-permute-start | bytes 884744 | tf_op jit(solution)/shard_map/ppermute | solution.py:338
  82.6 17.5 %collective-permute-start.8 = (bf16[384,768]{1,0:T(8,128)(2,1)S(1)}, bf16[384,768]{1,0:T(8,128)(2,1)S(1)}, u32[]{:S(2)}, u32[]{:S(2)}) collective-permute-start(bf16[384,768]{1,0:T(8,128)(2,1)S(1)} %collective-permute-done.1.p4), channel_id=1, source_target_pairs={{0,64},{64,0},{1,65},{65,1},{2,66},{66,2},{3,67},{67,3},{4,68},{68... | collective-permute-start | bytes 1769480 | tf_op jit(solution)/shard_map/ppermute | solution.py:340
  91.5 7.7 %collective-permute-start.6 = (bf16[192,768]{1,0:T(8,128)(2,1)}, bf16[192,768]{1,0:T(8,128)(2,1)S(1)}, u32[]{:S(2)}, u32[]{:S(2)}) collective-permute-start(bf16[192,768]{1,0:T(8,128)(2,1)} %collective-permute-done.3.p2), channel_id=1, source_target_pairs={{0,64},{64,0},{1,65},{65,1},{2,66},{66,2},{3,67},{67,3},{4,68},{68... | collective-permute-start | bytes 884744 | tf_op jit(solution)/shard_map/ppermute | solution.py:340
  95.9 4.2 %collective-permute-start.7 = (bf16[192,768]{1,0:T(8,128)(2,1)}, bf16[192,768]{1,0:T(8,128)(2,1)}, u32[]{:S(2)}, u32[]{:S(2)}) collective-permute-start(bf16[192,768]{1,0:T(8,128)(2,1)} %collective-permute-done.4.p3), channel_id=1, source_target_pairs={{0,64},{64,0},{1,65},{65,1},{2,66},{66,2},{3,67},{67,3},{4,68},{68... | collective-permute-start | bytes 884744 | tf_op jit(solution)/shard_map/ppermute | solution.py:340
  99.2 0.9 copy-start.6
  99.2 0.9 copy-start.8
  100.1 0.9 copy-start.7
  100.1 1.2 copy-start.4
  150.1 12.3 %all-to-all-start.5 = ((f32[16,1,1536]{2,1,0:T(1,128)}), f32[16,1,1536]{2,1,0:T(1,128)S(1)}, u32[]{:S(2)}, u32[]{:S(2)}) async-start(f32[16,1,1536]{2,1,0:T(1,128)} %broadcast_in_dim.11), calls=%async_computation.5 | async-start | bytes 196608 | tf_op jit(solution)/shard_map/all_to_all | solution.py:282

commit v6 on v5

--- a/solution.py
+++ b/solution.py
@@ -331,11 +331,13 @@
     (cot_sent,) = call(
         scatter_kernel, [SM, VM], [slots], [pltpu.SMEM((owners,), jnp.int32)], 60, "scatter", 0, 6 * cotangent.size
     )(flags, cotangent)
-    cot_sent, next_x, last_x, line_c = lax.optimization_barrier((cot_sent, next_x, last_x, line_c))
-    cot_slots = exchange(cot_sent, DP)
     part = line.shape[0] // 2
     far_low = lax.ppermute(next_x[:part], "x", ahead)
     far_high = lax.ppermute(last_x[part:], "x", behind)
+    cot_sent, next_x, last_x, line_c, far_low, far_high = lax.optimization_barrier(
+        (cot_sent, next_x, last_x, line_c, far_low, far_high)
+    )
+    cot_slots = exchange(cot_sent, DP)
     half_pieces = [line, next_x, far_low, far_high, last_x]
     pieces = half_pieces + [line_c] + [lax.ppermute(piece, "c", swap) for piece in half_pieces[1:]]
 

time: 165 us -> 170 us (1.030)
  waiting for transfers between devices: 27 us -> 31.7 us
  blocking collectives: 35.3 us -> 37.1 us
    ppermute x1, waiting for transfers between devices: 0.01 us -> 14.3 us  [body(): lax.ppermute(line, 'x', ahead)]
    ppermute x1, waiting for transfers between devices: 6.7 us -> 0.01 us  [body(): far_low = lax.ppermute(next_x[:part], 'x', ahead)]
    all_to_all x4, waiting for transfers between devices: 17.3 us -> 12.7 us  [exchange(): return lax.all_to_all(x, axes, split_axis=0, concat_axis=0, tiled=True)]
    ppermute x1, waiting for transfers between devices: 1.59 us -> 3.4 us  [body(): far_high = lax.ppermute(last_x[part:], 'x', behind)]
    all_to_all x2, blocking collectives: 35.3 us -> 37.1 us  [exchange(): return lax.all_to_all(x, axes, split_axis=0, concat_axis=0, tiled=True)]
  transfers between devices with their start and end apart: 13 -> 13, of which waited for: 7 -> 6; matrix products, arithmetic and copies ran while one was open for 2% -> 3% of each run, Pallas kernels for 11% -> 10%
where the time goes in v6:
time: 170 us; the launch traced here: 169 us
  starting transfers between devices  59.9 us (35%)
  blocking collectives  37.1 us (22%)
  waiting for transfers between devices  31.7 us (19%)
  Pallas kernels  29.9 us (18%)
  local copies, waits for them, and re-layouts  6.05 us (4%)
  other arithmetic  3.77 us (2%)
    all_to_all x2, blocking collectives, exchange(): return lax.all_to_all(x, axes, split_axis=0, concat_axis=0, tiled=True)  37.1 us
    all_to_all x4, starting transfers between devices, exchange(): return lax.all_to_all(x, axes, split_axis=0, concat_axis=0, tiled=True)  33.4 us
    ppermute x1, waiting for transfers between devices, body(): lax.ppermute(line, 'x', ahead)  14.3 us
    all_to_all x4, waiting for transfers between devices, exchange(): return lax.all_to_all(x, axes, split_axis=0, concat_axis=0, tiled=True)  12.7 us
    pallas_call x1, Pallas kernels, body(): call(backward_kernel, [SM] * 3 + [VM] * 4 + [HB] * 4 + [AN] * 10, [jax.Sh...  12.5 us
    ppermute x4, starting transfers between devices, body(): lax.ppermute(piece, 'c', swap)  11.1 us
    pallas_call x1, Pallas kernels, body(): call(forward_kernel, [SM, SM, VM, VM, VM], [slots, jax.ShapeDtypeStruct((...  9.66 us
    pallas_call x1, Pallas kernels, body(): call(project_kernel, [SM] * 3 + [VM] + [AN] * 10, [jax.ShapeDtypeStruct(c...  5.07 us
  transfers between devices with their start and end apart: 13, of which 6 were waited for; matrix products, arithmetic and copies ran while one was open for 3% of the time, Pallas kernels for 10%

profile of v6, /device:TPU:1, one launch (start us, length us, event | category | flops | bytes accessed | tf_op | source)
XLA Modules:
  0.0 169.2 jit_solution(10126750607804163216)
XLA Ops:
  0.6 1.2 multiply_subtract_fusion
  1.9 0.0 copy-start.7
  1.9 0.9 broadcast_in_dim.8
  2.8 9.6 %all-to-all-start = ((bf16[16,24,768]{2,1,0:T(8,128)(2,1)}), bf16[16,24,768]{2,1,0:T(8,128)(2,1)S(1)}, u32[]{:S(2)}, u32[]{:S(2)}) async-start(bf16[16,24,768]{2,1,0:T(8,128)(2,1)} %broadcast_in_dim.8), calls=%async_computation | async-start | bytes 1179648 | tf_op jit(solution)/shard_map/all_to_all | solution.py:282
  12.4 0.6 broadcast_in_dim.9.gain_ref
  13.0 9.7 %forward.1 = (bf16[64,4,1536]{2,1,0:T(4,128)(2,1)}, f32[192,128]{1,0:T(8,128)}, f32[192,1536]{1,0:T(8,128)}, f32[192,1536]{1,0:T(8,128)}, bf16[2880,192]{1,0:T(8,128)(2,1)}) custom-call(s32[8]{0:T(128)} %bitcast.14, s32[48]{0:T(128)} %bitcast.15, bf16[192,1536]{1,0:T(8,128)(2,1)} %frames_hbm.1, f32[15,1536]{1,0:T(8,128)} %kernel_ref.3, ...), custom_call_target="tpu_custom_call" | custom-call | flops 6794772480 | bytes 4718592 | tf_op jit(solution)/shard_map/forward/pallas_call | solution.py:304
  22.6 4.8 %all-to-all-done = bf16[16,24,768]{2,1,0:T(8,128)(2,1)S(1)} async-done(((bf16[16,24,768]{2,1,0:T(8,128)(2,1)}), bf16[16,24,768]{2,1,0:T(8,128)(2,1)S(1)}, u32[]{:S(2)}, u32[]{:S(2)}) %all-to-all-start) | async-done | bytes 589856 | tf_op jit(solution)/shard_map/all_to_all | solution.py:282
  27.4 9.6 %all-to-all-start.1 = ((bf16[64,4,1536]{2,1,0:T(4,128)(2,1)}), bf16[64,4,1536]{2,1,0:T(4,128)(2,1)S(1)}, u32[]{:S(2)}, u32[]{:S(2)}) async-start(bf16[64,4,1536]{2,1,0:T(4,128)(2,1)} %get-tuple-element.21), calls=%async_computation.1 | async-start | bytes 1572864 | tf_op jit(solution)/shard_map/all_to_all | solution.py:282
  37.0 4.2 %collective-permute-start = (bf16[384,768]{1,0:T(8,128)(2,1)S(1)}, bf16[384,768]{1,0:T(8,128)(2,1)S(1)}, u32[]{:S(2)}, u32[]{:S(2)}) collective-permute-start(bf16[384,768]{1,0:T(8,128)(2,1)S(1)} %bitcast.8), channel_id=1, source_target_pairs={{8,0},{16,8},{24,16},{0,24},{9,1},{17,9},{25,17},{1,25},{10,2},{18... | collective-permute-start | bytes 1769480 | tf_op jit(solution)/shard_map/ppermute | solution.py:329
  41.2 1.9 %collective-permute-start.1 = (bf16[384,768]{1,0:T(8,128)(2,1)S(1)}, bf16[384,768]{1,0:T(8,128)(2,1)S(1)}, u32[]{:S(2)}, u32[]{:S(2)}) collective-permute-start(bf16[384,768]{1,0:T(8,128)(2,1)S(1)} %bitcast.9), channel_id=1, source_target_pairs={{0,8},{8,16},{16,24},{24,0},{1,9},{9,17},{17,25},{25,1},{2,10},{10... | collective-permute-start | bytes 1769480 | tf_op jit(solution)/shard_map/ppermute | solution.py:329
  43.1 3.8 %collective-permute-start.2 = (bf16[384,768]{1,0:T(8,128)(2,1)S(1)}, bf16[384,768]{1,0:T(8,128)(2,1)S(1)}, u32[]{:S(2)}, u32[]{:S(2)}) collective-permute-start(bf16[384,768]{1,0:T(8,128)(2,1)S(1)} %bitcast.10), channel_id=1, source_target_pairs={{0,64},{64,0},{1,65},{65,1},{2,66},{66,2},{3,67},{67,3},{4,68},{68... | collective-permute-start | bytes 1769480 | tf_op jit(solution)/shard_map/ppermute | solution.py:330
  46.9 14.3 %collective-permute-done.p1 = bf16[384,768]{1,0:T(8,128)(2,1)S(1)} collective-permute-done((bf16[384,768]{1,0:T(8,128)(2,1)S(1)}, bf16[384,768]{1,0:T(8,128)(2,1)S(1)}, u32[]{:S(2)}, u32[]{:S(2)}) %collective-permute-start) | collective-permute-done | bytes 589856 | tf_op jit(solution)/shard_map/ppermute | solution.py:329
  61.2 0.8 slice.26
  62.0 3.5 %collective-permute-start.3 = (bf16[192,768]{1,0:T(8,128)(2,1)}, bf16[192,768]{1,0:T(8,128)(2,1)}, u32[]{:S(2)}, u32[]{:S(2)}) collective-permute-start(bf16[192,768]{1,0:T(8,128)(2,1)} %slice.26), channel_id=1, source_target_pairs={{8,0},{16,8},{24,16},{0,24},{9,1},{17,9},{25,17},{1,25},{10,2},{18... | collective-permute-start | bytes 884744 | tf_op jit(solution)/shard_map/ppermute | solution.py:335
  65.5 0.0 collective-permute-done.1.p4
  65.5 0.8 slice.27
  66.3 1.9 %collective-permute-start.4 = (bf16[192,768]{1,0:T(8,128)(2,1)}, bf16[192,768]{1,0:T(8,128)(2,1)}, u32[]{:S(2)}, u32[]{:S(2)}) collective-permute-start(bf16[192,768]{1,0:T(8,128)(2,1)} %slice.27), channel_id=1, source_target_pairs={{0,8},{8,16},{16,24},{24,0},{1,9},{9,17},{17,25},{25,1},{2,10},{10... | collective-permute-start | bytes 884744 | tf_op jit(solution)/shard_map/ppermute | solution.py:336
  68.2 0.0 all-to-all-done.1.slots_ref
  68.2 1.7 %fusion.flags_ref = s32[64]{0:T(128)} fusion(bf16[64,4,1536]{2,1,0:T(4,128)(2,1)S(1)} %all-to-all-done.1.slots_ref), kind=kLoop, calls=%fused_computation.4 | loop fusion | flops 128 | bytes 384 | tf_op jit(solution)/shard_map/convert_element_type | solution.py:328
  70.0 2.6 %scatter.1 = bf16[64,4,1536]{2,1,0:T(4,128)(2,1)} custom-call(s32[64]{0:T(128)} %fusion.flags_ref, bf16[128,1536]{1,0:T(8,128)(2,1)} %cot_ref.1), custom_call_target="tpu_custom_call" | custom-call | bytes 1179648 | tf_op jit(solution)/shard_map/scatter/pallas_call | solution.py:331
  72.6 0.0 collective-permute-done.2.q0
  72.6 0.0 collective-permute-done.3.p2
  72.6 3.4 %collective-permute-done.4.p3 = bf16[192,768]{1,0:T(8,128)(2,1)} collective-permute-done((bf16[192,768]{1,0:T(8,128)(2,1)}, bf16[192,768]{1,0:T(8,128)(2,1)}, u32[]{:S(2)}, u32[]{:S(2)}) %collective-permute-start.4) | collective-permute-done | bytes 294944 | tf_op jit(solution)/shard_map/ppermute | solution.py:336
  76.0 8.0 %all-to-all-start.2 = ((bf16[64,4,1536]{2,1,0:T(4,128)(2,1)}), bf16[64,4,1536]{2,1,0:T(4,128)(2,1)S(1)}, u32[]{:S(2)}, u32[]{:S(2)}) async-start(bf16[64,4,1536]{2,1,0:T(4,128)(2,1)} %scatter.1), calls=%async_computation.2 | async-start | bytes 1572864 | tf_op jit(solution)/shard_map/all_to_all | solution.py:282
  84.1 4.9 %collective-permute-start.5 = (bf16[384,768]{1,0:T(8,128)(2,1)S(1)}, bf16[384,768]{1,0:T(8,128)(2,1)S(1)}, u32[]{:S(2)}, u32[]{:S(2)}) collective-permute-start(bf16[384,768]{1,0:T(8,128)(2,1)S(1)} %collective-permute-done.p1), channel_id=1, source_target_pairs={{0,64},{64,0},{1,65},{65,1},{2,66},{66,2},{3,67},{67,3},{4,68},{68... | collective-permute-start | bytes 1769480 | tf_op jit(solution)/shard_map/ppermute | solution.py:342
  89.0 1.9 %collective-permute-start.8 = (bf16[384,768]{1,0:T(8,128)(2,1)S(1)}, bf16[384,768]{1,0:T(8,128)(2,1)}, u32[]{:S(2)}, u32[]{:S(2)}) collective-permute-start(bf16[384,768]{1,0:T(8,128)(2,1)S(1)} %collective-permute-done.1.p4), channel_id=1, source_target_pairs={{0,64},{64,0},{1,65},{65,1},{2,66},{66,2},{3,67},{67,3},{4,68},{68... | collective-permute-start | bytes 1769480 | tf_op jit(solution)/shard_map/ppermute | solution.py:342
  90.9 2.4 %collective-permute-start.6 = (bf16[192,768]{1,0:T(8,128)(2,1)}, bf16[192,768]{1,0:T(8,128)(2,1)}, u32[]{:S(2)}, u32[]{:S(2)}) collective-permute-start(bf16[192,768]{1,0:T(8,128)(2,1)} %collective-permute-done.3.p2), channel_id=1, source_target_pairs={{0,64},{64,0},{1,65},{65,1},{2,66},{66,2},{3,67},{67,3},{4,68},{68... | collective-permute-start | bytes 884744 | tf_op jit(solution)/shard_map/ppermute | solution.py:342
  93.3 1.9 %collective-permute-start.7 = (bf16[192,768]{1,0:T(8,128)(2,1)}, bf16[192,768]{1,0:T(8,128)(2,1)}, u32[]{:S(2)}, u32[]{:S(2)}) collective-permute-start(bf16[192,768]{1,0:T(8,128)(2,1)} %collective-permute-done.4.p3), channel_id=1, source_target_pairs={{0,64},{64,0},{1,65},{65,1},{2,66},{66,2},{3,67},{67,3},{4,68},{68... | collective-permute-start | bytes 884744 | tf_op jit(solution)/shard_map/ppermute | solution.py:342
  95.3 0.6 pad_add_fusion.place_ref
  95.8 0.0 collective-permute-done.6.q2
  95.8 1.3 collective-permute-done.7.q3
  97.1 0.0 collective-permute-done.5.q1
  97.2 0.0 collective-permute-done.8.q4
  97.2 7.0 %all-to-all-done.2.slots_ref = bf16[64,4,1536]{2,1,0:T(4,128)(2,1)S(1)} async-done(((bf16[64,4,1536]{2,1,0:T(4,128)(2,1)}), bf16[64,4,1536]{2,1,0:T(4,128)(2,1)S(1)}, u32[]{:S(2)}, u32[]{:S(2)}) %all-to-all-start.2) | async-done | bytes 786464 | tf_op jit(solution)/shard_map/all_to_all | solution.py:282
  104.1 0.0 copy-done.6
  104.1 0.9 copy-done.4
  105.0 12.5 %backward.1 = (bf16[192,1536]{1,0:T(8,128)(2,1)}, f32[16,1,1536]{2,1,0:T(1,128)}) custom-call(s32[48]{0:T(128)} %bitcast.16, s32[2]{0:T(128)} %pad_add_fusion.place_ref, s32[64]{0:T(128)} %order_ref.3, f32[15,1536]{1,0:T(8,128)} %kernel_ref.3, f32[1,1536]{1,0:T(1,128)} %broadcast_in_dim.9.gain_ref, f32[192,128]{1,0:T(8,128)} %get-tuple-element.28.inv_ref, ...), custom_call_target="tpu_custom_call" | custom-call | flops 7700742144 | bytes 9437184 | tf_op jit(solution)/shard_map/backward/pallas_call | solution.py:344
  117.6 14.6 %all_to_all.30 = f32[16,1,1536]{2,1,0:T(1,128)S(1)} all-to-all(f32[16,1,1536]{2,1,0:T(1,128)} %get-tuple-element.34), channel_id=1, replica_groups=mesh['zh'=4,'c'=2,'zl'=2,'x'=4,'y'=8] {'c','zl','x'}, dimensions={0} | all-to-all | bytes 196608 | tf_op jit(solution)/shard_map/all_to_all | solution.py:282
  132.2 0.1 reduce_sum.18
  132.3 0.1 broadcast_in_dim.10
  132.4 22.5 %all_to_all.31 = f32[32,1,1536]{2,1,0:T(1,128)S(1)} all-to-all(f32[32,1,1536]{2,1,0:T(1,128)S(1)} %broadcast_in_dim.10), channel_id=1, replica_groups=mesh['zh'=4,'c'=2,'zl'=2,'x'=4,'y'=8] {'zh','y'}, dimensions={0} | all-to-all | bytes 393216 | tf_op jit(solution)/shard_map/all_to_all | solution.py:282
  154.8 0.1 reduce_sum.19
  155.0 0.7 broadcast_in_dim.11
  155.7 6.3 %all-to-all-start.5 = ((f32[16,1,1536]{2,1,0:T(1,128)}), f32[16,1,1536]{2,1,0:T(1,128)S(1)}, u32[]{:S(2)}, u32[]{:S(2)}) async-start(f32[16,1,1536]{2,1,0:T(1,128)} %broadcast_in_dim.11), calls=%async_computation.5 | async-start | bytes 196608 | tf_op jit(solution)/shard_map/all_to_all | solution.py:282
  161.9 5.1 %project.1 = bf16[128,1536]{1,0:T(8,128)(2,1)} custom-call(s32[64]{0:T(128)} %fusion.flags_ref, s32[2]{0:T(128)} %pad_add_fusion.place_ref, s32[64]{0:T(128)} %order_ref.3, bf16[64,4,1536]{2,1,0:T(4,128)(2,1)} %copy-done, bf16[384,768]{1,0:T(8,128)(2,1)} %bitcast.12, bf16[384,768]{1,0:T(8,128)(2,1)} %copy-done.2, ...), custom_call_target="tpu_custom_call" | custom-call | flops 603979776 | bytes 5505024 | tf_op jit(solution)/shard_map/project/pallas_call | solution.py:378
  167.0 0.9 all-to-all-done.5
  168.0 0.7 copy.20
  168.6 0.6 slice_reduce_fusion
  (18 shorter events, 0.1 us)
Async XLA Ops:
  0.6 11.7 %copy-start.8 = (f32[1536]{0:T(1024)S(1)}, f32[1536]{0:T(1024)}, u32[]{:S(2)}) copy-start(f32[1536]{0:T(1024)} %param.15) | copy-start | bytes 18436
  1.9 20.7 %copy-start.7 = (f32[24,1536]{1,0:T(8,128)}, f32[24,1536]{1,0:T(8,128)S(1)}, u32[]{:S(2)}) copy-start(f32[24,1536]{1,0:T(8,128)S(1)} %multiply_subtract_fusion) | copy-start | bytes 442372
  2.8 24.6 %all-to-all-start = ((bf16[16,24,768]{2,1,0:T(8,128)(2,1)}), bf16[16,24,768]{2,1,0:T(8,128)(2,1)S(1)}, u32[]{:S(2)}, u32[]{:S(2)}) async-start(bf16[16,24,768]{2,1,0:T(8,128)(2,1)} %broadcast_in_dim.8), calls=%async_computation | async-start | bytes 1179648 | tf_op jit(solution)/shard_map/all_to_all | solution.py:282
  27.4 38.9 %copy-start.1 = (bf16[16,24,768]{2,1,0:T(8,128)(2,1)}, bf16[16,24,768]{2,1,0:T(8,128)(2,1)S(1)}, u32[]{:S(2)}) copy-start(bf16[16,24,768]{2,1,0:T(8,128)(2,1)S(1)} %all-to-all-done) | copy-start | bytes 1769476
  27.4 40.8 %all-to-all-start.1 = ((bf16[64,4,1536]{2,1,0:T(4,128)(2,1)}), bf16[64,4,1536]{2,1,0:T(4,128)(2,1)S(1)}, u32[]{:S(2)}, u32[]{:S(2)}) async-start(bf16[64,4,1536]{2,1,0:T(4,128)(2,1)} %get-tuple-element.21), calls=%async_computation.1 | async-start | bytes 1572864 | tf_op jit(solution)/shard_map/all_to_all | solution.py:282
  37.0 24.2 %collective-permute-start = (bf16[384,768]{1,0:T(8,128)(2,1)S(1)}, bf16[384,768]{1,0:T(8,128)(2,1)S(1)}, u32[]{:S(2)}, u32[]{:S(2)}) collective-permute-start(bf16[384,768]{1,0:T(8,128)(2,1)S(1)} %bitcast.8), channel_id=1, source_target_pairs={{8,0},{16,8},{24,16},{0,24},{9,1},{17,9},{25,17},{1,25},{10,2},{18... | collective-permute-start | bytes 1769480 | tf_op jit(solution)/shard_map/ppermute | solution.py:329
  41.2 24.3 %collective-permute-start.1 = (bf16[384,768]{1,0:T(8,128)(2,1)S(1)}, bf16[384,768]{1,0:T(8,128)(2,1)S(1)}, u32[]{:S(2)}, u32[]{:S(2)}) collective-permute-start(bf16[384,768]{1,0:T(8,128)(2,1)S(1)} %bitcast.9), channel_id=1, source_target_pairs={{0,8},{8,16},{16,24},{24,0},{1,9},{9,17},{17,25},{25,1},{2,10},{10... | collective-permute-start | bytes 1769480 | tf_op jit(solution)/shard_map/ppermute | solution.py:329
  43.1 29.5 %collective-permute-start.2 = (bf16[384,768]{1,0:T(8,128)(2,1)S(1)}, bf16[384,768]{1,0:T(8,128)(2,1)S(1)}, u32[]{:S(2)}, u32[]{:S(2)}) collective-permute-start(bf16[384,768]{1,0:T(8,128)(2,1)S(1)} %bitcast.10), channel_id=1, source_target_pairs={{0,64},{64,0},{1,65},{65,1},{2,66},{66,2},{3,67},{67,3},{4,68},{68... | collective-permute-start | bytes 1769480 | tf_op jit(solution)/shard_map/ppermute | solution.py:330
  61.2 22.9 %copy-start.2 = (bf16[384,768]{1,0:T(8,128)(2,1)}, bf16[384,768]{1,0:T(8,128)(2,1)S(1)}, u32[]{:S(2)}) copy-start(bf16[384,768]{1,0:T(8,128)(2,1)S(1)} %collective-permute-done.p1) | copy-start | bytes 1769476
  62.0 10.7 %collective-permute-start.3 = (bf16[192,768]{1,0:T(8,128)(2,1)}, bf16[192,768]{1,0:T(8,128)(2,1)}, u32[]{:S(2)}, u32[]{:S(2)}) collective-permute-start(bf16[192,768]{1,0:T(8,128)(2,1)} %slice.26), channel_id=1, source_target_pairs={{8,0},{16,8},{24,16},{0,24},{9,1},{17,9},{25,17},{1,25},{10,2},{18... | collective-permute-start | bytes 884744 | tf_op jit(solution)/shard_map/ppermute | solution.py:335
  65.5 23.5 %copy-start.3 = (bf16[384,768]{1,0:T(8,128)(2,1)}, bf16[384,768]{1,0:T(8,128)(2,1)S(1)}, u32[]{:S(2)}) copy-start(bf16[384,768]{1,0:T(8,128)(2,1)S(1)} %collective-permute-done.1.p4) | copy-start | bytes 1769476
  66.3 9.7 %collective-permute-start.4 = (bf16[192,768]{1,0:T(8,128)(2,1)}, bf16[192,768]{1,0:T(8,128)(2,1)}, u32[]{:S(2)}, u32[]{:S(2)}) collective-permute-start(bf16[192,768]{1,0:T(8,128)(2,1)} %slice.27), channel_id=1, source_target_pairs={{0,8},{8,16},{16,24},{24,0},{1,9},{9,17},{17,25},{25,1},{2,10},{10... | collective-permute-start | bytes 884744 | tf_op jit(solution)/shard_map/ppermute | solution.py:336
  68.2 7.8 %copy-start = (bf16[64,4,1536]{2,1,0:T(4,128)(2,1)}, bf16[64,4,1536]{2,1,0:T(4,128)(2,1)S(1)}, u32[]{:S(2)}) copy-start(bf16[64,4,1536]{2,1,0:T(4,128)(2,1)S(1)} %all-to-all-done.1.slots_ref) | copy-start | bytes 2359300
  72.6 31.5 %copy-start.5 = (bf16[384,768]{1,0:T(8,128)(2,1)}, bf16[384,768]{1,0:T(8,128)(2,1)S(1)}, u32[]{:S(2)}) copy-start(bf16[384,768]{1,0:T(8,128)(2,1)S(1)} %collective-permute-done.2.q0) | copy-start | bytes 1769476
  76.0 28.1 %all-to-all-start.2 = ((bf16[64,4,1536]{2,1,0:T(4,128)(2,1)}), bf16[64,4,1536]{2,1,0:T(4,128)(2,1)S(1)}, u32[]{:S(2)}, u32[]{:S(2)}) async-start(bf16[64,4,1536]{2,1,0:T(4,128)(2,1)} %scatter.1), calls=%async_computation.2 | async-start | bytes 1572864 | tf_op jit(solution)/shard_map/all_to_all | solution.py:282
  84.1 13.1 %collective-permute-start.5 = (bf16[384,768]{1,0:T(8,128)(2,1)S(1)}, bf16[384,768]{1,0:T(8,128)(2,1)S(1)}, u32[]{:S(2)}, u32[]{:S(2)}) collective-permute-start(bf16[384,768]{1,0:T(8,128)(2,1)S(1)} %collective-permute-done.p1), channel_id=1, source_target_pairs={{0,64},{64,0},{1,65},{65,1},{2,66},{66,2},{3,67},{67,3},{4,68},{68... | collective-permute-start | bytes 1769480 | tf_op jit(solution)/shard_map/ppermute | solution.py:342
  89.0 8.2 %collective-permute-start.8 = (bf16[384,768]{1,0:T(8,128)(2,1)S(1)}, bf16[384,768]{1,0:T(8,128)(2,1)}, u32[]{:S(2)}, u32[]{:S(2)}) collective-permute-start(bf16[384,768]{1,0:T(8,128)(2,1)S(1)} %collective-permute-done.1.p4), channel_id=1, source_target_pairs={{0,64},{64,0},{1,65},{65,1},{2,66},{66,2},{3,67},{67,3},{4,68},{68... | collective-permute-start | bytes 1769480 | tf_op jit(solution)/shard_map/ppermute | solution.py:342
  90.9 4.9 %collective-permute-start.6 = (bf16[192,768]{1,0:T(8,128)(2,1)}, bf16[192,768]{1,0:T(8,128)(2,1)}, u32[]{:S(2)}, u32[]{:S(2)}) collective-permute-start(bf16[192,768]{1,0:T(8,128)(2,1)} %collective-permute-done.3.p2), channel_id=1, source_target_pairs={{0,64},{64,0},{1,65},{65,1},{2,66},{66,2},{3,67},{67,3},{4,68},{68... | collective-permute-start | bytes 884744 | tf_op jit(solution)/shard_map/ppermute | solution.py:342
  93.3 3.8 %collective-permute-start.7 = (bf16[192,768]{1,0:T(8,128)(2,1)}, bf16[192,768]{1,0:T(8,128)(2,1)}, u32[]{:S(2)}, u32[]{:S(2)}) collective-permute-start(bf16[192,768]{1,0:T(8,128)(2,1)} %collective-permute-done.4.p3), channel_id=1, source_target_pairs={{0,64},{64,0},{1,65},{65,1},{2,66},{66,2},{3,67},{67,3},{4,68},{68... | collective-permute-start | bytes 884744 | tf_op jit(solution)/shard_map/ppermute | solution.py:342
  97.1 7.0 %copy-start.6 = (bf16[384,768]{1,0:T(8,128)(2,1)}, bf16[384,768]{1,0:T(8,128)(2,1)S(1)}, u32[]{:S(2)}) copy-start(bf16[384,768]{1,0:T(8,128)(2,1)S(1)} %collective-permute-done.5.q1) | copy-start | bytes 1769476
  104.1 0.9 copy-start.4
  155.7 12.3 %all-to-all-start.5 = ((f32[16,1,1536]{2,1,0:T(1,128)}), f32[16,1,1536]{2,1,0:T(1,128)S(1)}, u32[]{:S(2)}, u32[]{:S(2)}) async-start(f32[16,1,1536]{2,1,0:T(1,128)} %broadcast_in_dim.11), calls=%async_computation.5 | async-start | bytes 196608 | tf_op jit(solution)/shard_map/all_to_all | solution.py:282

commit v7 on v5

--- a/solution.py
+++ b/solution.py
@@ -294,7 +294,8 @@
     gain = norm_gain[None, :]
 
     updated = adam_step(master, moment, second, gradient)
-    bucket = lax.dynamic_slice_in_dim(updated, core * half, half, axis=1).astype(BF16)
+    state = [lax.dynamic_slice_in_dim(a, core * half, half, axis=1) for a in (master, moment, second, gradient)]
+    bucket = adam_step(*state).astype(BF16)
     near = lax.axis_size(("zl", "y"))
     line = exchange(jnp.broadcast_to(bucket[None], (near, *bucket.shape)), ("zl", "y")).reshape(-1, half)
 
@@ -336,6 +337,7 @@
     part = line.shape[0] // 2
     far_low = lax.ppermute(next_x[:part], "x", ahead)
     far_high = lax.ppermute(last_x[part:], "x", behind)
+    next_x, far_low = lax.optimization_barrier((next_x, far_low))
     half_pieces = [line, next_x, far_low, far_high, last_x]
     pieces = half_pieces + [line_c] + [lax.ppermute(piece, "c", swap) for piece in half_pieces[1:]]
 
@@ -370,9 +372,6 @@
     mine = jnp.sum(exchange(term, NEAR), axis=0, keepdims=True)
     far = lax.axis_size(FAR)
     mine = jnp.sum(exchange(jnp.broadcast_to(mine, (far, 1, columns)), FAR), axis=0, keepdims=True)
-    divisor = math.sqrt(lax.axis_size(("zh", "c")) * owners * ROWS)
-    sums = exchange(jnp.broadcast_to(mine / divisor, (taps + 1, 1, columns)), NEAR)[:, 0, :]
-
     (projected,) = call(
         project_kernel,
         [SM] * 3 + [VM] + [AN] * 10,
@@ -389,6 +388,9 @@
         2 * cotangent.size * columns,
         4 * cotangent.size + 2 * columns * columns,
     )(flags, place, bucket_order, act_slots, *pieces)
+    mine, projected = lax.optimization_barrier((mine, projected))
+    divisor = math.sqrt(lax.axis_size(("zh", "c")) * owners * ROWS)
+    sums = exchange(jnp.broadcast_to(mine / divisor, (taps + 1, 1, columns)), NEAR)[:, 0, :]
     return projected, frame_grad, sums[:taps], sums[taps], updated
 
 

time: 165 us -> 165 us (level)
  blocking collectives: 35.3 us -> 9.71 us
  starting transfers between devices: 61.3 us -> 76.1 us
  waiting for transfers between devices: 27 us -> 36.8 us
    all_to_all x2 -> x1, blocking collectives: 35.3 us -> 9.71 us  [exchange(): return lax.all_to_all(x, axes, split_axis=0, concat_axis=0, tiled=True)]
    all_to_all x4 -> x5, starting transfers between devices: 33.6 us -> 47.4 us  [exchange(): return lax.all_to_all(x, axes, split_axis=0, concat_axis=0, tiled=True)]
    all_to_all x4 -> x5, waiting for transfers between devices: 17.3 us -> 28 us  [exchange(): return lax.all_to_all(x, axes, split_axis=0, concat_axis=0, tiled=True)]
    ppermute x1, waiting for transfers between devices: 6.7 us -> 5.01 us  [body(): far_low = lax.ppermute(next_x[:part], 'x', ahead)]
  transfers between devices with their start and end apart: 13 -> 14, of which waited for: 7 -> 8; matrix products, arithmetic and copies ran while one was open for 2% -> 2% of each run, Pallas kernels for 11% -> 11%
where the time goes in v7:
time: 165 us; the launch traced here: 164 us
  starting transfers between devices  76.1 us (46%)
  waiting for transfers between devices  36.8 us (22%)
  Pallas kernels  30 us (18%)
  blocking collectives  9.71 us (6%)
  local copies, waits for them, and re-layouts  5.67 us (3%)
  other arithmetic  4.51 us (3%)
    all_to_all x5, starting transfers between devices, exchange(): return lax.all_to_all(x, axes, split_axis=0, concat_axis=0, tiled=True)  47.4 us
    all_to_all x5, waiting for transfers between devices, exchange(): return lax.all_to_all(x, axes, split_axis=0, concat_axis=0, tiled=True)  28 us
    ppermute x4, starting transfers between devices, body(): lax.ppermute(piece, 'c', swap)  12.7 us
    pallas_call x1, Pallas kernels, body(): call(backward_kernel, [SM] * 3 + [VM] * 4 + [HB] * 4 + [AN] * 10, [jax.Sh...  12.5 us
    all_to_all x1, blocking collectives, exchange(): return lax.all_to_all(x, axes, split_axis=0, concat_axis=0, tiled=True)  9.71 us
    pallas_call x1, Pallas kernels, body(): call(forward_kernel, [SM, SM, VM, VM, VM], [slots, jax.ShapeDtypeStruct((...  9.66 us
    pallas_call x1, Pallas kernels, body(): call(project_kernel, [SM] * 3 + [VM] + [AN] * 10, [jax.ShapeDtypeStruct(c...  5.15 us
    ppermute x1, waiting for transfers between devices, body(): far_low = lax.ppermute(next_x[:part], 'x', ahead)  5.01 us
  transfers between devices with their start and end apart: 14, of which 8 were waited for; matrix products, arithmetic and copies ran while one was open for 2% of the time, Pallas kernels for 11%

profile of v7, /device:TPU:1, one launch (start us, length us, event | category | flops | bytes accessed | tf_op | source)
XLA Modules:
  0.0 163.7 jit_solution(13949938815637803658)
XLA Ops:
  0.6 1.1 subtract_convert_fusion
  1.7 0.9 broadcast_in_dim.26
  2.6 9.6 %all-to-all-start = ((bf16[16,24,768]{2,1,0:T(8,128)(2,1)}), bf16[16,24,768]{2,1,0:T(8,128)(2,1)S(1)}, u32[]{:S(2)}, u32[]{:S(2)}) async-start(bf16[16,24,768]{2,1,0:T(8,128)(2,1)} %broadcast_in_dim.26), calls=%async_computation | async-start | bytes 1179648 | tf_op jit(solution)/shard_map/all_to_all | solution.py:282
  12.1 0.6 broadcast_in_dim.12.gain_ref
  12.7 9.7 %forward.1 = (bf16[64,4,1536]{2,1,0:T(4,128)(2,1)}, f32[192,128]{1,0:T(8,128)}, f32[192,1536]{1,0:T(8,128)}, f32[192,1536]{1,0:T(8,128)}, bf16[2880,192]{1,0:T(8,128)(2,1)}) custom-call(s32[8]{0:T(128)} %bitcast.14, s32[48]{0:T(128)} %bitcast.15, bf16[192,1536]{1,0:T(8,128)(2,1)} %frames_hbm.1, f32[15,1536]{1,0:T(8,128)} %kernel_ref.3, ...), custom_call_target="tpu_custom_call" | custom-call | flops 6794772480 | bytes 4718592 | tf_op jit(solution)/shard_map/forward/pallas_call | solution.py:305
  22.4 4.8 %all-to-all-done = bf16[16,24,768]{2,1,0:T(8,128)(2,1)S(1)} async-done(((bf16[16,24,768]{2,1,0:T(8,128)(2,1)}), bf16[16,24,768]{2,1,0:T(8,128)(2,1)S(1)}, u32[]{:S(2)}, u32[]{:S(2)}) %all-to-all-start) | async-done | bytes 589856 | tf_op jit(solution)/shard_map/all_to_all | solution.py:282
  27.2 9.6 %all-to-all-start.1 = ((bf16[64,4,1536]{2,1,0:T(4,128)(2,1)}), bf16[64,4,1536]{2,1,0:T(4,128)(2,1)S(1)}, u32[]{:S(2)}, u32[]{:S(2)}) async-start(bf16[64,4,1536]{2,1,0:T(4,128)(2,1)} %get-tuple-element.24), calls=%async_computation.1 | async-start | bytes 1572864 | tf_op jit(solution)/shard_map/all_to_all | solution.py:282
  36.8 4.2 %collective-permute-start = (bf16[384,768]{1,0:T(8,128)(2,1)S(1)}, bf16[384,768]{1,0:T(8,128)(2,1)S(1)}, u32[]{:S(2)}, u32[]{:S(2)}) collective-permute-start(bf16[384,768]{1,0:T(8,128)(2,1)S(1)} %bitcast.8), channel_id=1, source_target_pairs={{8,0},{16,8},{24,16},{0,24},{9,1},{17,9},{25,17},{1,25},{10,2},{18... | collective-permute-start | bytes 1769480 | tf_op jit(solution)/shard_map/ppermute | solution.py:330
  41.0 1.9 %collective-permute-start.1 = (bf16[384,768]{1,0:T(8,128)(2,1)S(1)}, bf16[384,768]{1,0:T(8,128)(2,1)S(1)}, u32[]{:S(2)}, u32[]{:S(2)}) collective-permute-start(bf16[384,768]{1,0:T(8,128)(2,1)S(1)} %bitcast.9), channel_id=1, source_target_pairs={{0,8},{8,16},{16,24},{24,0},{1,9},{9,17},{17,25},{25,1},{2,10},{10... | collective-permute-start | bytes 1769480 | tf_op jit(solution)/shard_map/ppermute | solution.py:330
  42.9 3.8 %collective-permute-start.2 = (bf16[384,768]{1,0:T(8,128)(2,1)S(1)}, bf16[384,768]{1,0:T(8,128)(2,1)S(1)}, u32[]{:S(2)}, u32[]{:S(2)}) collective-permute-start(bf16[384,768]{1,0:T(8,128)(2,1)S(1)} %bitcast.10), channel_id=1, source_target_pairs={{0,64},{64,0},{1,65},{65,1},{2,66},{66,2},{3,67},{67,3},{4,68},{68... | collective-permute-start | bytes 1769480 | tf_op jit(solution)/shard_map/ppermute | solution.py:331
  46.7 11.6 %all-to-all-done.1.slots_ref = bf16[64,4,1536]{2,1,0:T(4,128)(2,1)S(1)} async-done(((bf16[64,4,1536]{2,1,0:T(4,128)(2,1)}), bf16[64,4,1536]{2,1,0:T(4,128)(2,1)S(1)}, u32[]{:S(2)}, u32[]{:S(2)}) %all-to-all-start.1) | async-done | bytes 786464 | tf_op jit(solution)/shard_map/all_to_all | solution.py:282
  58.3 1.8 %fusion.flags_ref = s32[64]{0:T(128)} fusion(bf16[64,4,1536]{2,1,0:T(4,128)(2,1)S(1)} %all-to-all-done.1.slots_ref), kind=kLoop, calls=%fused_computation.4 | loop fusion | flops 128 | bytes 384 | tf_op jit(solution)/shard_map/convert_element_type | solution.py:329
  60.1 2.6 %scatter.1 = bf16[64,4,1536]{2,1,0:T(4,128)(2,1)} custom-call(s32[64]{0:T(128)} %fusion.flags_ref, bf16[128,1536]{1,0:T(8,128)(2,1)} %cot_ref.1), custom_call_target="tpu_custom_call" | custom-call | bytes 1179648 | tf_op jit(solution)/shard_map/scatter/pallas_call | solution.py:332
  62.7 0.0 collective-permute-done.p1
  62.7 0.5 collective-permute-done.1.p4
  63.3 0.0 collective-permute-done.2.q0
  63.3 8.2 %all-to-all-start.2 = ((bf16[64,4,1536]{2,1,0:T(4,128)(2,1)}), bf16[64,4,1536]{2,1,0:T(4,128)(2,1)S(1)}, u32[]{:S(2)}, u32[]{:S(2)}) async-start(bf16[64,4,1536]{2,1,0:T(4,128)(2,1)} %scatter.1), calls=%async_computation.2 | async-start | bytes 1572864 | tf_op jit(solution)/shard_map/all_to_all | solution.py:282
  71.5 4.2 %collective-permute-start.3 = (bf16[192,768]{1,0:T(8,128)(2,1)S(1)}, bf16[192,768]{1,0:T(8,128)(2,1)}, u32[]{:S(2)}, u32[]{:S(2)}) collective-permute-start(bf16[192,768]{1,0:T(8,128)(2,1)S(1)} %slice.20), channel_id=1, source_target_pairs={{8,0},{16,8},{24,16},{0,24},{9,1},{17,9},{25,17},{1,25},{10,2},{18... | collective-permute-start | bytes 884744 | tf_op jit(solution)/shard_map/ppermute | solution.py:338
  75.7 4.3 %collective-permute-start.8 = (bf16[384,768]{1,0:T(8,128)(2,1)S(1)}, bf16[384,768]{1,0:T(8,128)(2,1)S(1)}, u32[]{:S(2)}, u32[]{:S(2)}) collective-permute-start(bf16[384,768]{1,0:T(8,128)(2,1)S(1)} %collective-permute-done.1.p4), channel_id=1, source_target_pairs={{0,64},{64,0},{1,65},{65,1},{2,66},{66,2},{3,67},{67,3},{4,68},{68... | collective-permute-start | bytes 1769480 | tf_op jit(solution)/shard_map/ppermute | solution.py:342
  80.0 1.9 %collective-permute-start.4 = (bf16[192,768]{1,0:T(8,128)(2,1)S(1)}, bf16[192,768]{1,0:T(8,128)(2,1)S(1)}, u32[]{:S(2)}, u32[]{:S(2)}) collective-permute-start(bf16[192,768]{1,0:T(8,128)(2,1)S(1)} %slice.21), channel_id=1, source_target_pairs={{0,8},{8,16},{16,24},{24,0},{1,9},{9,17},{17,25},{25,1},{2,10},{10... | collective-permute-start | bytes 884744 | tf_op jit(solution)/shard_map/ppermute | solution.py:339
  82.0 5.0 %collective-permute-done.3.p2 = bf16[192,768]{1,0:T(8,128)(2,1)} collective-permute-done((bf16[192,768]{1,0:T(8,128)(2,1)S(1)}, bf16[192,768]{1,0:T(8,128)(2,1)}, u32[]{:S(2)}, u32[]{:S(2)}) %collective-permute-start.3) | collective-permute-done | bytes 294944 | tf_op jit(solution)/shard_map/ppermute | solution.py:338
  87.0 4.0 %collective-permute-start.5 = (bf16[384,768]{1,0:T(8,128)(2,1)S(1)}, bf16[384,768]{1,0:T(8,128)(2,1)S(1)}, u32[]{:S(2)}, u32[]{:S(2)}) collective-permute-start(bf16[384,768]{1,0:T(8,128)(2,1)S(1)} %collective-permute-done.p1), channel_id=1, source_target_pairs={{0,64},{64,0},{1,65},{65,1},{2,66},{66,2},{3,67},{67,3},{4,68},{68... | collective-permute-start | bytes 1769480 | tf_op jit(solution)/shard_map/ppermute | solution.py:342
  91.0 1.9 %collective-permute-start.6 = (bf16[192,768]{1,0:T(8,128)(2,1)}, bf16[192,768]{1,0:T(8,128)(2,1)}, u32[]{:S(2)}, u32[]{:S(2)}) collective-permute-start(bf16[192,768]{1,0:T(8,128)(2,1)} %collective-permute-done.3.p2), channel_id=1, source_target_pairs={{0,64},{64,0},{1,65},{65,1},{2,66},{66,2},{3,67},{67,3},{4,68},{68... | collective-permute-start | bytes 884744 | tf_op jit(solution)/shard_map/ppermute | solution.py:342
  92.9 2.6 %collective-permute-done.4.p3 = bf16[192,768]{1,0:T(8,128)(2,1)S(1)} collective-permute-done((bf16[192,768]{1,0:T(8,128)(2,1)S(1)}, bf16[192,768]{1,0:T(8,128)(2,1)S(1)}, u32[]{:S(2)}, u32[]{:S(2)}) %collective-permute-start.4) | collective-permute-done | bytes 294944 | tf_op jit(solution)/shard_map/ppermute | solution.py:339
  95.5 2.5 %collective-permute-start.7 = (bf16[192,768]{1,0:T(8,128)(2,1)S(1)}, bf16[192,768]{1,0:T(8,128)(2,1)}, u32[]{:S(2)}, u32[]{:S(2)}) collective-permute-start(bf16[192,768]{1,0:T(8,128)(2,1)S(1)} %collective-permute-done.4.p3), channel_id=1, source_target_pairs={{0,64},{64,0},{1,65},{65,1},{2,66},{66,2},{3,67},{67,3},{4,68},{68... | collective-permute-start | bytes 884744 | tf_op jit(solution)/shard_map/ppermute | solution.py:342
  97.9 0.6 pad_add_fusion.place_ref
  98.6 0.7 collective-permute-done.7.q3
  99.3 0.8 copy-done.6
  100.1 0.2 copy-done.7
  100.3 0.3 copy-done.4
  100.7 12.5 %backward.1 = (bf16[192,1536]{1,0:T(8,128)(2,1)}, f32[16,1,1536]{2,1,0:T(1,128)}) custom-call(s32[48]{0:T(128)} %bitcast.16, s32[2]{0:T(128)} %pad_add_fusion.place_ref, s32[64]{0:T(128)} %order_ref.3, f32[15,1536]{1,0:T(8,128)} %kernel_ref.3, f32[1,1536]{1,0:T(1,128)} %broadcast_in_dim.12.gain_ref, f32[192,128]{1,0:T(8,128)} %get-tuple-element.22.inv_ref, ...), custom_call_target="tpu_custom_call" | custom-call | flops 7700742144 | bytes 9437184 | tf_op jit(solution)/shard_map/backward/pallas_call | solution.py:344
  113.2 9.7 %all_to_all.30 = f32[16,1,1536]{2,1,0:T(1,128)S(1)} all-to-all(f32[16,1,1536]{2,1,0:T(1,128)} %get-tuple-element.35), channel_id=1, replica_groups=mesh['zh'=4,'c'=2,'zl'=2,'x'=4,'y'=8] {'c','zl','x'}, dimensions={0} | all-to-all | bytes 196608 | tf_op jit(solution)/shard_map/all_to_all | solution.py:282
  122.9 0.1 reduce_sum.18
  123.0 0.8 broadcast_in_dim.27
  123.8 13.8 %all-to-all-start.4 = ((f32[32,1,1536]{2,1,0:T(1,128)}), f32[32,1,1536]{2,1,0:T(1,128)S(1)}, u32[]{:S(2)}, u32[]{:S(2)}) async-start(f32[32,1,1536]{2,1,0:T(1,128)} %broadcast_in_dim.27), calls=%async_computation.4 | async-start | bytes 393216 | tf_op jit(solution)/shard_map/all_to_all | solution.py:282
  137.6 0.0 copy-start.8
  137.6 0.0 copy-start.9
  137.6 0.0 copy-start.10
  137.6 0.0 copy-start.11
  137.7 5.2 %project.1 = bf16[128,1536]{1,0:T(8,128)(2,1)} custom-call(s32[64]{0:T(128)} %fusion.flags_ref, s32[2]{0:T(128)} %pad_add_fusion.place_ref, s32[64]{0:T(128)} %order_ref.3, bf16[64,4,1536]{2,1,0:T(4,128)(2,1)} %copy-done, bf16[384,768]{1,0:T(8,128)(2,1)} %bitcast.12, bf16[384,768]{1,0:T(8,128)(2,1)} %copy-done.2, ...), custom_call_target="tpu_custom_call" | custom-call | flops 603979776 | bytes 5505024 | tf_op jit(solution)/shard_map/project/pallas_call | solution.py:375
  142.8 6.5 %all-to-all-done.4 = f32[32,1,1536]{2,1,0:T(1,128)S(1)} async-done(((f32[32,1,1536]{2,1,0:T(1,128)}), f32[32,1,1536]{2,1,0:T(1,128)S(1)}, u32[]{:S(2)}, u32[]{:S(2)}) %all-to-all-start.4) | async-done | bytes 196640 | tf_op jit(solution)/shard_map/all_to_all | solution.py:282
  149.3 0.1 reduce_sum.19
  149.4 0.7 broadcast_in_dim.30
  150.1 6.3 %all-to-all-start.5 = ((f32[16,1,1536]{2,1,0:T(1,128)}), f32[16,1,1536]{2,1,0:T(1,128)S(1)}, u32[]{:S(2)}, u32[]{:S(2)}) async-start(f32[16,1,1536]{2,1,0:T(1,128)} %broadcast_in_dim.30), calls=%async_computation.5 | async-start | bytes 196608 | tf_op jit(solution)/shard_map/all_to_all | solution.py:282
  156.4 0.8 multiply_subtract_fusion
  157.2 5.2 %all-to-all-done.5 = f32[16,1,1536]{2,1,0:T(1,128)S(1)} async-done(((f32[16,1,1536]{2,1,0:T(1,128)}), f32[16,1,1536]{2,1,0:T(1,128)S(1)}, u32[]{:S(2)}, u32[]{:S(2)}) %all-to-all-start.5) | async-done | bytes 98336 | tf_op jit(solution)/shard_map/all_to_all | solution.py:282
  162.4 0.7 copy.20
  163.1 0.6 slice_reduce_fusion
  (30 shorter events, 0.1 us)
Async XLA Ops:
  0.6 11.5 %copy-start.13 = (f32[1536]{0:T(1024)S(1)}, f32[1536]{0:T(1024)}, u32[]{:S(2)}) copy-start(f32[1536]{0:T(1024)} %param.15) | copy-start | bytes 18436
  2.6 24.6 %all-to-all-start = ((bf16[16,24,768]{2,1,0:T(8,128)(2,1)}), bf16[16,24,768]{2,1,0:T(8,128)(2,1)S(1)}, u32[]{:S(2)}, u32[]{:S(2)}) async-start(bf16[16,24,768]{2,1,0:T(8,128)(2,1)} %broadcast_in_dim.26), calls=%async_computation | async-start | bytes 1179648 | tf_op jit(solution)/shard_map/all_to_all | solution.py:282
  27.2 35.5 %copy-start.1 = (bf16[16,24,768]{2,1,0:T(8,128)(2,1)}, bf16[16,24,768]{2,1,0:T(8,128)(2,1)S(1)}, u32[]{:S(2)}) copy-start(bf16[16,24,768]{2,1,0:T(8,128)(2,1)S(1)} %all-to-all-done) | copy-start | bytes 1769476
  27.2 31.1 %all-to-all-start.1 = ((bf16[64,4,1536]{2,1,0:T(4,128)(2,1)}), bf16[64,4,1536]{2,1,0:T(4,128)(2,1)S(1)}, u32[]{:S(2)}, u32[]{:S(2)}) async-start(bf16[64,4,1536]{2,1,0:T(4,128)(2,1)} %get-tuple-element.24), calls=%async_computation.1 | async-start | bytes 1572864 | tf_op jit(solution)/shard_map/all_to_all | solution.py:282
  36.8 25.9 %collective-permute-start = (bf16[384,768]{1,0:T(8,128)(2,1)S(1)}, bf16[384,768]{1,0:T(8,128)(2,1)S(1)}, u32[]{:S(2)}, u32[]{:S(2)}) collective-permute-start(bf16[384,768]{1,0:T(8,128)(2,1)S(1)} %bitcast.8), channel_id=1, source_target_pairs={{8,0},{16,8},{24,16},{0,24},{9,1},{17,9},{25,17},{1,25},{10,2},{18... | collective-permute-start | bytes 1769480 | tf_op jit(solution)/shard_map/ppermute | solution.py:330
  41.0 22.3 %collective-permute-start.1 = (bf16[384,768]{1,0:T(8,128)(2,1)S(1)}, bf16[384,768]{1,0:T(8,128)(2,1)S(1)}, u32[]{:S(2)}, u32[]{:S(2)}) collective-permute-start(bf16[384,768]{1,0:T(8,128)(2,1)S(1)} %bitcast.9), channel_id=1, source_target_pairs={{0,8},{8,16},{16,24},{24,0},{1,9},{9,17},{17,25},{25,1},{2,10},{10... | collective-permute-start | bytes 1769480 | tf_op jit(solution)/shard_map/ppermute | solution.py:330
  42.9 20.4 %collective-permute-start.2 = (bf16[384,768]{1,0:T(8,128)(2,1)S(1)}, bf16[384,768]{1,0:T(8,128)(2,1)S(1)}, u32[]{:S(2)}, u32[]{:S(2)}) collective-permute-start(bf16[384,768]{1,0:T(8,128)(2,1)S(1)} %bitcast.10), channel_id=1, source_target_pairs={{0,64},{64,0},{1,65},{65,1},{2,66},{66,2},{3,67},{67,3},{4,68},{68... | collective-permute-start | bytes 1769480 | tf_op jit(solution)/shard_map/ppermute | solution.py:331
  58.3 5.0 %copy-start = (bf16[64,4,1536]{2,1,0:T(4,128)(2,1)}, bf16[64,4,1536]{2,1,0:T(4,128)(2,1)S(1)}, u32[]{:S(2)}) copy-start(bf16[64,4,1536]{2,1,0:T(4,128)(2,1)S(1)} %all-to-all-done.1.slots_ref) | copy-start | bytes 2359300
  62.7 24.2 %copy-start.2 = (bf16[384,768]{1,0:T(8,128)(2,1)}, bf16[384,768]{1,0:T(8,128)(2,1)S(1)}, u32[]{:S(2)}) copy-start(bf16[384,768]{1,0:T(8,128)(2,1)S(1)} %collective-permute-done.p1) | copy-start | bytes 1769476
  63.3 12.4 %copy-start.3 = (bf16[384,768]{1,0:T(8,128)(2,1)}, bf16[384,768]{1,0:T(8,128)(2,1)S(1)}, u32[]{:S(2)}) copy-start(bf16[384,768]{1,0:T(8,128)(2,1)S(1)} %collective-permute-done.1.p4) | copy-start | bytes 1769476
  63.3 12.4 %copy-start.5 = (bf16[384,768]{1,0:T(8,128)(2,1)}, bf16[384,768]{1,0:T(8,128)(2,1)S(1)}, u32[]{:S(2)}) copy-start(bf16[384,768]{1,0:T(8,128)(2,1)S(1)} %collective-permute-done.2.q0) | copy-start | bytes 1769476
  63.3 36.0 %all-to-all-start.2 = ((bf16[64,4,1536]{2,1,0:T(4,128)(2,1)}), bf16[64,4,1536]{2,1,0:T(4,128)(2,1)S(1)}, u32[]{:S(2)}, u32[]{:S(2)}) async-start(bf16[64,4,1536]{2,1,0:T(4,128)(2,1)} %scatter.1), calls=%async_computation.2 | async-start | bytes 1572864 | tf_op jit(solution)/shard_map/all_to_all | solution.py:282
  71.5 15.5 %collective-permute-start.3 = (bf16[192,768]{1,0:T(8,128)(2,1)S(1)}, bf16[192,768]{1,0:T(8,128)(2,1)}, u32[]{:S(2)}, u32[]{:S(2)}) collective-permute-start(bf16[192,768]{1,0:T(8,128)(2,1)S(1)} %slice.20), channel_id=1, source_target_pairs={{8,0},{16,8},{24,16},{0,24},{9,1},{17,9},{25,17},{1,25},{10,2},{18... | collective-permute-start | bytes 884744 | tf_op jit(solution)/shard_map/ppermute | solution.py:338
  75.7 23.6 %collective-permute-start.8 = (bf16[384,768]{1,0:T(8,128)(2,1)S(1)}, bf16[384,768]{1,0:T(8,128)(2,1)S(1)}, u32[]{:S(2)}, u32[]{:S(2)}) collective-permute-start(bf16[384,768]{1,0:T(8,128)(2,1)S(1)} %collective-permute-done.1.p4), channel_id=1, source_target_pairs={{0,64},{64,0},{1,65},{65,1},{2,66},{66,2},{3,67},{67,3},{4,68},{68... | collective-permute-start | bytes 1769480 | tf_op jit(solution)/shard_map/ppermute | solution.py:342
  80.0 15.4 %collective-permute-start.4 = (bf16[192,768]{1,0:T(8,128)(2,1)S(1)}, bf16[192,768]{1,0:T(8,128)(2,1)S(1)}, u32[]{:S(2)}, u32[]{:S(2)}) collective-permute-start(bf16[192,768]{1,0:T(8,128)(2,1)S(1)} %slice.21), channel_id=1, source_target_pairs={{0,8},{8,16},{16,24},{24,0},{1,9},{9,17},{17,25},{25,1},{2,10},{10... | collective-permute-start | bytes 884744 | tf_op jit(solution)/shard_map/ppermute | solution.py:339
  87.0 12.3 %collective-permute-start.5 = (bf16[384,768]{1,0:T(8,128)(2,1)S(1)}, bf16[384,768]{1,0:T(8,128)(2,1)S(1)}, u32[]{:S(2)}, u32[]{:S(2)}) collective-permute-start(bf16[384,768]{1,0:T(8,128)(2,1)S(1)} %collective-permute-done.p1), channel_id=1, source_target_pairs={{0,64},{64,0},{1,65},{65,1},{2,66},{66,2},{3,67},{67,3},{4,68},{68... | collective-permute-start | bytes 1769480 | tf_op jit(solution)/shard_map/ppermute | solution.py:342
  91.0 7.6 %collective-permute-start.6 = (bf16[192,768]{1,0:T(8,128)(2,1)}, bf16[192,768]{1,0:T(8,128)(2,1)}, u32[]{:S(2)}, u32[]{:S(2)}) collective-permute-start(bf16[192,768]{1,0:T(8,128)(2,1)} %collective-permute-done.3.p2), channel_id=1, source_target_pairs={{0,64},{64,0},{1,65},{65,1},{2,66},{66,2},{3,67},{67,3},{4,68},{68... | collective-permute-start | bytes 884744 | tf_op jit(solution)/shard_map/ppermute | solution.py:342
  95.5 3.8 %copy-start.12 = (bf16[192,768]{1,0:T(8,128)(2,1)}, bf16[192,768]{1,0:T(8,128)(2,1)S(1)}, u32[]{:S(2)}) copy-start(bf16[192,768]{1,0:T(8,128)(2,1)S(1)} %collective-permute-done.4.p3) | copy-start | bytes 884740
  95.5 3.8 %collective-permute-start.7 = (bf16[192,768]{1,0:T(8,128)(2,1)S(1)}, bf16[192,768]{1,0:T(8,128)(2,1)}, u32[]{:S(2)}, u32[]{:S(2)}) collective-permute-start(bf16[192,768]{1,0:T(8,128)(2,1)S(1)} %collective-permute-done.4.p3), channel_id=1, source_target_pairs={{0,64},{64,0},{1,65},{65,1},{2,66},{66,2},{3,67},{67,3},{4,68},{68... | collective-permute-start | bytes 884744 | tf_op jit(solution)/shard_map/ppermute | solution.py:342
  99.3 0.9 copy-start.6
  99.3 1.1 copy-start.7
  99.3 1.4 copy-start.4
  123.8 25.5 %all-to-all-start.4 = ((f32[32,1,1536]{2,1,0:T(1,128)}), f32[32,1,1536]{2,1,0:T(1,128)S(1)}, u32[]{:S(2)}, u32[]{:S(2)}) async-start(f32[32,1,1536]{2,1,0:T(1,128)} %broadcast_in_dim.27), calls=%async_computation.4 | async-start | bytes 393216 | tf_op jit(solution)/shard_map/all_to_all | solution.py:282
  137.6 18.8 %copy-start.8 = (f32[24,1536]{1,0:T(8,128)S(1)}, f32[24,1536]{1,0:T(8,128)}, u32[]{:S(2)}) copy-start(f32[24,1536]{1,0:T(8,128)} %param.18) | copy-start | bytes 442372
  137.6 18.8 %copy-start.9 = (f32[24,1536]{1,0:T(8,128)S(1)}, f32[24,1536]{1,0:T(8,128)}, u32[]{:S(2)}) copy-start(f32[24,1536]{1,0:T(8,128)} %param.19) | copy-start | bytes 442372
  137.6 18.8 %copy-start.10 = (f32[24,1536]{1,0:T(8,128)S(1)}, f32[24,1536]{1,0:T(8,128)}, u32[]{:S(2)}) copy-start(f32[24,1536]{1,0:T(8,128)} %param.17) | copy-start | bytes 442372
  137.6 18.8 %copy-start.11 = (f32[24,1536]{1,0:T(8,128)S(1)}, f32[24,1536]{1,0:T(8,128)}, u32[]{:S(2)}) copy-start(f32[24,1536]{1,0:T(8,128)} %param.16) | copy-start | bytes 442372
  150.1 12.3 %all-to-all-start.5 = ((f32[16,1,1536]{2,1,0:T(1,128)}), f32[16,1,1536]{2,1,0:T(1,128)S(1)}, u32[]{:S(2)}, u32[]{:S(2)}) async-start(f32[16,1,1536]{2,1,0:T(1,128)} %broadcast_in_dim.30), calls=%async_computation.5 | async-start | bytes 196608 | tf_op jit(solution)/shard_map/all_to_all | solution.py:282
